TPU v7x, 32 devices: a whole 2x2x4 slice. The times are simulated.
32 devices in a mesh: space: 8 (over y, x, core), src: 4 (over z).
Axes of the slice: x: 2, y: 2, z: 4, core: 2. Of those that a mesh axis runs over, the one named last changes fastest.
Arguments:
- potential_start: float32 [16, 4, 128, 1024], P('src', None, 'space'), may hold values from -6 to 6
- adjoint_start: float32 [16, 4, 128, 1024], P('src', None, 'space'), may hold values from -6 to 6
- conductivity: float32 [4, 128, 1024], P(None, 'space', 'src'), may hold values from 0.1 to 1
- electrodes: int32 [16, 2], P('src'), may hold values from 0 to 131071
- receivers: int32 [16, 32, 2], P('src'), may hold values from 0 to 131071
- observed: float32 [16, 32], P('src'), may hold values from -6 to 6
Outputs:
- gradient: float32 [4, 128, 1024], P(None, 'space', 'src')
Inputs may be any that keep to these rules, and one draw needn't show every extreme that they name: `electrodes`: each entry is a surface node id row * 1024 + column. `receivers`: each entry is a surface node id row * 1024 + column.
All inputs are finite; a program needn't handle non-finite values.
Results may differ from a plain program's by a relative error of at most 0.00002.
Values sent between devices are 32-bit elements; how exact they have to be, the bound alone decides.
No kernel may reach another device: no remote copies, remote signals or barrier semaphores. Data moves between devices by JAX's collectives and lax.ppermute only.
A program may use at most 64 MiB of HBM per device.

v0:
```python
import jax
import jax.numpy as jnp
from jax import lax
from jax.sharding import PartitionSpec as P

SWEEPS = 4


GAMMA = 0.5
CURRENT = 4.0
THETA = 1.025
DELTA = 0.975
RATIO = THETA / DELTA


def padded_2(block, sides, width):
    for axis, dim in sides:
        count = lax.axis_size(axis)
        forward = [(i, i + 1) for i in range(count - 1)]
        backward = [(target, source) for source, target in forward]
        low = lax.ppermute(
            lax.slice_in_dim(block, block.shape[dim] - width, None, axis=dim), axis, forward
        )
        high = lax.ppermute(lax.slice_in_dim(block, 0, width, axis=dim), axis, backward)
        block = jnp.concatenate([low, block, high], axis=dim)
    return block


def pad_axis(field, dimension, margin):
    widths = [(0, 0)] * field.ndim
    widths[dimension % field.ndim] = (margin, margin)
    return jnp.pad(field, widths)


def coefficients(padded_sigma):
    centre_sigma = padded_sigma[:, 1:-1, :]
    layer_pad = pad_axis(centre_sigma, 0, 1)
    column_pad = pad_axis(centre_sigma, 2, 1)
    face_terms = (
        0.5 * (centre_sigma + padded_sigma[:, :-2, :]),
        0.5 * (centre_sigma + padded_sigma[:, 2:, :]),
        0.5 * (centre_sigma + column_pad[:, :, :-2]),
        0.5 * (centre_sigma + column_pad[:, :, 2:]),
        0.5 * (centre_sigma + layer_pad[:-2]),
        0.5 * (centre_sigma + layer_pad[2:]),
    )
    diagonal = (
        face_terms[0]
        + face_terms[1]
        + face_terms[2]
        + face_terms[3]
        + face_terms[4]
        + face_terms[5]
        + GAMMA * centre_sigma
    )
    return (face_terms, diagonal)


def apply_operator(padded, face_terms, diagonal):
    centre = padded[..., 1:-1, :]
    layer_pad = pad_axis(centre, -3, 1)
    column_pad = pad_axis(centre, -1, 1)
    neighbours = (
        face_terms[0] * padded[..., :-2, :]
        + face_terms[1] * padded[..., 2:, :]
        + face_terms[2] * column_pad[..., :-2]
        + face_terms[3] * column_pad[..., 2:]
        + face_terms[4] * layer_pad[..., :-2, :, :]
        + face_terms[5] * layer_pad[..., 2:, :, :]
    )
    return diagonal * centre - neighbours


def chebyshev(initial, source, face_terms, diagonal, inverse, extend, inside_rows):
    residual = source - apply_operator(extend(initial), face_terms, diagonal)
    residual = residual * inside_rows
    direction = inverse * residual / THETA
    factor = 1.0 / RATIO
    potential = initial
    for sweep in range(SWEEPS):
        potential = potential + direction
        if sweep + 1 < SWEEPS:
            residual = residual - apply_operator(extend(direction), face_terms, diagonal)
            residual = residual * inside_rows
            factor_next = 1.0 / (2.0 * RATIO - factor)
            direction = (
                factor_next * factor * direction + 2.0 * factor_next / DELTA * inverse * residual
            )
            factor = factor_next
    return potential


def sensitivity(forward_pad, adjoint_pad):
    forward_mid = forward_pad[..., 1:-1, :]
    adjoint_mid = adjoint_pad[..., 1:-1, :]
    forward_layer = pad_axis(forward_mid, -3, 1)
    adjoint_layer = pad_axis(adjoint_mid, -3, 1)
    forward_column = pad_axis(forward_mid, -1, 1)
    adjoint_column = pad_axis(adjoint_mid, -1, 1)
    pairs = (
        (forward_pad[..., :-2, :], adjoint_pad[..., :-2, :]),
        (forward_pad[..., 2:, :], adjoint_pad[..., 2:, :]),
        (forward_column[..., :-2], adjoint_column[..., :-2]),
        (forward_column[..., 2:], adjoint_column[..., 2:]),
        (forward_layer[..., :-2, :, :], adjoint_layer[..., :-2, :, :]),
        (forward_layer[..., 2:, :, :], adjoint_layer[..., 2:, :, :]),
    )
    running = GAMMA * forward_mid * adjoint_mid
    for forward_near, adjoint_near in pairs:
        running = running + 0.5 * (forward_mid - forward_near) * (adjoint_mid - adjoint_near)
    return -running


def local_pad(field):
    return pad_axis(field, -2, 1)


def surface_source(node_ids, amounts, base_row, span, layer_count, columns):
    sources_here = node_ids.shape[0]
    local_ids = node_ids - base_row * columns
    inside = (local_ids >= 0) & (local_ids < span * columns)
    slots = jnp.clip(local_ids, 0, span * columns - 1)
    source_rows = jnp.broadcast_to(
        jnp.arange(sources_here, dtype=jnp.int32)[:, None], node_ids.shape
    )
    plane = (
        jnp.zeros((sources_here, span * columns), jnp.float32)
        .at[source_rows, slots]
        .add(jnp.where(inside, amounts, 0.0))
    )
    plane = plane.reshape(sources_here, 1, span, columns)
    return jnp.concatenate(
        [plane, jnp.zeros((sources_here, layer_count - 1, span, columns), jnp.float32)], axis=1
    )


def per_device(potential_start, adjoint_start, conductivity, electrodes, receivers, observed):
    sources_here, layer_count, row_count, columns = potential_start.shape
    whole_sigma = lax.all_gather(conductivity, "src", axis=2, tiled=True)
    first_row = lax.axis_index("space") * row_count
    total_rows = row_count * lax.axis_size("space")
    margin_rows = SWEEPS + 1

    def widen(field):
        return padded_2(field, (("space", 2),), margin_rows)

    padded_sigma = padded_2(whole_sigma, (("space", 1),), margin_rows + 1)
    face_terms, diagonal = coefficients(padded_sigma)
    global_rows = first_row - margin_rows + jnp.arange(row_count + 2 * margin_rows, dtype=jnp.int32)
    inside_rows = ((global_rows >= 0) & (global_rows < total_rows)).astype(jnp.float32)[:, None]
    inverse = 1.0 / jnp.where(inside_rows > 0, diagonal, 1.0)
    forward_init = widen(potential_start)
    adjoint_init = widen(adjoint_start)
    span = row_count + 2 * margin_rows
    base_row = first_row - margin_rows
    currents = jnp.broadcast_to(jnp.array([CURRENT, -CURRENT], jnp.float32), electrodes.shape)
    injected = surface_source(electrodes, currents, base_row, span, layer_count, columns)
    forward = chebyshev(
        forward_init, injected, face_terms, diagonal, inverse, local_pad, inside_rows
    )
    surface = forward[:, 0, margin_rows : margin_rows + row_count, :].reshape(
        sources_here, row_count * columns
    )

    def read_nodes(node_ids):
        local_ids = node_ids - first_row * columns
        inside = (local_ids >= 0) & (local_ids < row_count * columns)
        picked = jnp.take_along_axis(
            surface, jnp.clip(local_ids, 0, row_count * columns - 1), axis=1
        )
        return jnp.where(inside, picked, 0.0)

    local_readings = read_nodes(receivers[:, :, 0]) - read_nodes(receivers[:, :, 1])
    predicted = lax.psum(local_readings, "space")
    misfit = predicted - observed
    adjoint_source = surface_source(
        jnp.concatenate([receivers[:, :, 0], receivers[:, :, 1]], axis=1),
        jnp.concatenate([misfit, -misfit], axis=1),
        base_row,
        span,
        layer_count,
        columns,
    )
    adjoint = chebyshev(
        adjoint_init, adjoint_source, face_terms, diagonal, inverse, local_pad, inside_rows
    )
    forward_pad = forward[:, :, margin_rows - 1 : margin_rows + row_count + 1, :]
    adjoint_pad = adjoint[:, :, margin_rows - 1 : margin_rows + row_count + 1, :]
    local_terms = jnp.sum(sensitivity(forward_pad, adjoint_pad), axis=0)
    summed = lax.psum(local_terms, "src")
    share = columns // lax.axis_size("src")
    return lax.dynamic_slice_in_dim(summed, lax.axis_index("src") * share, share, 2)


def solution(mesh):
    return jax.shard_map(
        per_device,
        mesh=mesh,
        in_specs=(
            P("src", None, "space", None),
            P("src", None, "space", None),
            P(None, "space", "src"),
            P("src", None),
            P("src", None, None),
            P("src", None),
        ),
        out_specs=P(None, "space", "src"),
        check_vma=False,
    )
```

profile of v0, /device:TPU:0, one launch (start us, length us, event | category | flops | bytes accessed | tf_op | source)
XLA Modules:
  0.0 187.7 jit_solution(12918429776498886450)
XLA Ops:
  6.5 16.0 %all_gather.3 = f32[4,16,1024]{2,1,0:T(8,128)S(1)} all-gather(f32[4,16,256]{2,1,0:T(8,128)} %param.11), channel_id=1, replica_groups=mesh['space'=8,'src'=4] {'src'}, dimensions={2}, use_global_device_ids=true | all-gather | bytes 327680 | tf_op jit(solution)/shard_map/all_gather | solution.py:139
  22.6 1.3 collective-permute-start.2
  23.9 1.3 collective-permute-start.3
  25.2 2.3 %fusion.150 = (f32[4,4,5,1024]{3,2,0,1:T(8,128)}, f32[4,4,5,1024]{3,2,0,1:T(8,128)}) fusion(f32[4,4,16,1024]{3,2,1,0:T(8,128)} %param.9), kind=kLoop, calls=%fused_computation.233 | loop fusion | bytes 1703936 | tf_op jit(solution)/shard_map/slice | solution.py:22
  27.5 5.6 %collective-permute-start = (f32[4,4,5,1024]{3,2,0,1:T(8,128)}, f32[4,4,5,1024]{3,2,0,1:T(8,128)}, u32[]{:S(2)}, u32[]{:S(2)}) collective-permute-start(f32[4,4,5,1024]{3,2,0,1:T(8,128)} %get-tuple-element.28), channel_id=1, source_target_pairs={{0,4},{4,8},{8,12},{12,16},{16,20},{20,24},{24,28},{1,5},{5,9},{9,... | collective-permute-start | bytes 983048 | tf_op jit(solution)/shard_map/ppermute | solution.py:21
  33.1 1.3 collective-permute-start.1
  34.4 1.1 fusion.149
  35.5 4.3 %collective-permute-start.4 = (f32[4,4,5,1024]{3,2,0,1:T(8,128)}, f32[4,4,5,1024]{3,2,0,1:T(8,128)}, u32[]{:S(2)}, u32[]{:S(2)}) collective-permute-start(f32[4,4,5,1024]{3,2,0,1:T(8,128)} %get-tuple-element.26), channel_id=1, source_target_pairs={{0,4},{4,8},{8,12},{12,16},{16,20},{20,24},{24,28},{1,5},{5,9},{9,... | collective-permute-start | bytes 983048 | tf_op jit(solution)/shard_map/ppermute | solution.py:21
  39.8 0.1 copy.15
  39.9 0.1 reshape.112
  40.0 0.1 copy.16
  40.1 0.1 reshape.114
  40.3 0.9 scatter_fusion
  41.1 1.1 reshape.97
  42.3 0.1 fusion.134
  42.4 0.1 reshape.135
  42.5 0.1 reshape.140
  42.6 1.3 collective-permute-start.5
  44.1 0.6 broadcast_multiply_fusion
  44.7 0.9 fusion.131
  45.7 0.4 copy-done.8
  46.1 2.2 %pad_maximum_fusion = f32[4,4,26,1024]{3,2,0,1:T(8,128)S(1)} fusion(f32[4,4,5,1024]{3,2,0,1:T(8,128)} %collective-permute-done.1, f32[4,4,5,1024]{3,2,0,1:T(8,128)} %collective-permute-done, f32[4,4,16,1024]{3,2,1,0:T(8,128)S(1)} %copy-done.8), kind=kLoop, calls=%fused_computation.130 | loop fusion | flops 851968 | bytes 3407872 | tf_op jit(solution)/shard_map/concatenate | solution.py:25
  48.3 2.6 %multiply_multiply_fusion.1 = (f32[4,4,26,1024]{3,2,0,1:T(8,128)S(1)}, f32[4,4,26,1024]{3,2,0,1:T(8,128)S(1)}) fusion(f32[4,26,1024]{2,1,0:T(8,128)S(1)} %get-tuple-element.15, f32[26]{0:T(128)S(1)} %and_convert_fusion, f32[4,26,1024]{2,1,0:T(8,128)S(1)} %get-tuple-element.31, f32[4,4,26,1024]{3,2,0,1:T(8,128)S(1)} %pad_maximum_fusion, ...), kind=kLoop, calls=%fused_computation.137 | loop fusion | flops 7241728 | bytes 8945768 | tf_op jit(solution)/shard_map/div | solution.py:77
  50.9 2.8 %multiply_add_fusion.3 = (f32[4,4,26,1024]{3,2,0,1:T(8,128)S(1)}, f32[4,4,26,1024]{3,2,0,1:T(8,128)S(1)}) fusion(f32[4,4,26,1024]{3,2,0,1:T(8,128)S(1)} %get-tuple-element.23, f32[4,26,1024]{2,1,0:T(8,128)S(1)} %get-tuple-element.41, f32[4,26,1024]{2,1,0:T(8,128)S(1)} %get-tuple-element.15, f32[26]{0:T(128)S(1)} %and_convert_fusion, ...), kind=kLoop, calls=%fused_computation.135 | loop fusion | flops 8093696 | bytes 10649704 | tf_op jit(solution)/shard_map/add | solution.py:87
  53.7 3.1 %multiply_add_fusion.2 = (f32[4,4,26,1024]{3,2,0,1:T(8,128)S(1)}, f32[4,4,26,1024]{3,2,0,1:T(8,128)S(1)}) fusion(f32[4,26,1024]{2,1,0:T(8,128)S(1)} %get-tuple-element.40, f32[4,4,26,1024]{3,2,0,1:T(8,128)S(1)} %get-tuple-element.21, f32[4,26,1024]{2,1,0:T(8,128)S(1)} %get-tuple-element.41, f32[4,4,26,1024]{3,2,0,1:T(8,128)S(1)} %get-tuple-element.23, ...), kind=kLoop, calls=%fused_computation.134 | loop fusion | flops 9371648 | bytes 12779624 | tf_op jit(solution)/shard_map/add | solution.py:87
  56.9 4.9 %fusion.37 = f32[4,4,26,1024]{3,2,0,1:T(8,128)S(1)} fusion(f32[4,4,26,1024]{3,2,0,1:T(8,128)S(1)} %get-tuple-element.19, f32[4,4,26,1024]{3,2,0,1:T(8,128)S(1)} %get-tuple-element.18, f32[4,4,26,1024]{3,2,0,1:T(8,128)S(1)} %get-tuple-element.23, f32[4,26,1024]{2,1,0:T(8,128)S(1)} %get-tuple-element.14, f32[26]{0:T(128)S(1)} %and_convert_fusion, ...), kind=kLoop, calls=%fused_computation.73 | loop fusion | flops 12353536 | bytes 14483560 | tf_op jit(solution)/shard_map/add | solution.py:81
  61.9 1.3 copy-done.6
  63.2 1.1 slice.345
  64.3 0.2 copy.20
  64.5 1.5 gather_fusion
  66.1 1.5 gather_fusion.1
  67.7 0.1 reshape.143
  67.8 16.1 %psum.14 = f32[4,32]{1,0:T(4,128)S(1)} all-reduce(f32[4,32]{1,0:T(4,128)S(1)} %fusion.136), channel_id=1, replica_groups=mesh['space'=8,'src'=4] {'space'}, use_global_device_ids=true, to_apply=%region_1.3 | all-reduce | flops 128 | bytes 1024 | tf_op jit(solution)/shard_map/psum | solution.py:174
  84.0 0.1 reshape.120
  84.1 0.8 broadcast.247
  84.9 35.7 %scatter_fusion.1 = f32[4,26624]{1,0:T(4,128)} fusion(f32[4,26624]{1,0:T(4,128)} %broadcast.247, s32[256]{0:T(256)S(1)} %reshape.118, f32[256]{0:T(256)S(1)} %reshape.120), kind=kCustom, calls=%fused_computation.3 | custom fusion | flops 256 | bytes 5120 | tf_op jit(solution)/shard_map/scatter-add | solution.py:129
  120.6 2.2 %reshape.98 = f32[4,1,26,1024]{3,2,0,1:T(8,128)} reshape(f32[4,26624]{1,0:T(4,128)} %scatter_fusion.1) | data formatting | bytes 851968 | tf_op jit(solution)/shard_map/reshape | solution.py:131
  122.8 2.0 %pad_maximum_fusion.1 = f32[4,4,26,1024]{3,2,0,1:T(8,128)S(1)} fusion(f32[4,4,5,1024]{3,2,0,1:T(8,128)} %collective-permute-done.5, f32[4,4,5,1024]{3,2,0,1:T(8,128)} %collective-permute-done.4, f32[4,4,16,1024]{3,2,1,0:T(8,128)} %param.10), kind=kLoop, calls=%fused_computation.131 | loop fusion | flops 851968 | bytes 3407872 | tf_op jit(solution)/shard_map/concatenate | solution.py:25
  124.8 2.6 %multiply_multiply_fusion = (f32[4,4,26,1024]{3,2,0,1:T(8,128)S(1)}, f32[4,4,26,1024]{3,2,0,1:T(8,128)S(1)}) fusion(f32[4,26,1024]{2,1,0:T(8,128)S(1)} %get-tuple-element.15, f32[26]{0:T(128)S(1)} %and_convert_fusion, f32[4,26,1024]{2,1,0:T(8,128)S(1)} %get-tuple-element.31, f32[4,4,26,1024]{3,2,0,1:T(8,128)S(1)} %pad_maximum_fusion.1, ...), kind=kLoop, calls=%fused_computation.136 | loop fusion | flops 7241728 | bytes 8945768 | tf_op jit(solution)/shard_map/div | solution.py:77
  127.4 2.8 %multiply_add_fusion.1 = (f32[4,4,26,1024]{3,2,0,1:T(8,128)S(1)}, f32[4,4,26,1024]{3,2,0,1:T(8,128)S(1)}) fusion(f32[4,4,26,1024]{3,2,0,1:T(8,128)S(1)} %get-tuple-element.11, f32[4,26,1024]{2,1,0:T(8,128)S(1)} %copy-done.5, f32[4,26,1024]{2,1,0:T(8,128)S(1)} %get-tuple-element.15, f32[26]{0:T(128)S(1)} %and_convert_fusion, ...), kind=kLoop, calls=%fused_computation.133 | loop fusion | flops 8093696 | bytes 10649704 | tf_op jit(solution)/shard_map/add | solution.py:87
  130.2 3.1 %multiply_add_fusion = (f32[4,4,26,1024]{3,2,0,1:T(8,128)S(1)}, f32[4,4,26,1024]{3,2,0,1:T(8,128)S(1)}) fusion(f32[4,26,1024]{2,1,0:T(8,128)S(1)} %copy-done.14, f32[4,4,26,1024]{3,2,0,1:T(8,128)S(1)} %get-tuple-element.9, f32[4,26,1024]{2,1,0:T(8,128)S(1)} %copy-done.5, f32[4,4,26,1024]{3,2,0,1:T(8,128)S(1)} %get-tuple-element.11, ...), kind=kLoop, calls=%fused_computation.132 | loop fusion | flops 9371648 | bytes 12779624 | tf_op jit(solution)/shard_map/add | solution.py:87
  133.4 5.0 %fusion.76 = f32[4,4,26,1024]{3,2,0,1:T(8,128)S(1)} fusion(f32[4,4,26,1024]{3,2,0,1:T(8,128)S(1)} %get-tuple-element.7, f32[4,4,26,1024]{3,2,0,1:T(8,128)S(1)} %get-tuple-element.6, f32[4,4,26,1024]{3,2,0,1:T(8,128)S(1)} %get-tuple-element.11, f32[4,26,1024]{2,1,0:T(8,128)S(1)} %copy-done.12, f32[26]{0:T(128)S(1)} %and_convert_fusion, ...), kind=kLoop, calls=%fused_computation.112 | loop fusion | flops 12353536 | bytes 14483560 | tf_op jit(solution)/shard_map/add | solution.py:81
  138.4 0.1 slice.349
  138.6 1.4 copy-done.7
  140.0 1.8 fusion.101
  141.8 0.7 neg.7
  142.6 36.8 %all-reduce.34.cloned.1.call-done = f32[4,16,1024]{2,1,0:T(8,128)} async-done(((f32[4,16,1024]{2,1,0:T(8,128)}), f32[4,16,1024]{2,1,0:T(8,128)}) %all-reduce.34.cloned.1.call-update) | async-done | bytes 262160 | tf_op jit(solution)/shard_map/psum | solution.py:190
  179.3 1.5 constant_dynamic-slice_fusion
  (69 shorter events, 0.7 us)
Async XLA Ops:
  6.5 27.8 %copy-start.9 = (f32[4,4,16,1024]{3,2,1,0:T(8,128)S(1)}, f32[4,4,16,1024]{3,2,1,0:T(8,128)}, u32[]{:S(2)}) copy-start(f32[4,4,16,1024]{3,2,1,0:T(8,128)} %param.10) | copy-start | bytes 3145732
  6.5 172.8 %all-reduce.34.cloned.1.call-start = ((), (), s32[]{:S(2)}) async-start(), calls=%async_computation | async-start | bytes 524288 | tf_op jit(solution)/shard_map/psum | solution.py:190
  22.6 20.1 %collective-permute-start.2 = (f32[4,6,1024]{2,1,0:T(8,128)S(1)}, f32[4,6,1024]{2,1,0:T(8,128)S(1)}, u32[]{:S(2)}, u32[]{:S(2)}) collective-permute-start(f32[4,6,1024]{2,1,0:T(8,128)S(1)} %get-tuple-element.36), channel_id=1, source_target_pairs={{0,4},{4,8},{8,12},{12,16},{16,20},{20,24},{24,28},{1,5},{5,9},{9,... | collective-permute-start | bytes 294920 | tf_op jit(solution)/shard_map/ppermute | solution.py:21
  23.9 15.9 %copy-start.20 = (s32[4,2]{0,1:T(2,128)S(1)}, s32[4,2]{0,1:T(2,128)}, u32[]{:S(2)}) copy-start(s32[4,2]{0,1:T(2,128)} %param.12) | copy-start | bytes 100
  23.9 16.1 %copy-start.23 = (f32[2]{0:T(128)S(1)}, f32[2]{0:T(128)}, u32[]{:S(2)}) copy-start(f32[2]{0:T(128)} %constant.30.clone) | copy-start | bytes 28
  23.9 20.1 %collective-permute-start.3 = (f32[4,6,1024]{2,1,0:T(8,128)S(1)}, f32[4,6,1024]{2,1,0:T(8,128)S(1)}, u32[]{:S(2)}, u32[]{:S(2)}) collective-permute-start(f32[4,6,1024]{2,1,0:T(8,128)S(1)} %get-tuple-element.37), channel_id=1, source_target_pairs={{4,0},{8,4},{12,8},{16,12},{20,16},{24,20},{28,24},{5,1},{9,5},{13... | collective-permute-start | bytes 294920 | tf_op jit(solution)/shard_map/ppermute | solution.py:24
  27.5 18.2 %collective-permute-start = (f32[4,4,5,1024]{3,2,0,1:T(8,128)}, f32[4,4,5,1024]{3,2,0,1:T(8,128)}, u32[]{:S(2)}, u32[]{:S(2)}) collective-permute-start(f32[4,4,5,1024]{3,2,0,1:T(8,128)} %get-tuple-element.28), channel_id=1, source_target_pairs={{0,4},{4,8},{8,12},{12,16},{16,20},{20,24},{24,28},{1,5},{5,9},{9,... | collective-permute-start | bytes 983048 | tf_op jit(solution)/shard_map/ppermute | solution.py:21
  33.1 12.6 %collective-permute-start.1 = (f32[4,4,5,1024]{3,2,0,1:T(8,128)}, f32[4,4,5,1024]{3,2,0,1:T(8,128)}, u32[]{:S(2)}, u32[]{:S(2)}) collective-permute-start(f32[4,4,5,1024]{3,2,0,1:T(8,128)} %get-tuple-element.29), channel_id=1, source_target_pairs={{4,0},{8,4},{12,8},{16,12},{20,16},{24,20},{28,24},{5,1},{9,5},{13... | collective-permute-start | bytes 983048 | tf_op jit(solution)/shard_map/ppermute | solution.py:24
  35.5 87.3 %collective-permute-start.4 = (f32[4,4,5,1024]{3,2,0,1:T(8,128)}, f32[4,4,5,1024]{3,2,0,1:T(8,128)}, u32[]{:S(2)}, u32[]{:S(2)}) collective-permute-start(f32[4,4,5,1024]{3,2,0,1:T(8,128)} %get-tuple-element.26), channel_id=1, source_target_pairs={{0,4},{4,8},{8,12},{12,16},{16,20},{20,24},{24,28},{1,5},{5,9},{9,... | collective-permute-start | bytes 983048 | tf_op jit(solution)/shard_map/ppermute | solution.py:21
  40.3 2.0 %copy-start.21 = (s32[4,32,2]{1,2,0:T(2,128)S(1)}, s32[4,32,2]{1,2,0:T(2,128)}, u32[]{:S(2)}) copy-start(s32[4,32,2]{1,2,0:T(2,128)} %param.13) | copy-start | bytes 3076
  42.6 80.1 %collective-permute-start.5 = (f32[4,4,5,1024]{3,2,0,1:T(8,128)}, f32[4,4,5,1024]{3,2,0,1:T(8,128)}, u32[]{:S(2)}, u32[]{:S(2)}) collective-permute-start(f32[4,4,5,1024]{3,2,0,1:T(8,128)} %get-tuple-element.27), channel_id=1, source_target_pairs={{4,0},{8,4},{12,8},{16,12},{20,16},{24,20},{28,24},{5,1},{9,5},{13... | collective-permute-start | bytes 983048 | tf_op jit(solution)/shard_map/ppermute | solution.py:24
  44.6 12.2 %copy-start.11 = (f32[4,26,1024]{2,1,0:T(8,128)}, f32[4,26,1024]{2,1,0:T(8,128)S(1)}, u32[]{:S(2)}) copy-start(f32[4,26,1024]{2,1,0:T(8,128)S(1)} %get-tuple-element.14) | copy-start | bytes 1277956
  44.7 1.4 copy-start.8
  45.6 5.3 %copy-start.15 = (f32[4,26,1024]{2,1,0:T(8,128)}, f32[4,26,1024]{2,1,0:T(8,128)S(1)}, u32[]{:S(2)}) copy-start(f32[4,26,1024]{2,1,0:T(8,128)S(1)} %get-tuple-element.24) | copy-start | bytes 1277956
  45.6 8.1 %copy-start.13 = (f32[4,26,1024]{2,1,0:T(8,128)}, f32[4,26,1024]{2,1,0:T(8,128)S(1)}, u32[]{:S(2)}) copy-start(f32[4,26,1024]{2,1,0:T(8,128)S(1)} %get-tuple-element.40) | copy-start | bytes 1277956
  45.6 11.3 %copy-start = (f32[4,26,1024]{2,1,0:T(8,128)}, f32[4,26,1024]{2,1,0:T(8,128)S(1)}, u32[]{:S(2)}) copy-start(f32[4,26,1024]{2,1,0:T(8,128)S(1)} %get-tuple-element.33) | copy-start | bytes 1277956
  45.6 11.3 %copy-start.2 = (f32[4,26,1024]{2,1,0:T(8,128)}, f32[4,26,1024]{2,1,0:T(8,128)S(1)}, u32[]{:S(2)}) copy-start(f32[4,26,1024]{2,1,0:T(8,128)S(1)} %get-tuple-element.25) | copy-start | bytes 1277956
  45.6 11.3 %copy-start.4 = (f32[4,26,1024]{2,1,0:T(8,128)}, f32[4,26,1024]{2,1,0:T(8,128)S(1)}, u32[]{:S(2)}) copy-start(f32[4,26,1024]{2,1,0:T(8,128)S(1)} %get-tuple-element.41) | copy-start | bytes 1277956
  45.6 2.6 %copy-start.18 = (f32[4,1,26,1024]{3,2,0,1:T(8,128)S(1)}, f32[4,1,26,1024]{3,2,0,1:T(8,128)}, u32[]{:S(2)}) copy-start(f32[4,1,26,1024]{3,2,0,1:T(8,128)} %reshape.97) | copy-start | bytes 1277956
  61.8 1.3 copy-start.6
  64.5 19.4 %copy-start.22 = (f32[4,32]{1,0:T(4,128)S(1)}, f32[4,32]{1,0:T(4,128)}, u32[]{:S(2)}) copy-start(f32[4,32]{1,0:T(4,128)} %param.14) | copy-start | bytes 1540
  122.7 2.0 %copy-start.1 = (f32[4,26,1024]{2,1,0:T(8,128)S(1)}, f32[4,26,1024]{2,1,0:T(8,128)}, u32[]{:S(2)}) copy-start(f32[4,26,1024]{2,1,0:T(8,128)} %copy-done) | copy-start | bytes 1277956
  122.7 2.0 %copy-start.3 = (f32[4,26,1024]{2,1,0:T(8,128)S(1)}, f32[4,26,1024]{2,1,0:T(8,128)}, u32[]{:S(2)}) copy-start(f32[4,26,1024]{2,1,0:T(8,128)} %copy-done.2) | copy-start | bytes 1277956
  122.7 2.0 %copy-start.19 = (f32[4,1,26,1024]{3,2,0,1:T(8,128)S(1)}, f32[4,1,26,1024]{3,2,0,1:T(8,128)}, u32[]{:S(2)}) copy-start(f32[4,1,26,1024]{3,2,0,1:T(8,128)} %reshape.98) | copy-start | bytes 1277956
  124.8 2.6 %copy-start.5 = (f32[4,26,1024]{2,1,0:T(8,128)S(1)}, f32[4,26,1024]{2,1,0:T(8,128)}, u32[]{:S(2)}) copy-start(f32[4,26,1024]{2,1,0:T(8,128)} %copy-done.4) | copy-start | bytes 1277956
  124.8 2.6 %copy-start.16 = (f32[4,26,1024]{2,1,0:T(8,128)S(1)}, f32[4,26,1024]{2,1,0:T(8,128)}, u32[]{:S(2)}) copy-start(f32[4,26,1024]{2,1,0:T(8,128)} %copy-done.15) | copy-start | bytes 1277956
  127.4 2.8 %copy-start.14 = (f32[4,26,1024]{2,1,0:T(8,128)S(1)}, f32[4,26,1024]{2,1,0:T(8,128)}, u32[]{:S(2)}) copy-start(f32[4,26,1024]{2,1,0:T(8,128)} %copy-done.13) | copy-start | bytes 1277956
  130.2 3.2 %copy-start.10 = (f32[4,4,16,1024]{3,2,1,0:T(8,128)S(1)}, f32[4,4,16,1024]{3,2,1,0:T(8,128)}, u32[]{:S(2)}) copy-start(f32[4,4,16,1024]{3,2,1,0:T(8,128)} %param.10) | copy-start | bytes 3145732
  130.2 3.2 %copy-start.12 = (f32[4,26,1024]{2,1,0:T(8,128)S(1)}, f32[4,26,1024]{2,1,0:T(8,128)}, u32[]{:S(2)}) copy-start(f32[4,26,1024]{2,1,0:T(8,128)} %copy-done.11) | copy-start | bytes 1277956
  133.4 5.2 %copy-start.17 = (f32[4,4,16,1024]{3,2,0,1:T(8,128)S(1)}, f32[4,4,16,1024]{3,2,0,1:T(8,128)}, u32[]{:S(2)}) copy-start(f32[4,4,16,1024]{3,2,0,1:T(8,128)} %slice.345) | copy-start | bytes 3145732
  138.4 1.6 copy-start.7
Sparse Core Ops, SparseCore 0:
  142.7 36.6 all-reduce.33
where the time goes:
time: 189 us; the launch traced here: 188 us
  other arithmetic  72.1 us (38%)
  waiting for transfers between devices  36.8 us (19%)
  blocking collectives  32.1 us (17%)
  local copies, waits for them, and re-layouts  17.7 us (9%)
  starting transfers between devices  15 us (8%)
  between operations  14 us (7%)
    psum x1, waiting for transfers between devices, per_device(): summed = lax.psum(local_terms, 'src')  36.8 us
    scatter-add x2, other arithmetic, surface_source(): plane = jnp.zeros((sources_here, span * columns), jnp.float32).at[source_...  36.6 us
    psum x1, blocking collectives, per_device(): predicted = lax.psum(local_readings, 'space')  16.1 us
    all_gather x1, blocking collectives, per_device(): whole_sigma = lax.all_gather(conductivity, 'src', axis=2, tiled=True)  16 us
    add x4, other arithmetic, chebyshev(): factor_next * factor * direction  11.9 us
    ppermute x3, starting transfers between devices, padded_2(): lax.ppermute(lax.slice_in_dim(block, block.shape[dim] - width, None, axis...  11.1 us
    add x2, other arithmetic, chebyshev(): potential = potential + direction  9.93 us
    div x2, other arithmetic, chebyshev(): direction = inverse * residual / THETA  5.15 us
  transfers between devices with their start and end apart: 7, of which 1 were waited for; matrix products, arithmetic and copies ran while one was open for 36% of the time, Pallas kernels for 0%

commit v1 on v0

v1 whole, which is shorter than its diff:
```python
import functools

import jax
import jax.numpy as jnp
from jax import lax
from jax.experimental import pallas as pl
from jax.experimental.pallas import tpu as pltpu
from jax.sharding import PartitionSpec as P

SWEEPS = 4
GAMMA = 0.5
CURRENT = 4.0
THETA = 1.025
DELTA = 0.975
RATIO = THETA / DELTA
LANES = 128
HALO = SWEEPS + 1

VMEM = pl.BlockSpec(memory_space=pltpu.VMEM)
SMEM = pl.BlockSpec(memory_space=pltpu.SMEM)


def recurrence():
    steps = [(THETA - 1.0, 0.0, 1.0)]
    before, scale = 1.0, 1.0 / THETA
    factor = 1.0 / RATIO
    for _ in range(SWEEPS - 1):
        factor_next = 1.0 / (2.0 * RATIO - factor)
        alpha = factor_next * factor
        beta = 2.0 * factor_next / DELTA
        after = beta * scale
        steps.append(((1.0 + alpha - beta) / beta, alpha * before / after, 1.0 / scale))
        before, scale, factor = scale, after, factor_next
    return steps, scale


STEPS, FINAL = recurrence()


def rows_of(start, count, groups):
    begin = start * groups
    if not isinstance(begin, int):
        begin = pl.multiple_of(begin, groups)
    return pl.ds(begin, count * groups)


def to_rows(read, write, rows, groups):
    for j in range(groups):
        write(pl.ds(j, rows, stride=groups), read(pl.ds(j * LANES, LANES)))


def from_right(v, last_lane):
    groups = v.shape[0]
    turned = pltpu.roll(v, LANES - 1, 1)
    return jnp.where(last_lane, pltpu.roll(turned, groups - 1, 0), turned)


def from_left(v, first_lane):
    turned = pltpu.roll(v, 1, 1)
    return jnp.where(first_lane, pltpu.roll(turned, 1, 0), turned)


def lane_masks(groups):
    lane = lax.broadcasted_iota(jnp.int32, (groups, LANES), 1)
    group = lax.broadcasted_iota(jnp.int32, (groups, LANES), 0)
    first_lane = lane == 0
    last_lane = lane == LANES - 1
    first_column = first_lane & (group == 0)
    last_column = last_lane & (group == groups - 1)
    return first_lane, last_lane, first_column, last_column


def three_parts(x):
    high = x.astype(jnp.bfloat16)
    rest = x - high.astype(jnp.float32)
    middle = rest.astype(jnp.bfloat16)
    low = (rest - middle.astype(jnp.float32)).astype(jnp.bfloat16)
    return jnp.concatenate([high, middle, low], axis=0)


def column_hits(columns, j):
    nodes = columns.shape[1]
    c = lax.broadcasted_iota(jnp.int32, (LANES, nodes), 0) + j * LANES
    return jnp.where(c == columns, 1.0, 0.0).astype(jnp.bfloat16)


def halo_kernel(groups, x_ref, top_ref, bottom_ref, work):
    sources, layers, rows, _ = x_ref.shape
    for s in range(sources):
        for l in range(layers):
            for j in range(groups):
                work[s, l, pl.ds(j, rows, stride=groups), :] = x_ref[s, l, :, j * LANES : (j + 1) * LANES]
    top_ref[...] = work[:, :, : HALO * groups, :]
    bottom_ref[...] = work[:, :, (rows - HALO) * groups :, :]


def make_halos(x):
    sources, layers, rows, columns = x.shape
    groups = columns // LANES
    shape = jax.ShapeDtypeStruct((sources, layers, HALO * groups, LANES), jnp.float32)
    return pl.pallas_call(
        functools.partial(halo_kernel, groups),
        out_shape=(shape, shape),
        in_specs=[VMEM],
        out_specs=(VMEM, VMEM),
        scratch_shapes=[pltpu.VMEM((sources, layers, rows * groups, LANES), jnp.float32)],
        name="halo",
    )(x)


def sigma_kernel(groups, me_ref, *refs):
    pieces, (own_ref, top_ref, bottom_ref, stage) = refs[:-4], refs[-4:]
    count = len(pieces)
    layers, rows, share = pieces[0].shape
    me = me_ref[0]
    for k, piece in enumerate(pieces):
        stage[me ^ k] = piece[...]
    per = share // LANES
    for q in range(count):
        for l in range(layers):
            for t in range(per):
                own_ref[l, pl.ds(q * per + t, rows, stride=groups), :] = stage[
                    q, l, :, t * LANES : (t + 1) * LANES
                ]
    top_ref[...] = own_ref[:, : HALO * groups, :]
    bottom_ref[...] = own_ref[:, (rows - HALO) * groups :, :]


def assemble_sigma(me, pieces, groups):
    layers, rows, share = pieces[0].shape
    halo = jax.ShapeDtypeStruct((layers, HALO * groups, LANES), jnp.float32)
    return pl.pallas_call(
        functools.partial(sigma_kernel, groups),
        out_shape=(jax.ShapeDtypeStruct((layers, rows * groups, LANES), jnp.float32), halo, halo),
        in_specs=[SMEM] + [VMEM] * len(pieces),
        out_specs=(VMEM, VMEM, VMEM),
        scratch_shapes=[pltpu.VMEM((len(pieces), layers, rows, share), jnp.float32)],
        name="sigma",
    )(me, *pieces)


def coefficient_rows(sigma, coef, surface, groups, first, last):
    layers = sigma.shape[0]
    first_lane, last_lane, first_column, last_column = lane_masks(groups)

    def body(e, carry):
        here = rows_of(e, 1, groups)
        above = rows_of(e - 1, 1, groups)
        below = rows_of(e + 1, 1, groups)
        centre = [sigma[l, here, :] for l in range(layers)]
        for l in range(layers):
            c = centre[l]
            up = 0.5 * (c + sigma[l, above, :])
            down = 0.5 * (c + sigma[l, below, :])
            left = 0.5 * (c + jnp.where(first_column, 0.0, from_left(c, first_lane)))
            right = 0.5 * (c + jnp.where(last_column, 0.0, from_right(c, last_lane)))
            lower = 0.5 * (c + centre[l - 1]) if l > 0 else 0.5 * c
            upper = 0.5 * (c + centre[l + 1]) if l + 1 < layers else 0.5 * c
            diagonal = up + down + left + right + lower + upper + GAMMA * c
            inside = c > 0.0
            inverse = jnp.where(inside, 1.0 / jnp.where(inside, diagonal, 1.0), 0.0)
            coef[0, l, here, :] = up * inverse
            coef[1, l, here, :] = down * inverse
            coef[2, l, here, :] = jnp.where(first_column, 0.0, left * inverse)
            coef[3, l, here, :] = jnp.where(last_column, 0.0, right * inverse)
            if l > 0:
                coef[4, l, here, :] = lower * inverse
            if l + 1 < layers:
                coef[5, l, here, :] = upper * inverse
            if l == 0:
                surface[here, :] = inverse
        return carry

    lax.fori_loop(first, last, body, 0)


def sweep(step, old, new, coef, plane, groups, first, last):
    p, q, g = STEPS[step]
    sources, layers = old.shape[:2]
    first_lane, last_lane, _, _ = lane_masks(groups)

    def body(e, carry):
        here = rows_of(e, 1, groups)
        above = rows_of(e - 1, 1, groups)
        below = rows_of(e + 1, 1, groups)
        for l in range(layers):
            weight = [coef[i, l, here, :] for i in range(4)]
            lower = coef[4, l, here, :] if l > 0 else None
            upper = coef[5, l, here, :] if l + 1 < layers else None
            for s in range(sources):
                v = old[s, l, here, :]
                total = p * v
                total += weight[0] * old[s, l, above, :]
                total += weight[1] * old[s, l, below, :]
                total += weight[2] * from_left(v, first_lane)
                total += weight[3] * from_right(v, last_lane)
                if lower is not None:
                    total += lower * old[s, l - 1, here, :]
                if upper is not None:
                    total += upper * old[s, l + 1, here, :]
                if step > 0:
                    total -= q * new[s, l, here, :]
                if l == 0 and plane is not None:
                    amount = plane[s, here, :]
                    total += amount if g == 1.0 else g * amount
                new[s, l, here, :] = total
        return carry

    lax.fori_loop(first, last, body, 0)


def widen(x_ref, top_ref, bottom_ref, wide, groups):
    sources, layers, rows, _ = x_ref.shape
    for s in range(sources):
        for l in range(layers):
            for j in range(groups):
                wide[s, l, pl.ds(HALO * groups + j, rows, stride=groups), :] = x_ref[
                    s, l, :, j * LANES : (j + 1) * LANES
                ]
    wide[:, :, : HALO * groups, :] = top_ref[...]
    wide[:, :, (HALO + rows) * groups :, :] = bottom_ref[...]


def forward_kernel(
    groups, position_ref, electrodes_ref, sigma_ref, sigma_top, sigma_bottom, x_ref, top_ref, bottom_ref, nodes_ref,
    coef, surface, last_field, readings_ref, sigma, other, plane,
):
    sources, layers, rows, columns = x_ref.shape
    extent = rows + 2 * HALO
    first_row = position_ref[0] * rows
    sigma[:, : HALO * groups, :] = sigma_top[...]
    sigma[:, HALO * groups : (HALO + rows) * groups, :] = sigma_ref[...]
    sigma[:, (HALO + rows) * groups :, :] = sigma_bottom[...]
    widen(x_ref, top_ref, bottom_ref, last_field, groups)
    coefficient_rows(sigma, coef, surface, groups, 1, extent - 1)

    plane[...] = jnp.zeros(plane.shape, jnp.float32)
    column = lax.broadcasted_iota(jnp.int32, (groups, LANES), 0) * LANES + lax.broadcasted_iota(
        jnp.int32, (groups, LANES), 1
    )
    for s in range(sources):
        for k, current in enumerate((CURRENT, -CURRENT)):
            node = electrodes_ref[s, k]
            row = node // columns
            e = row - first_row + HALO
            inside = (e >= 1) & (e < extent - 1)
            here = rows_of(jnp.clip(e, 1, extent - 2), 1, groups)
            hit = (column == node - row * columns) & inside
            plane[s, here, :] += jnp.where(hit, current * surface[here, :], 0.0)

    old, new = last_field, other
    for step in range(SWEEPS):
        sweep(step, old, new, coef, plane, groups, 1 + step, extent - 1 - step)
        old, new = new, old

    node = nodes_ref[...]
    node_row = node // columns
    node_column = node - node_row * columns
    count = node.shape[1]
    picked = jnp.zeros((3 * sources * rows, count), jnp.float32)
    for j in range(groups):
        tile = jnp.concatenate(
            [old[s, 0, pl.ds(HALO * groups + j, rows, stride=groups), :] for s in range(sources)], axis=0
        )
        picked += jnp.dot(three_parts(tile), column_hits(node_column, j), preferred_element_type=jnp.float32)
    size = sources * rows
    picked = picked[:size] + picked[size : 2 * size] + picked[2 * size :]
    r = lax.broadcasted_iota(jnp.int32, (size, count), 0)
    k = lax.broadcasted_iota(jnp.int32, (size, count), 1)
    hit = (r // rows == k // (count // sources)) & (node_row - first_row == r % rows)
    readings_ref[...] = FINAL * jnp.sum(jnp.where(hit, picked, 0.0), axis=0, keepdims=True)


def forward_solve(position, electrodes, sigma, sigma_top, sigma_bottom, x, top, bottom, nodes):
    sources, layers, rows, columns = x.shape
    groups = columns // LANES
    tall = (rows + 2 * HALO) * groups
    f32 = jnp.float32
    return pl.pallas_call(
        functools.partial(forward_kernel, groups),
        out_shape=(
            jax.ShapeDtypeStruct((6, layers, tall, LANES), f32),
            jax.ShapeDtypeStruct((tall, LANES), f32),
            jax.ShapeDtypeStruct((sources, layers, tall, LANES), f32),
            jax.ShapeDtypeStruct((1, nodes.shape[1]), f32),
        ),
        in_specs=[SMEM, SMEM] + [VMEM] * 7,
        out_specs=(VMEM,) * 4,
        scratch_shapes=[
            pltpu.VMEM((layers, tall, LANES), f32),
            pltpu.VMEM((sources, layers, tall, LANES), f32),
            pltpu.VMEM((sources, tall, LANES), f32),
        ],
        name="forward",
    )(position, electrodes, sigma, sigma_top, sigma_bottom, x, top, bottom, nodes)


def adjoint_first_kernel(groups, x_ref, top_ref, bottom_ref, coef, wide, new):
    rows = x_ref.shape[2]
    widen(x_ref, top_ref, bottom_ref, wide, groups)
    sweep(0, wide, new, coef, None, groups, 1, rows + 2 * HALO - 1)


def adjoint_first(x, top, bottom, coef):
    sources, layers, rows, columns = x.shape
    groups = columns // LANES
    shape = jax.ShapeDtypeStruct((sources, layers, (rows + 2 * HALO) * groups, LANES), jnp.float32)
    return pl.pallas_call(
        functools.partial(adjoint_first_kernel, groups),
        out_shape=(shape, shape),
        in_specs=[VMEM] * 4,
        out_specs=(VMEM, VMEM),
        name="adjoint_first",
    )(x, top, bottom, coef)


def adjoint_kernel(
    rows, columns, position_ref, nodes_ref, readings_ref, observed_ref, wide_in, new_in, coef, surface, forward,
    *refs,
):
    blocks, (wide, new, plane, gradient, staged) = refs[:-5], refs[-5:]
    sources, layers, tall, _ = wide.shape
    groups = columns // LANES
    extent = tall // groups
    count = nodes_ref.shape[1]
    per_source = count // sources
    receivers = per_source // 2
    first_row = position_ref[0] * rows

    lane = lax.broadcasted_iota(jnp.int32, (1, count), 1)
    positive = (lane // receivers) % 2 == 0
    readings = readings_ref[...]
    partner = jnp.where(
        positive, pltpu.roll(readings, count - receivers, 1), pltpu.roll(readings, receivers, 1)
    )
    amounts = readings - partner - jnp.where(positive, observed_ref[...], -observed_ref[...])
    node = nodes_ref[...]
    node_row = node // columns
    node_column = node - node_row * columns
    span = extent - 2
    size = sources * span
    r = lax.broadcasted_iota(jnp.int32, (size, count), 0)
    k = lax.broadcasted_iota(jnp.int32, (size, count), 1)
    hit = (r // span == k // per_source) & (node_row - first_row + HALO - 1 == r % span)
    spread = three_parts(jnp.where(hit, amounts, 0.0))
    for j in range(groups):
        part = lax.dot_general(
            spread, column_hits(node_column, j), (((1,), (1,)), ((), ())), preferred_element_type=jnp.float32
        )
        part = part[:size] + part[size : 2 * size] + part[2 * size :]
        weight = surface[pl.ds(groups + j, span, stride=groups), :]
        for s in range(sources):
            plane[s, pl.ds(groups + j, span, stride=groups), :] = part[s * span : (s + 1) * span] * weight

    def copy_in(e, carry):
        here = rows_of(e, 1, groups)
        for s in range(sources):
            for l in range(layers):
                wide[s, l, here, :] = wide_in[s, l, here, :]
                fresh = new_in[s, l, here, :]
                new[s, l, here, :] = fresh + plane[s, here, :] if l == 0 else fresh
        return carry

    lax.fori_loop(1, extent - 1, copy_in, 0)

    old, newer = new, wide
    for step in range(1, SWEEPS):
        sweep(step, old, newer, coef, plane, groups, 1 + step, extent - 1 - step)
        old, newer = newer, old
    adjoint = old

    first_lane, last_lane, first_column, last_column = lane_masks(groups)

    def pair(s, l, e):
        here = rows_of(e, 1, groups)
        return forward[s, l, here, :], adjoint[s, l, here, :]

    def body(e, above_faces):
        below_faces = []
        products, layer_faces, right_faces = [], [], []
        for l in range(layers):
            product = row_face = right_face = layer_face = None
            for s in range(sources):
                u, a = pair(s, l, e)
                u_below, a_below = pair(s, l, e + 1)
                u_right = jnp.where(last_column, 0.0, from_right(u, last_lane))
                a_right = jnp.where(last_column, 0.0, from_right(a, last_lane))
                terms = [u * a, (u - u_below) * (a - a_below), (u - u_right) * (a - a_right)]
                if l + 1 < layers:
                    u_next, a_next = pair(s, l + 1, e)
                    terms.append((u - u_next) * (a - a_next))
                if s == 0:
                    sums = terms
                else:
                    sums = [x + y for x, y in zip(sums, terms)]
            products.append(sums[0])
            below_faces.append(sums[1])
            right_faces.append(sums[2])
            layer_faces.append(sums[3] if l + 1 < layers else sums[0])
        for l in range(layers):
            left_face = jnp.where(first_column, products[l], from_left(right_faces[l], first_lane))
            total = products[l] + above_faces[l] + below_faces[l] + right_faces[l] + left_face
            total += layer_faces[l] + (layer_faces[l - 1] if l > 0 else products[l])
            gradient[l, rows_of(e - HALO, 1, groups), :] = (-0.5 * FINAL * FINAL) * total
        return tuple(below_faces)

    start = []
    for l in range(layers):
        running = None
        for s in range(sources):
            u, a = pair(s, l, HALO - 1)
            u_below, a_below = pair(s, l, HALO)
            term = (u - u_below) * (a - a_below)
            running = term if s == 0 else running + term
        start.append(running)
    lax.fori_loop(HALO, HALO + rows, body, tuple(start))

    me = position_ref[1]
    count_blocks = len(blocks)
    per = groups // count_blocks
    for q in range(count_blocks):
        for l in range(layers):
            for t in range(per):
                staged[q, l, :, t * LANES : (t + 1) * LANES] = gradient[
                    l, pl.ds(q * per + t, rows, stride=groups), :
                ]
    for i, block in enumerate(blocks):
        block[...] = staged[me ^ i]


def adjoint_solve(position, nodes, readings, observed, wide, new, coef, surface, forward, rows, columns, blocks):
    sources, layers, tall, _ = wide.shape
    groups = columns // LANES
    f32 = jnp.float32
    block = jax.ShapeDtypeStruct((layers, rows, columns // blocks), f32)
    return pl.pallas_call(
        functools.partial(adjoint_kernel, rows, columns),
        out_shape=(block,) * blocks,
        in_specs=[SMEM] + [VMEM] * 8,
        out_specs=(VMEM,) * blocks,
        scratch_shapes=[
            pltpu.VMEM((sources, layers, tall, LANES), f32),
            pltpu.VMEM((sources, layers, tall, LANES), f32),
            pltpu.VMEM((sources, tall, LANES), f32),
            pltpu.VMEM((layers, rows * groups, LANES), f32),
            pltpu.VMEM((blocks, layers, rows, columns // blocks), f32),
        ],
        name="adjoint",
    )(position, nodes, readings, observed, wide, new, coef, surface, forward)


def is_power_of_two(n):
    return n & (n - 1) == 0


def exchange(value, axis, mask):
    count = lax.axis_size(axis)
    return lax.ppermute(value, axis, [(i, i ^ mask) for i in range(count)])


def shift_down(value, axis):
    count = lax.axis_size(axis)
    return lax.ppermute(value, axis, [(i, i + 1) for i in range(count - 1)])


def shift_up(value, axis):
    count = lax.axis_size(axis)
    return lax.ppermute(value, axis, [(i + 1, i) for i in range(count - 1)])


def sum_over(value, axis):
    count = lax.axis_size(axis)
    if not is_power_of_two(count):
        return lax.psum(value, axis)
    mask = 1
    while mask < count:
        value = value + exchange(value, axis, mask)
        mask *= 2
    return value


def per_device(potential_start, adjoint_start, conductivity, electrodes, receivers, observed):
    sources, layers, rows, columns = potential_start.shape
    groups = columns // LANES
    split = lax.axis_size("src")
    direct = is_power_of_two(split) and split <= 4 and (columns // split) % LANES == 0
    position = jnp.stack([lax.axis_index("space"), lax.axis_index("src")]).astype(jnp.int32)

    if direct:
        pieces = [conductivity] + [None] * (split - 1)
        for k in reversed(range(1, split)):
            pieces[k] = exchange(conductivity, "src", k)
        me = position[1:]
    else:
        pieces = [lax.all_gather(conductivity, "src", axis=2, tiled=True)]
        me = jnp.zeros((1,), jnp.int32)
    sigma, sigma_first, sigma_last = assemble_sigma(me, pieces, groups)
    x_first, x_last = make_halos(potential_start)
    a_first, a_last = make_halos(adjoint_start)
    x_top, x_bottom = shift_down(x_last, "space"), shift_up(x_first, "space")
    sigma_top, sigma_bottom = shift_down(sigma_last, "space"), shift_up(sigma_first, "space")
    a_top, a_bottom = shift_down(a_last, "space"), shift_up(a_first, "space")

    nodes = receivers.transpose(0, 2, 1).reshape(1, -1)
    measured = jnp.broadcast_to(observed[:, None, :], (sources, 2, observed.shape[1])).reshape(1, -1)
    coef, surface, forward, readings = forward_solve(
        position, electrodes, sigma, sigma_top, sigma_bottom, potential_start, x_top, x_bottom, nodes
    )
    readings = sum_over(readings, "space")
    wide, new = adjoint_first(adjoint_start, a_top, a_bottom, coef)
    blocks = adjoint_solve(
        position, nodes, readings, measured, wide, new, coef, surface, forward, rows, columns, split if direct else 1
    )
    if direct:
        total = blocks[0]
        for k in reversed(range(1, split)):
            total = total + exchange(blocks[k], "src", k)
        return total
    summed = lax.psum(blocks[0], "src")
    share = columns // split
    return lax.dynamic_slice_in_dim(summed, lax.axis_index("src") * share, share, 2)


def solution(mesh):
    return jax.shard_map(
        per_device,
        mesh=mesh,
        in_specs=(
            P("src", None, "space", None),
            P("src", None, "space", None),
            P(None, "space", "src"),
            P("src", None),
            P("src", None, None),
            P("src", None),
        ),
        out_specs=P(None, "space", "src"),
        check_vma=False,
    )
```

time: 189 us -> 98.6 us (0.52)
  other arithmetic: 72.1 us -> 3.31 us
  Pallas kernels: 0 us -> 42.8 us
  blocking collectives: 32.1 us -> 0 us
  waiting for transfers between devices: 36.8 us -> 16 us
  starting transfers between devices: 15 us -> 31.5 us
  between operations: 14 us -> 0.17 us
  local copies, waits for them, and re-layouts: 17.7 us -> 4.33 us
    pallas_call x0 -> x6, Pallas kernels: none -> 42.8 us  [the longest x1 15.4 us: forward_solve(): pl.pallas_call(functools.partial(forward_kernel, groups), out_shape=(jax....]
    psum x1 -> x0, waiting for transfers between devices: 36.8 us -> none  [per_device(): summed = lax.psum(local_terms, 'src')]
    scatter-add x2 -> x0, other arithmetic: 36.6 us -> none  [surface_source(): plane = jnp.zeros((sources_here, span * columns), jnp.float32).at[source_...]
    add x6 -> x4, other arithmetic: 21.8 us -> 2.7 us  [the longest x1 1.49 us: per_device(): total = total + exchange(blocks[k], 'src', k)]
    ppermute x6 -> x15, starting transfers between devices: 15 us -> 31.5 us  [the longest x9 18.6 us: exchange(): return lax.ppermute(value, axis, [(i, i ^ mask) for i in range(count)])]
    psum x1 -> x0, blocking collectives: 16.1 us -> none  [per_device(): predicted = lax.psum(local_readings, 'space')]
    all_gather x1 -> x0, blocking collectives: 16 us -> none  [per_device(): whole_sigma = lax.all_gather(conductivity, 'src', axis=2, tiled=True)]
    ppermute x6 -> x15, waiting for transfers between devices: 0.02 us -> 16 us  [the longest x9 11.1 us: exchange(): return lax.ppermute(value, axis, [(i, i ^ mask) for i in range(count)])]
  transfers between devices with their start and end apart: 7 -> 15, of which waited for: 1 -> 6; matrix products, arithmetic and copies ran while one was open for 36% -> 3% of each run, Pallas kernels for 0% -> 29%
where the time goes in v1:
time: 98.6 us; the launch traced here: 98.1 us
  Pallas kernels  42.8 us (43%)
  starting transfers between devices  31.5 us (32%)
  waiting for transfers between devices  16 us (16%)
  local copies, waits for them, and re-layouts  4.33 us (4%)
  other arithmetic  3.31 us (3%)
    ppermute x9, starting transfers between devices, exchange(): return lax.ppermute(value, axis, [(i, i ^ mask) for i in range(count)])  18.6 us
    pallas_call x1, Pallas kernels, forward_solve(): pl.pallas_call(functools.partial(forward_kernel, groups), out_shape=(jax....  15.4 us
    pallas_call x1, Pallas kernels, adjoint_solve(): pl.pallas_call(functools.partial(adjoint_kernel, rows, columns), out_shap...  14.5 us
    ppermute x9, waiting for transfers between devices, exchange(): return lax.ppermute(value, axis, [(i, i ^ mask) for i in range(count)])  11.1 us
    ppermute x3, starting transfers between devices, shift_down(): return lax.ppermute(value, axis, [(i, i + 1) for i in range(count - 1)])  9.03 us
    pallas_call x1, Pallas kernels, adjoint_first(): pl.pallas_call(functools.partial(adjoint_first_kernel, groups), out_shape...  6.65 us
    ppermute x3, waiting for transfers between devices, shift_up(): return lax.ppermute(value, axis, [(i + 1, i) for i in range(count - 1)])  4.84 us
    pallas_call x2, Pallas kernels, make_halos(): pl.pallas_call(functools.partial(halo_kernel, groups), out_shape=(shape,...  4.48 us
  transfers between devices with their start and end apart: 15, of which 6 were waited for; matrix products, arithmetic and copies ran while one was open for 3% of the time, Pallas kernels for 29%

profile of v1, /device:TPU:0, one launch (start us, length us, event | category | flops | bytes accessed | tf_op | source)
XLA Modules:
  0.0 98.1 jit_solution(9159999826664180655)
XLA Ops:
  0.0 3.1 %collective-permute-start = (f32[4,16,256]{2,1,0:T(8,128)}, f32[4,16,256]{2,1,0:T(8,128)S(1)}, u32[]{:S(2)}, u32[]{:S(2)}) collective-permute-start(f32[4,16,256]{2,1,0:T(8,128)} %refs_0_.1), channel_id=1, source_target_pairs={{0,1},{1,0},{2,3},{3,2},{4,5},{5,4},{6,7},{7,6},{8,9},{9,8},{10,11... | collective-permute-start | bytes 196616 | tf_op jit(solution)/shard_map/ppermute | solution.py:458
  3.1 2.2 %halo.2 = (f32[4,4,40,128]{3,2,1,0:T(8,128)}, f32[4,4,40,128]{3,2,1,0:T(8,128)}) custom-call(f32[4,4,16,1024]{3,2,1,0:T(8,128)} %x_ref.5), custom_call_target="tpu_custom_call" | custom-call | tf_op jit(solution)/shard_map/halo/pallas_call | solution.py:101
  5.4 1.5 %collective-permute-start.5 = (f32[4,4,40,128]{3,2,1,0:T(8,128)}, f32[4,4,40,128]{3,2,1,0:T(8,128)S(1)}, u32[]{:S(2)}, u32[]{:S(2)}) collective-permute-start(f32[4,4,40,128]{3,2,1,0:T(8,128)} %get-tuple-element.25), channel_id=1, source_target_pairs={{0,4},{4,8},{8,12},{12,16},{16,20},{20,24},{24,28},{1,5},{5,9},{9,... | collective-permute-start | bytes 983048 | tf_op jit(solution)/shard_map/ppermute | solution.py:463
  6.8 0.0 copy-start.11
  6.9 1.3 %collective-permute-start.6 = (f32[4,4,40,128]{3,2,1,0:T(8,128)}, f32[4,4,40,128]{3,2,1,0:T(8,128)S(1)}, u32[]{:S(2)}, u32[]{:S(2)}) collective-permute-start(f32[4,4,40,128]{3,2,1,0:T(8,128)} %get-tuple-element.26), channel_id=1, source_target_pairs={{4,0},{8,4},{12,8},{16,12},{20,16},{24,20},{28,24},{5,1},{9,5},{13... | collective-permute-start | bytes 983048 | tf_op jit(solution)/shard_map/ppermute | solution.py:468
  8.2 2.7 %collective-permute-start.1 = (f32[4,16,256]{2,1,0:T(8,128)}, f32[4,16,256]{2,1,0:T(8,128)S(1)}, u32[]{:S(2)}, u32[]{:S(2)}) collective-permute-start(f32[4,16,256]{2,1,0:T(8,128)} %refs_0_.1), channel_id=1, source_target_pairs={{0,2},{1,3},{2,0},{3,1},{4,6},{5,7},{6,4},{7,5},{8,10},{9,11},{10,... | collective-permute-start | bytes 196616 | tf_op jit(solution)/shard_map/ppermute | solution.py:458
  10.8 2.2 %halo.3 = (f32[4,4,40,128]{3,2,1,0:T(8,128)}, f32[4,4,40,128]{3,2,1,0:T(8,128)}) custom-call(f32[4,4,16,1024]{3,2,1,0:T(8,128)} %x_ref.7), custom_call_target="tpu_custom_call" | custom-call | tf_op jit(solution)/shard_map/halo/pallas_call | solution.py:101
  13.1 4.3 %collective-permute-start.10 = (f32[4,4,40,128]{3,2,1,0:T(8,128)}, f32[4,4,40,128]{3,2,1,0:T(8,128)S(1)}, u32[]{:S(2)}, u32[]{:S(2)}) collective-permute-start(f32[4,4,40,128]{3,2,1,0:T(8,128)} %get-tuple-element.28), channel_id=1, source_target_pairs={{0,4},{4,8},{8,12},{12,16},{16,20},{20,24},{24,28},{1,5},{5,9},{9,... | collective-permute-start | bytes 983048 | tf_op jit(solution)/shard_map/ppermute | solution.py:463
  17.4 0.0 collective-permute-done.refs_1_
  17.4 0.0 copy-start.7
  17.4 1.3 %collective-permute-start.11 = (f32[4,4,40,128]{3,2,1,0:T(8,128)}, f32[4,4,40,128]{3,2,1,0:T(8,128)S(1)}, u32[]{:S(2)}, u32[]{:S(2)}) collective-permute-start(f32[4,4,40,128]{3,2,1,0:T(8,128)} %get-tuple-element.29), channel_id=1, source_target_pairs={{4,0},{8,4},{12,8},{16,12},{20,16},{24,20},{28,24},{5,1},{9,5},{13... | collective-permute-start | bytes 983048 | tf_op jit(solution)/shard_map/ppermute | solution.py:468
  18.7 0.0 collective-permute-done.1.refs_2_
  18.7 0.3 collective-permute-start.2
  19.0 5.9 %collective-permute-done.2.refs_3_ = f32[4,16,256]{2,1,0:T(8,128)S(1)} collective-permute-done((f32[4,16,256]{2,1,0:T(8,128)S(1)}, f32[4,16,256]{2,1,0:T(8,128)S(1)}, u32[]{:S(2)}, u32[]{:S(2)}) %collective-permute-start.2) | collective-permute-done | bytes 65568 | tf_op jit(solution)/shard_map/ppermute | solution.py:458
  24.9 0.6 copy-done.9
  25.6 1.8 %sigma.1 = (f32[4,128,128]{2,1,0:T(8,128)}, f32[4,40,128]{2,1,0:T(8,128)}, f32[4,40,128]{2,1,0:T(8,128)}) custom-call(s32[1]{0:T(128)} %bitcast.1.me_ref, f32[4,16,256]{2,1,0:T(8,128)} %refs_0_.1, f32[4,16,256]{2,1,0:T(8,128)} %copy-done.7, f32[4,16,256]{2,1,0:T(8,128)} %copy-done.8, f32[4,16,256]{2,1,0:T(8,128)} %copy-done.9), custom_call_target="tpu_custom_call" | custom-call | tf_op jit(solution)/shard_map/sigma/pallas_call | solution.py:132
  27.3 3.3 %collective-permute-start.3 = (f32[4,40,128]{2,1,0:T(8,128)}, f32[4,40,128]{2,1,0:T(8,128)S(1)}, u32[]{:S(2)}, u32[]{:S(2)}) collective-permute-start(f32[4,40,128]{2,1,0:T(8,128)} %get-tuple-element.23), channel_id=1, source_target_pairs={{0,4},{4,8},{8,12},{12,16},{16,20},{20,24},{24,28},{1,5},{5,9},{9,... | collective-permute-start | bytes 245768 | tf_op jit(solution)/shard_map/ppermute | solution.py:463
  30.6 0.6 reshape.7.nodes_ref
  31.3 0.7 copy.7.electrodes_ref
  31.9 0.0 collective-permute-done.3.sigma_top
  31.9 1.3 %collective-permute-start.4 = (f32[4,40,128]{2,1,0:T(8,128)}, f32[4,40,128]{2,1,0:T(8,128)S(1)}, u32[]{:S(2)}, u32[]{:S(2)}) collective-permute-start(f32[4,40,128]{2,1,0:T(8,128)} %get-tuple-element.24), channel_id=1, source_target_pairs={{4,0},{8,4},{12,8},{16,12},{20,16},{24,20},{28,24},{5,1},{9,5},{13... | collective-permute-start | bytes 245768 | tf_op jit(solution)/shard_map/ppermute | solution.py:468
  33.2 0.6 pad_add_fusion.position_ref
  33.8 4.8 %collective-permute-done.4.sigma_bottom = f32[4,40,128]{2,1,0:T(8,128)S(1)} collective-permute-done((f32[4,40,128]{2,1,0:T(8,128)}, f32[4,40,128]{2,1,0:T(8,128)S(1)}, u32[]{:S(2)}, u32[]{:S(2)}) %collective-permute-start.4) | collective-permute-done | bytes 81952 | tf_op jit(solution)/shard_map/ppermute | solution.py:468
  38.7 0.0 collective-permute-done.5.top_ref
  38.7 0.0 collective-permute-done.6.bottom_ref
  38.7 0.6 copy-done.5
  39.3 0.1 copy-done.2
  39.4 0.1 copy-done.3
  39.6 15.4 %forward.1 = (f32[6,4,208,128]{3,2,1,0:T(8,128)}, f32[208,128]{1,0:T(8,128)}, f32[4,4,208,128]{3,2,1,0:T(8,128)}, f32[1,256]{1,0:T(1,128)}) custom-call(s32[2]{0:T(128)} %pad_add_fusion.position_ref, s32[4,2]{1,0:T(4,128)} %copy.7.electrodes_ref, f32[4,128,128]{2,1,0:T(8,128)} %get-tuple-element.22.sigma_ref, f32[4,40,128]{2,1,0:T(8,128)} %copy-done.4, ...), custom_call_target="tpu_custom_call" | custom-call | tf_op jit(solution)/shard_map/forward/pallas_call | solution.py:279
  54.9 3.6 %collective-permute-start.7 = (f32[1,256]{1,0:T(1,128)}, f32[1,256]{1,0:T(1,128)S(1)}, u32[]{:S(2)}, u32[]{:S(2)}) collective-permute-start(f32[1,256]{1,0:T(1,128)} %get-tuple-element.27), channel_id=1, source_target_pairs={{0,4},{4,0},{8,12},{12,8},{16,20},{20,16},{24,28},{28,24},{1,5},{5... | collective-permute-start | bytes 3080 | tf_op jit(solution)/shard_map/ppermute | solution.py:458
  58.5 1.0 %collective-permute-done.7 = f32[1,256]{1,0:T(1,128)S(1)} collective-permute-done((f32[1,256]{1,0:T(1,128)}, f32[1,256]{1,0:T(1,128)S(1)}, u32[]{:S(2)}, u32[]{:S(2)}) %collective-permute-start.7) | collective-permute-done | bytes 1056 | tf_op jit(solution)/shard_map/ppermute | solution.py:458
  59.6 0.7 add.18
  60.2 3.7 %collective-permute-start.8 = (f32[1,256]{1,0:T(1,128)S(1)}, f32[1,256]{1,0:T(1,128)S(1)}, u32[]{:S(2)}, u32[]{:S(2)}) collective-permute-start(f32[1,256]{1,0:T(1,128)S(1)} %add.18), channel_id=1, source_target_pairs={{0,8},{4,12},{8,0},{12,4},{16,24},{20,28},{24,16},{28,20},{1,9},{5... | collective-permute-start | bytes 3080 | tf_op jit(solution)/shard_map/ppermute | solution.py:458
  63.9 1.6 %collective-permute-done.8 = f32[1,256]{1,0:T(1,128)S(1)} collective-permute-done((f32[1,256]{1,0:T(1,128)S(1)}, f32[1,256]{1,0:T(1,128)S(1)}, u32[]{:S(2)}, u32[]{:S(2)}) %collective-permute-start.8) | collective-permute-done | bytes 1056 | tf_op jit(solution)/shard_map/ppermute | solution.py:458
  65.5 0.8 collective-permute-start.9
  66.3 0.6 reshape.8.observed_ref
  67.0 0.0 collective-permute-done.11.bottom_ref
  67.0 0.8 copy-done
  67.7 0.1 copy-done.1
  67.9 6.7 %adjoint_first.1 = (f32[4,4,208,128]{3,2,1,0:T(8,128)}, f32[4,4,208,128]{3,2,1,0:T(8,128)}) custom-call(f32[4,4,16,1024]{3,2,1,0:T(8,128)} %x_ref.7, f32[4,4,40,128]{3,2,1,0:T(8,128)} %copy-done, f32[4,4,40,128]{3,2,1,0:T(8,128)} %copy-done.1, f32[6,4,208,128]{3,2,1,0:T(8,128)} %get-tuple-element.30.coef), custom_call_target="tpu_custom_call" | custom-call | tf_op jit(solution)/shard_map/adjoint_first/pallas_call | solution.py:308
  74.5 0.5 add.20.readings_ref
  75.1 14.5 %adjoint.1 = (f32[4,16,256]{2,1,0:T(8,128)}, f32[4,16,256]{2,1,0:T(8,128)}, f32[4,16,256]{2,1,0:T(8,128)}, f32[4,16,256]{2,1,0:T(8,128)}) custom-call(s32[2]{0:T(128)} %pad_add_fusion.position_ref, s32[1,256]{1,0:T(1,128)} %reshape.7.nodes_ref, f32[1,256]{1,0:T(1,128)} %add.20.readings_ref, f32[1,256]{1,0:T(1,128)} %reshape.8.observed_ref, ...), custom_call_target="tpu_custom_call" | custom-call | tf_op jit(solution)/shard_map/adjoint/pallas_call | solution.py:436
  89.6 0.2 collective-permute-start.12
  89.8 0.0 collective-permute-start.13
  89.8 4.2 %collective-permute-start.14 = (f32[4,16,256]{2,1,0:T(8,128)}, f32[4,16,256]{2,1,0:T(8,128)S(1)}, u32[]{:S(2)}, u32[]{:S(2)}) collective-permute-start(f32[4,16,256]{2,1,0:T(8,128)} %get-tuple-element.38), channel_id=1, source_target_pairs={{0,1},{1,0},{2,3},{3,2},{4,5},{5,4},{6,7},{7,6},{8,9},{9,8},{10,11... | collective-permute-start | bytes 196616 | tf_op jit(solution)/shard_map/ppermute | solution.py:458
  94.0 1.9 %collective-permute-done.12 = f32[4,16,256]{2,1,0:T(8,128)S(1)} collective-permute-done((f32[4,16,256]{2,1,0:T(8,128)}, f32[4,16,256]{2,1,0:T(8,128)S(1)}, u32[]{:S(2)}, u32[]{:S(2)}) %collective-permute-start.12) | collective-permute-done | bytes 65568 | tf_op jit(solution)/shard_map/ppermute | solution.py:458
  95.9 0.7 collective-permute-done.14
  96.6 1.5 %add_add_fusion = f32[4,16,256]{2,1,0:T(8,128)} fusion(f32[4,16,256]{2,1,0:T(8,128)S(1)} %collective-permute-done.14, f32[4,16,256]{2,1,0:T(8,128)S(1)} %collective-permute-done.13, f32[4,16,256]{2,1,0:T(8,128)} %get-tuple-element.35, f32[4,16,256]{2,1,0:T(8,128)S(1)} %collective-permute-done.12), kind=kLoop, calls=%fused_computation | loop fusion | flops 49152 | bytes 327680 | tf_op jit(solution)/shard_map/add | solution.py:517
  (23 shorter events, 0.0 us)
Async XLA Ops:
  0.0 18.7 %copy-start.6 = (f32[4,16,256]{2,1,0:T(8,128)S(1)}, f32[4,16,256]{2,1,0:T(8,128)}, u32[]{:S(2)}) copy-start(f32[4,16,256]{2,1,0:T(8,128)} %refs_0_.1) | copy-start | bytes 196612
  0.0 30.6 %copy-start.10 = (s32[4,32,2]{1,2,0:T(2,128)S(1)}, s32[4,32,2]{1,2,0:T(2,128)}, u32[]{:S(2)}) copy-start(s32[4,32,2]{1,2,0:T(2,128)} %param.10) | copy-start | bytes 3076
  0.0 31.2 %copy-start.12 = (s32[4,2]{0,1:T(2,128)S(1)}, s32[4,2]{0,1:T(2,128)}, u32[]{:S(2)}) copy-start(s32[4,2]{0,1:T(2,128)} %param.9) | copy-start | bytes 100
  0.0 17.4 %collective-permute-start = (f32[4,16,256]{2,1,0:T(8,128)}, f32[4,16,256]{2,1,0:T(8,128)S(1)}, u32[]{:S(2)}, u32[]{:S(2)}) collective-permute-start(f32[4,16,256]{2,1,0:T(8,128)} %refs_0_.1), channel_id=1, source_target_pairs={{0,1},{1,0},{2,3},{3,2},{4,5},{5,4},{6,7},{7,6},{8,9},{9,8},{10,11... | collective-permute-start | bytes 196616 | tf_op jit(solution)/shard_map/ppermute | solution.py:458
  5.4 33.3 %collective-permute-start.5 = (f32[4,4,40,128]{3,2,1,0:T(8,128)}, f32[4,4,40,128]{3,2,1,0:T(8,128)S(1)}, u32[]{:S(2)}, u32[]{:S(2)}) collective-permute-start(f32[4,4,40,128]{3,2,1,0:T(8,128)} %get-tuple-element.25), channel_id=1, source_target_pairs={{0,4},{4,8},{8,12},{12,16},{16,20},{20,24},{24,28},{1,5},{5,9},{9,... | collective-permute-start | bytes 983048 | tf_op jit(solution)/shard_map/ppermute | solution.py:463
  6.8 59.5 %copy-start.11 = (f32[4,32]{1,0:T(4,128)S(1)}, f32[4,32]{1,0:T(4,128)}, u32[]{:S(2)}) copy-start(f32[4,32]{1,0:T(4,128)} %param.11) | copy-start | bytes 1540
  6.9 31.8 %collective-permute-start.6 = (f32[4,4,40,128]{3,2,1,0:T(8,128)}, f32[4,4,40,128]{3,2,1,0:T(8,128)S(1)}, u32[]{:S(2)}, u32[]{:S(2)}) collective-permute-start(f32[4,4,40,128]{3,2,1,0:T(8,128)} %get-tuple-element.26), channel_id=1, source_target_pairs={{4,0},{8,4},{12,8},{16,12},{20,16},{24,20},{28,24},{5,1},{9,5},{13... | collective-permute-start | bytes 983048 | tf_op jit(solution)/shard_map/ppermute | solution.py:468
  8.2 10.5 %collective-permute-start.1 = (f32[4,16,256]{2,1,0:T(8,128)}, f32[4,16,256]{2,1,0:T(8,128)S(1)}, u32[]{:S(2)}, u32[]{:S(2)}) collective-permute-start(f32[4,16,256]{2,1,0:T(8,128)} %refs_0_.1), channel_id=1, source_target_pairs={{0,2},{1,3},{2,0},{3,1},{4,6},{5,7},{6,4},{7,5},{8,10},{9,11},{10,... | collective-permute-start | bytes 196616 | tf_op jit(solution)/shard_map/ppermute | solution.py:458
  13.1 53.9 %collective-permute-start.10 = (f32[4,4,40,128]{3,2,1,0:T(8,128)}, f32[4,4,40,128]{3,2,1,0:T(8,128)S(1)}, u32[]{:S(2)}, u32[]{:S(2)}) collective-permute-start(f32[4,4,40,128]{3,2,1,0:T(8,128)} %get-tuple-element.28), channel_id=1, source_target_pairs={{0,4},{4,8},{8,12},{12,16},{16,20},{20,24},{24,28},{1,5},{5,9},{9,... | collective-permute-start | bytes 983048 | tf_op jit(solution)/shard_map/ppermute | solution.py:463
  17.4 7.6 %copy-start.7 = (f32[4,16,256]{2,1,0:T(8,128)}, f32[4,16,256]{2,1,0:T(8,128)S(1)}, u32[]{:S(2)}) copy-start(f32[4,16,256]{2,1,0:T(8,128)S(1)} %collective-permute-done.refs_1_) | copy-start | bytes 196612
  17.4 49.6 %collective-permute-start.11 = (f32[4,4,40,128]{3,2,1,0:T(8,128)}, f32[4,4,40,128]{3,2,1,0:T(8,128)S(1)}, u32[]{:S(2)}, u32[]{:S(2)}) collective-permute-start(f32[4,4,40,128]{3,2,1,0:T(8,128)} %get-tuple-element.29), channel_id=1, source_target_pairs={{4,0},{8,4},{12,8},{16,12},{20,16},{24,20},{28,24},{5,1},{9,5},{13... | collective-permute-start | bytes 983048 | tf_op jit(solution)/shard_map/ppermute | solution.py:468
  18.7 6.2 %copy-start.8 = (f32[4,16,256]{2,1,0:T(8,128)}, f32[4,16,256]{2,1,0:T(8,128)S(1)}, u32[]{:S(2)}) copy-start(f32[4,16,256]{2,1,0:T(8,128)S(1)} %collective-permute-done.1.refs_2_) | copy-start | bytes 196612
  18.7 6.2 %collective-permute-start.2 = (f32[4,16,256]{2,1,0:T(8,128)S(1)}, f32[4,16,256]{2,1,0:T(8,128)S(1)}, u32[]{:S(2)}, u32[]{:S(2)}) collective-permute-start(f32[4,16,256]{2,1,0:T(8,128)S(1)} %copy-done.6), channel_id=1, source_target_pairs={{0,3},{1,2},{2,1},{3,0},{4,7},{5,6},{6,5},{7,4},{8,11},{9,10},{10,... | collective-permute-start | bytes 196616 | tf_op jit(solution)/shard_map/ppermute | solution.py:458
  24.9 0.6 copy-start.9
  27.3 4.6 %collective-permute-start.3 = (f32[4,40,128]{2,1,0:T(8,128)}, f32[4,40,128]{2,1,0:T(8,128)S(1)}, u32[]{:S(2)}, u32[]{:S(2)}) collective-permute-start(f32[4,40,128]{2,1,0:T(8,128)} %get-tuple-element.23), channel_id=1, source_target_pairs={{0,4},{4,8},{8,12},{12,16},{16,20},{20,24},{24,28},{1,5},{5,9},{9,... | collective-permute-start | bytes 245768 | tf_op jit(solution)/shard_map/ppermute | solution.py:463
  31.9 6.8 %copy-start.4 = (f32[4,40,128]{2,1,0:T(8,128)}, f32[4,40,128]{2,1,0:T(8,128)S(1)}, u32[]{:S(2)}) copy-start(f32[4,40,128]{2,1,0:T(8,128)S(1)} %collective-permute-done.3.sigma_top) | copy-start | bytes 245764
  31.9 6.7 %collective-permute-start.4 = (f32[4,40,128]{2,1,0:T(8,128)}, f32[4,40,128]{2,1,0:T(8,128)S(1)}, u32[]{:S(2)}, u32[]{:S(2)}) collective-permute-start(f32[4,40,128]{2,1,0:T(8,128)} %get-tuple-element.24), channel_id=1, source_target_pairs={{4,0},{8,4},{12,8},{16,12},{20,16},{24,20},{28,24},{5,1},{9,5},{13... | collective-permute-start | bytes 245768 | tf_op jit(solution)/shard_map/ppermute | solution.py:468
  38.7 0.6 copy-start.5
  38.7 0.8 copy-start.2
  38.7 0.9 copy-start.3
  54.9 4.7 %collective-permute-start.7 = (f32[1,256]{1,0:T(1,128)}, f32[1,256]{1,0:T(1,128)S(1)}, u32[]{:S(2)}, u32[]{:S(2)}) collective-permute-start(f32[1,256]{1,0:T(1,128)} %get-tuple-element.27), channel_id=1, source_target_pairs={{0,4},{4,0},{8,12},{12,8},{16,20},{20,16},{24,28},{28,24},{1,5},{5... | collective-permute-start | bytes 3080 | tf_op jit(solution)/shard_map/ppermute | solution.py:458
  60.2 5.2 %collective-permute-start.8 = (f32[1,256]{1,0:T(1,128)S(1)}, f32[1,256]{1,0:T(1,128)S(1)}, u32[]{:S(2)}, u32[]{:S(2)}) collective-permute-start(f32[1,256]{1,0:T(1,128)S(1)} %add.18), channel_id=1, source_target_pairs={{0,8},{4,12},{8,0},{12,4},{16,24},{20,28},{24,16},{28,20},{1,9},{5... | collective-permute-start | bytes 3080 | tf_op jit(solution)/shard_map/ppermute | solution.py:458
  65.5 9.0 %collective-permute-start.9 = (f32[1,256]{1,0:T(1,128)S(1)}, f32[1,256]{1,0:T(1,128)S(1)}, u32[]{:S(2)}, u32[]{:S(2)}) collective-permute-start(f32[1,256]{1,0:T(1,128)S(1)} %add.19), channel_id=1, source_target_pairs={{0,16},{4,20},{8,24},{12,28},{16,0},{20,4},{24,8},{28,12},{1,17},{... | collective-permute-start | bytes 3080 | tf_op jit(solution)/shard_map/ppermute | solution.py:458
  66.9 0.8 copy-start
  67.0 0.9 copy-start.1
  89.6 6.3 %collective-permute-start.12 = (f32[4,16,256]{2,1,0:T(8,128)}, f32[4,16,256]{2,1,0:T(8,128)S(1)}, u32[]{:S(2)}, u32[]{:S(2)}) collective-permute-start(f32[4,16,256]{2,1,0:T(8,128)} %get-tuple-element.36), channel_id=1, source_target_pairs={{0,3},{1,2},{2,1},{3,0},{4,7},{5,6},{6,5},{7,4},{8,11},{9,10},{10,... | collective-permute-start | bytes 196616 | tf_op jit(solution)/shard_map/ppermute | solution.py:458
  89.8 6.1 %collective-permute-start.13 = (f32[4,16,256]{2,1,0:T(8,128)}, f32[4,16,256]{2,1,0:T(8,128)S(1)}, u32[]{:S(2)}, u32[]{:S(2)}) collective-permute-start(f32[4,16,256]{2,1,0:T(8,128)} %get-tuple-element.37), channel_id=1, source_target_pairs={{0,2},{1,3},{2,0},{3,1},{4,6},{5,7},{6,4},{7,5},{8,10},{9,11},{10,... | collective-permute-start | bytes 196616 | tf_op jit(solution)/shard_map/ppermute | solution.py:458
  89.8 6.8 %collective-permute-start.14 = (f32[4,16,256]{2,1,0:T(8,128)}, f32[4,16,256]{2,1,0:T(8,128)S(1)}, u32[]{:S(2)}, u32[]{:S(2)}) collective-permute-start(f32[4,16,256]{2,1,0:T(8,128)} %get-tuple-element.38), channel_id=1, source_target_pairs={{0,1},{1,0},{2,3},{3,2},{4,5},{5,4},{6,7},{7,6},{8,9},{9,8},{10,11... | collective-permute-start | bytes 196616 | tf_op jit(solution)/shard_map/ppermute | solution.py:458

commit v2 on v1

v2 whole, which is shorter than its diff:
```python
import functools
import math

import jax
import jax.numpy as jnp
from jax import lax
from jax.experimental import pallas as pl
from jax.experimental.pallas import tpu as pltpu
from jax.sharding import PartitionSpec as P


SWEEPS = 4
GAMMA = 0.5
CURRENT = 4.0
THETA = 1.025
DELTA = 0.975
LANES = 128
HALO = SWEEPS + 1

VMEM = pl.BlockSpec(memory_space=pltpu.VMEM)
SMEM = pl.BlockSpec(memory_space=pltpu.SMEM)
GRANT = pltpu.CompilerParams(vmem_limit_bytes=20 * 1024 * 1024)


def product_form():
    roots = [THETA + DELTA * math.cos((2 * i + 1) * math.pi / (2 * SWEEPS)) for i in range(SWEEPS)]
    order = sorted(roots)
    order = [order[i // 2] if i % 2 == 0 else order[-1 - i // 2] for i in range(SWEEPS)]
    steps, scale = [], 1.0
    for root in order:
        steps.append((root - 1.0, 1.0 / scale))
        scale /= root
    return steps, scale


STEPS, FINAL = product_form()


def rows_of(start, count, groups):
    begin = start * groups
    if not isinstance(begin, int):
        begin = pl.multiple_of(begin, groups)
    return pl.ds(begin, count * groups)


def from_right(v, last_lane):
    groups = v.shape[0]
    turned = pltpu.roll(v, LANES - 1, 1)
    return jnp.where(last_lane, pltpu.roll(turned, groups - 1, 0), turned)


def from_left(v, first_lane):
    turned = pltpu.roll(v, 1, 1)
    return jnp.where(first_lane, pltpu.roll(turned, 1, 0), turned)


def lane_masks(groups):
    lane = lax.broadcasted_iota(jnp.int32, (groups, LANES), 1)
    group = lax.broadcasted_iota(jnp.int32, (groups, LANES), 0)
    first_lane = lane == 0
    last_lane = lane == LANES - 1
    first_column = first_lane & (group == 0)
    last_column = last_lane & (group == groups - 1)
    return first_lane, last_lane, first_column, last_column


def three_parts(x):
    high = x.astype(jnp.bfloat16)
    rest = x - high.astype(jnp.float32)
    middle = rest.astype(jnp.bfloat16)
    low = (rest - middle.astype(jnp.float32)).astype(jnp.bfloat16)
    return jnp.concatenate([high, middle, low], axis=0)


def column_hits(columns, j):
    nodes = columns.shape[1]
    c = lax.broadcasted_iota(jnp.int32, (LANES, nodes), 0) + j * LANES
    return jnp.where(c == columns, 1.0, 0.0).astype(jnp.bfloat16)


def spread_kernel(groups, x_ref, a_ref, x_wide, a_wide, first_ref, last_ref):
    sources, layers, rows, _ = x_ref.shape
    for i, (field, wide) in enumerate(((x_ref, x_wide), (a_ref, a_wide))):
        for s in range(sources):
            for l in range(layers):
                for j in range(groups):
                    wide[s, l, pl.ds(HALO * groups + j, rows, stride=groups), :] = field[
                        s, l, :, j * LANES : (j + 1) * LANES
                    ]
        first_ref[i] = wide[:, :, HALO * groups : 2 * HALO * groups, :]
        last_ref[i] = wide[:, :, rows * groups : (HALO + rows) * groups, :]


def spread_rows(x, a):
    sources, layers, rows, columns = x.shape
    groups = columns // LANES
    wide = jax.ShapeDtypeStruct((sources, layers, (rows + 2 * HALO) * groups, LANES), jnp.float32)
    halo = jax.ShapeDtypeStruct((2, sources, layers, HALO * groups, LANES), jnp.float32)
    return pl.pallas_call(
        functools.partial(spread_kernel, groups),
        out_shape=(wide, wide, halo, halo),
        in_specs=[VMEM, VMEM],
        out_specs=(VMEM,) * 4,
        compiler_params=GRANT,
        name="spread",
    )(x, a)


def nodes_kernel(receivers_ref, observed_ref, nodes_ref, measured_ref):
    sources, ends, count = receivers_ref.shape
    for s in range(sources):
        for end in range(ends):
            lanes = pl.ds((s * ends + end) * count, count)
            nodes_ref[:, lanes] = receivers_ref[s, end : end + 1, :]
            seen = observed_ref[s : s + 1, :]
            measured_ref[:, lanes] = seen if end == 0 else -seen


def lay_out_nodes(receivers, observed):
    sources, ends, count = receivers.shape
    total = sources * ends * count
    return pl.pallas_call(
        nodes_kernel,
        out_shape=(jax.ShapeDtypeStruct((1, total), jnp.int32), jax.ShapeDtypeStruct((1, total), jnp.float32)),
        in_specs=[VMEM, VMEM],
        out_specs=(VMEM, VMEM),
        compiler_params=GRANT,
        name="nodes",
    )(receivers, observed)


def sigma_kernel(groups, *refs):
    pieces, (wide_ref, first_ref, last_ref, stage) = refs[:-4], refs[-4:]
    count = len(pieces)
    layers, rows, share = pieces[0].shape
    me = lax.axis_index("src") if count > 1 else 0
    for k, piece in enumerate(pieces):
        stage[me ^ k] = piece[...]
    per = share // LANES
    for q in range(count):
        for l in range(layers):
            for t in range(per):
                wide_ref[l, pl.ds(HALO * groups + q * per + t, rows, stride=groups), :] = stage[
                    q, l, :, t * LANES : (t + 1) * LANES
                ]
    first_ref[...] = wide_ref[:, HALO * groups : 2 * HALO * groups, :]
    last_ref[...] = wide_ref[:, rows * groups : (HALO + rows) * groups, :]


def assemble_sigma(pieces, groups):
    layers, rows, share = pieces[0].shape
    wide = jax.ShapeDtypeStruct((layers, (rows + 2 * HALO) * groups, LANES), jnp.float32)
    halo = jax.ShapeDtypeStruct((layers, HALO * groups, LANES), jnp.float32)
    return pl.pallas_call(
        functools.partial(sigma_kernel, groups),
        out_shape=(wide, halo, halo),
        in_specs=[VMEM] * len(pieces),
        out_specs=(VMEM, VMEM, VMEM),
        scratch_shapes=[pltpu.VMEM((len(pieces), layers, rows, share), jnp.float32)],
        compiler_params=GRANT,
        name="sigma",
    )(*pieces)


def row_numbers(segments):
    (first, middle), count = segments[0], segments[0][1] - segments[0][0]
    if len(segments) == 1:
        return count, lambda i: first + i
    start, end = segments[1]

    def number(i):
        if isinstance(i, int):
            return first + i if i < count else start + i - count
        return first + i + jnp.where(i >= count, start - middle, 0)

    return count + end - start, number


def coefficient_rows(sigma, coef, surface, groups, segments):
    layers = sigma.shape[0]
    first_lane, last_lane, first_column, last_column = lane_masks(groups)
    count, number = row_numbers(segments)

    def body(i, carry):
        e = number(i)
        here = rows_of(e, 1, groups)
        above = rows_of(e - 1, 1, groups)
        below = rows_of(e + 1, 1, groups)
        centre = [sigma[l, here, :] for l in range(layers)]
        for l in range(layers):
            c = centre[l]
            up = 0.5 * (c + sigma[l, above, :])
            down = 0.5 * (c + sigma[l, below, :])
            left = 0.5 * (c + jnp.where(first_column, 0.0, from_left(c, first_lane)))
            right = 0.5 * (c + jnp.where(last_column, 0.0, from_right(c, last_lane)))
            lower = 0.5 * (c + centre[l - 1]) if l > 0 else 0.5 * c
            upper = 0.5 * (c + centre[l + 1]) if l + 1 < layers else 0.5 * c
            diagonal = up + down + left + right + lower + upper + GAMMA * c
            inside = c > 0.0
            inverse = jnp.where(inside, 1.0 / jnp.where(inside, diagonal, 1.0), 0.0)
            coef[0, l, here, :] = up * inverse
            coef[1, l, here, :] = down * inverse
            coef[2, l, here, :] = jnp.where(first_column, 0.0, left * inverse)
            coef[3, l, here, :] = jnp.where(last_column, 0.0, right * inverse)
            if l > 0:
                coef[4, l, here, :] = lower * inverse
            if l + 1 < layers:
                coef[5, l, here, :] = upper * inverse
            if l == 0:
                surface[here, :] = inverse
        return carry

    lax.fori_loop(0, count, body, 0)


def sweep(step, old, new, coef, plane, shifted, groups, segments):
    p, g = STEPS[step]
    sources, layers = old.shape[:2]
    first_lane, last_lane, _, _ = lane_masks(groups)
    count, number = row_numbers(segments)

    def turn(e):
        here = rows_of(e, 1, groups)
        before = pl.ds(e * groups - 1, groups)
        after = pl.ds(e * groups + 1, groups)
        for l in range(layers):
            for s in range(sources):
                v = old[s, l, here, :]
                shifted[0, s, l] = pltpu.roll(jnp.where(last_lane, old[s, l, before, :], v), 1, 1)
                shifted[1, s, l] = pltpu.roll(jnp.where(first_lane, old[s, l, after, :], v), LANES - 1, 1)

    def row(e):
        here = rows_of(e, 1, groups)
        above = rows_of(e - 1, 1, groups)
        below = rows_of(e + 1, 1, groups)
        for l in range(layers):
            weight = [coef[i, l, here, :] for i in range(4)]
            lower = coef[4, l, here, :] if l > 0 else None
            upper = coef[5, l, here, :] if l + 1 < layers else None
            for s in range(sources):
                total = p * old[s, l, here, :]
                total += weight[0] * old[s, l, above, :]
                total += weight[1] * old[s, l, below, :]
                total += weight[2] * shifted[0, s, l]
                total += weight[3] * shifted[1, s, l]
                if lower is not None:
                    total += lower * old[s, l - 1, here, :]
                if upper is not None:
                    total += upper * old[s, l + 1, here, :]
                if l == 0 and plane is not None:
                    amount = plane[s, here, :]
                    total += amount if g == 1.0 else g * amount
                new[s, l, here, :] = total

    def body(i, carry):
        row(number(i))
        turn(number(i + 1))
        return carry

    turn(number(0))
    lax.fori_loop(0, count - 1, body, 0)
    row(number(count - 1))


def inner_rows(step, rows):
    return [(HALO + 1 + step, HALO + rows - 1 - step)]


def outer_rows(step, rows):
    return [(1 + step, HALO + 1 + step), (HALO + rows - 1 - step, 2 * HALO + rows - 1 - step)]


def add_electrodes(electrodes_ref, plane, surface, rows, groups, segments):
    columns = groups * LANES
    first_row = lax.axis_index("space") * rows
    lowest, highest = segments[0][0], segments[-1][1] - 1
    column = lax.broadcasted_iota(jnp.int32, (groups, LANES), 0) * LANES + lax.broadcasted_iota(
        jnp.int32, (groups, LANES), 1
    )
    for s in range(plane.shape[0]):
        for k, current in enumerate((CURRENT, -CURRENT)):
            node = electrodes_ref[k, s]
            row = node // columns
            e = row - first_row + HALO
            inside = functools.reduce(jnp.logical_or, [(e >= a) & (e < b) for a, b in segments])
            here = rows_of(jnp.clip(e, lowest, highest), 1, groups)
            hit = (column == node - row * columns) & inside
            plane[s, here, :] += jnp.where(hit, current * surface[here, :], 0.0)


def inner_kernel(groups, electrodes_ref, sigma, _, wide, coef, surface, other, plane, shifted):
    rows = wide.shape[2] // groups - 2 * HALO
    segments = inner_rows(0, rows)
    coefficient_rows(sigma, coef, surface, groups, segments)
    plane[...] = jnp.zeros(plane.shape, jnp.float32)
    add_electrodes(electrodes_ref, plane, surface, rows, groups, segments)
    old, new = wide, other
    for step in range(SWEEPS):
        sweep(step, old, new, coef, plane, shifted, groups, inner_rows(step, rows))
        old, new = new, old


def inner_solve(groups, electrodes, sigma, wide):
    sources, layers, tall, _ = wide.shape
    f32 = jnp.float32
    return pl.pallas_call(
        functools.partial(inner_kernel, groups),
        out_shape=(
            jax.ShapeDtypeStruct(wide.shape, f32),
            jax.ShapeDtypeStruct((6, layers, tall, LANES), f32),
            jax.ShapeDtypeStruct((tall, LANES), f32),
            jax.ShapeDtypeStruct(wide.shape, f32),
            jax.ShapeDtypeStruct((sources, tall, LANES), f32),
        ),
        in_specs=[SMEM, VMEM, VMEM],
        out_specs=(VMEM,) * 5,
        scratch_shapes=[pltpu.VMEM((2, sources, layers, groups, LANES), f32)],
        input_output_aliases={2: 0},
        compiler_params=GRANT,
        name="inner",
    )(electrodes, sigma, wide)


def outer_kernel(
    groups, electrodes_ref, sigma_top, sigma_bottom, top_ref, bottom_ref, nodes_ref, *refs
):
    sigma, wide, coef, surface, other, plane, readings_ref, shifted = refs[6:]
    sources, _, tall, _ = wide.shape
    columns = groups * LANES
    rows = tall // groups - 2 * HALO
    first_row = lax.axis_index("space") * rows
    bottom = (HALO + rows) * groups
    sigma[:, : HALO * groups, :] = sigma_top[...]
    sigma[:, bottom:, :] = sigma_bottom[...]
    wide[:, :, : HALO * groups, :] = top_ref[0]
    wide[:, :, bottom:, :] = bottom_ref[0]
    segments = outer_rows(0, rows)
    coefficient_rows(sigma, coef, surface, groups, segments)
    add_electrodes(electrodes_ref, plane, surface, rows, groups, segments)
    old, new = wide, other
    for step in range(SWEEPS):
        sweep(step, old, new, coef, plane, shifted, groups, outer_rows(step, rows))
        old, new = new, old

    node = nodes_ref[...]
    node_row = node // columns
    node_column = node - node_row * columns
    count = node.shape[1]
    picked = jnp.zeros((3 * sources * rows, count), jnp.float32)
    for j in range(groups):
        tile = jnp.concatenate(
            [old[s, 0, pl.ds(HALO * groups + j, rows, stride=groups), :] for s in range(sources)], axis=0
        )
        picked += jnp.dot(three_parts(tile), column_hits(node_column, j), preferred_element_type=jnp.float32)
    size = sources * rows
    picked = picked[:size] + picked[size : 2 * size] + picked[2 * size :]
    r = lax.broadcasted_iota(jnp.int32, (size, count), 0)
    k = lax.broadcasted_iota(jnp.int32, (size, count), 1)
    hit = (r // rows == k // (count // sources)) & (node_row - first_row == r % rows)
    readings_ref[...] = FINAL * jnp.sum(jnp.where(hit, picked, 0.0), axis=0, keepdims=True)


def outer_solve(groups, electrodes, sigma_top, sigma_bottom, top, bottom, nodes, sigma, inner):
    carried = (sigma,) + tuple(inner)
    sources, layers = inner[0].shape[:2]
    f32 = jnp.float32
    kept = tuple(jax.ShapeDtypeStruct(x.shape, f32) for x in carried)
    return pl.pallas_call(
        functools.partial(outer_kernel, groups),
        out_shape=kept + (jax.ShapeDtypeStruct((1, nodes.shape[1]), f32),),
        in_specs=[SMEM] + [VMEM] * 11,
        out_specs=(VMEM,) * 7,
        scratch_shapes=[pltpu.VMEM((2, sources, layers, groups, LANES), f32)],
        input_output_aliases={6 + i: i for i in range(6)},
        compiler_params=GRANT,
        name="outer",
    )(electrodes, sigma_top, sigma_bottom, top, bottom, nodes, *carried)


def begin_kernel(groups, start, end, top_ref, bottom_ref, coef, *refs):
    wide, new, shifted = refs[-3:]
    if start == 1:
        rows = wide.shape[2] // groups - 2 * HALO
        wide[:, :, : HALO * groups, :] = top_ref[1]
        wide[:, :, (HALO + rows) * groups :, :] = bottom_ref[1]
    sweep(0, wide, new, coef, None, shifted, groups, [(start, end)])


def begin_adjoint(groups, part, top, bottom, coef, wide, new):
    f32 = jnp.float32
    shape = jax.ShapeDtypeStruct(wide.shape, f32)
    arguments = (top, bottom, coef, wide) + (() if new is None else (new,))
    return pl.pallas_call(
        functools.partial(begin_kernel, groups, part[0], part[-1] + 1),
        out_shape=(shape, shape),
        in_specs=[VMEM] * len(arguments),
        out_specs=(VMEM, VMEM),
        scratch_shapes=[pltpu.VMEM((2,) + wide.shape[:2] + (groups, LANES), f32)],
        input_output_aliases={3: 0} if new is None else {3: 0, 4: 1},
        compiler_params=GRANT,
        name="begin",
    )(*arguments)


def adjoint_kernel(groups, parts, nodes_ref, observed_ref, coef, surface, forward, *refs):
    readings_refs, refs = refs[:parts], refs[parts + 2 :]
    (wide, new), blocks, (plane, gradient, staged, shifted) = refs[:2], refs[2:-4], refs[-4:]
    sources, layers, tall, _ = wide.shape
    columns = groups * LANES
    extent = tall // groups
    rows = extent - 2 * HALO
    count = nodes_ref.shape[1]
    per_source = count // sources
    receivers = per_source // 2
    first_row = lax.axis_index("space") * rows

    lane = lax.broadcasted_iota(jnp.int32, (1, count), 1)
    positive = (lane // receivers) % 2 == 0
    readings = sum(part[...] for part in readings_refs)
    partner = jnp.where(
        positive, pltpu.roll(readings, count - receivers, 1), pltpu.roll(readings, receivers, 1)
    )
    amounts = readings - partner - observed_ref[...]
    node = nodes_ref[...]
    node_row = node // columns
    node_column = node - node_row * columns
    span = extent - 2
    size = sources * span
    r = lax.broadcasted_iota(jnp.int32, (size, count), 0)
    k = lax.broadcasted_iota(jnp.int32, (size, count), 1)
    hit = (r // span == k // per_source) & (node_row - first_row + HALO - 1 == r % span)
    spread = three_parts(jnp.where(hit, amounts, 0.0))
    for j in range(groups):
        part = lax.dot_general(
            spread, column_hits(node_column, j), (((1,), (1,)), ((), ())), preferred_element_type=jnp.float32
        )
        part = part[:size] + part[size : 2 * size] + part[2 * size :]
        where = pl.ds(groups + j, span, stride=groups)
        weight = surface[where, :]
        for s in range(sources):
            amount = part[s * span : (s + 1) * span] * weight
            plane[s, where, :] = amount
            new[s, 0, where, :] += amount

    old, newer = new, wide
    for step in range(1, SWEEPS):
        sweep(step, old, newer, coef, plane, shifted, groups, [(1 + step, extent - 1 - step)])
        old, newer = newer, old
    adjoint = old

    first_lane, _, first_column, last_column = lane_masks(groups)
    both = (forward, adjoint)

    def turn(e):
        here = rows_of(e, 1, groups)
        after = pl.ds(e * groups + 1, groups)
        for i, field in enumerate(both):
            for l in range(layers):
                for s in range(sources):
                    v = jnp.where(first_lane, field[s, l, after, :], field[s, l, here, :])
                    shifted[i, s, l] = pltpu.roll(v, LANES - 1, 1)

    def row(e, above_faces):
        here = rows_of(e, 1, groups)
        below = rows_of(e + 1, 1, groups)
        sums = []
        for l in range(layers):
            for s in range(sources):
                u, a = forward[s, l, here, :], adjoint[s, l, here, :]
                terms = [
                    u * a,
                    (u - forward[s, l, below, :]) * (a - adjoint[s, l, below, :]),
                    (u - shifted[0, s, l]) * (a - shifted[1, s, l]),
                ]
                if l + 1 < layers:
                    terms.append((u - forward[s, l + 1, here, :]) * (a - adjoint[s, l + 1, here, :]))
                total = terms if s == 0 else [x + y for x, y in zip(total, terms)]
            sums.append(total)
        for l in range(layers):
            product, down, right = sums[l][:3]
            right = jnp.where(last_column, product, right)
            left = jnp.where(first_column, product, from_left(right, first_lane))
            upper = sums[l][3] if l + 1 < layers else product
            lower = sums[l - 1][3] if l > 0 else product
            total = product + above_faces[l] + down + right + left + lower + upper
            gradient[l, rows_of(e - HALO, 1, groups), :] = (-0.5 * FINAL * FINAL) * total
        return tuple(sums[l][1] for l in range(layers))

    above_faces = []
    for l in range(layers):
        for s in range(sources):
            above, here = rows_of(HALO - 1, 1, groups), rows_of(HALO, 1, groups)
            term = (forward[s, l, above, :] - forward[s, l, here, :]) * (
                adjoint[s, l, above, :] - adjoint[s, l, here, :]
            )
            total = term if s == 0 else total + term
        above_faces.append(total)

    def body(e, above_faces):
        above_faces = row(e, above_faces)
        turn(e + 1)
        return above_faces

    turn(HALO)
    above_faces = lax.fori_loop(HALO, HALO + rows - 1, body, tuple(above_faces))
    row(HALO + rows - 1, above_faces)

    count_blocks = len(blocks)
    me = lax.axis_index("src") if count_blocks > 1 else 0
    per = groups // count_blocks
    for q in range(count_blocks):
        for l in range(layers):
            for t in range(per):
                staged[q, l, :, t * LANES : (t + 1) * LANES] = gradient[
                    l, pl.ds(q * per + t, rows, stride=groups), :
                ]
    for i, block in enumerate(blocks):
        block[...] = staged[me ^ i]


def finish_adjoint(groups, nodes, readings, observed, wide, new, coef, surface, forward, blocks):
    sources, layers, tall, _ = wide.shape
    rows = tall // groups - 2 * HALO
    columns = groups * LANES
    f32 = jnp.float32
    block = jax.ShapeDtypeStruct((layers, rows, columns // blocks), f32)
    shape = jax.ShapeDtypeStruct(wide.shape, f32)
    parts = len(readings)
    return pl.pallas_call(
        functools.partial(adjoint_kernel, groups, parts),
        out_shape=(shape, shape) + (block,) * blocks,
        in_specs=[VMEM] * (7 + parts),
        out_specs=(VMEM,) * (2 + blocks),
        scratch_shapes=[
            pltpu.VMEM((sources, tall, LANES), f32),
            pltpu.VMEM((layers, rows * groups, LANES), f32),
            pltpu.VMEM((blocks, layers, rows, columns // blocks), f32),
            pltpu.VMEM((2, sources, layers, groups, LANES), f32),
        ],
        input_output_aliases={5 + parts: 0, 6 + parts: 1},
        compiler_params=GRANT,
        name="adjoint",
    )(nodes, observed, coef, surface, forward, *readings, wide, new)[2:]


def is_power_of_two(n):
    return n & (n - 1) == 0


def exchange(value, axis, mask):
    count = lax.axis_size(axis)
    return lax.ppermute(value, axis, [(i, i ^ mask) for i in range(count)])


def shift_down(value, axis):
    count = lax.axis_size(axis)
    return lax.ppermute(value, axis, [(i, i + 1) for i in range(count - 1)])


def shift_up(value, axis):
    count = lax.axis_size(axis)
    return lax.ppermute(value, axis, [(i + 1, i) for i in range(count - 1)])


def shares(first, last, parts):
    cuts = [first + (last - first) * i // parts for i in range(parts + 1)]
    return [range(a, b) for a, b in zip(cuts, cuts[1:])]


def per_device(potential_start, adjoint_start, conductivity, electrodes, receivers, observed):
    _, _, rows, columns = potential_start.shape
    groups = columns // LANES
    split, strips = lax.axis_size("src"), lax.axis_size("space")
    direct = is_power_of_two(split) and split <= 4 and (columns // split) % LANES == 0

    if direct:
        pieces = [conductivity] + [None] * (split - 1)
        for k in reversed(range(1, split)):
            pieces[k] = exchange(conductivity, "src", k)
    else:
        pieces = [lax.all_gather(conductivity, "src", axis=2, tiled=True)]
    x_wide, a_wide, first, last = spread_rows(potential_start, adjoint_start)
    top = shift_down(last, "space")
    bottom = shift_up(first, "space")
    nodes, measured = lay_out_nodes(receivers.transpose(0, 2, 1), observed)
    sigma, sigma_first, sigma_last = assemble_sigma(pieces, groups)
    sigma_top = shift_down(sigma_last, "space")
    sigma_bottom = shift_up(sigma_first, "space")
    ends = electrodes.T
    inner = inner_solve(groups, ends, sigma, x_wide)
    _, forward, coef, surface, _, _, readings = outer_solve(
        groups, ends, sigma_top, sigma_bottom, top, bottom, nodes, sigma, inner
    )

    begun = None
    if is_power_of_two(strips):
        rounds = strips.bit_length() - 1
        parts = shares(1, rows + 2 * HALO - 1, max(rounds, 1))
        for i in range(rounds):
            other = exchange(readings, "space", 1 << i)
            a_wide, begun = begin_adjoint(groups, parts[i], top, bottom, coef, a_wide, begun)
            if i + 1 < rounds:
                readings = readings + other
        terms = [readings, other] if rounds else [readings]
        parts = parts[rounds:]
    else:
        terms = [lax.psum(readings, "space")]
        parts = shares(1, rows + 2 * HALO - 1, 1)
    for part in parts:
        a_wide, begun = begin_adjoint(groups, part, top, bottom, coef, a_wide, begun)
    blocks = finish_adjoint(
        groups, nodes, terms, measured, a_wide, begun, coef, surface, forward, split if direct else 1
    )
    if direct:
        total = blocks[0]
        for k in reversed(range(1, split)):
            total = total + exchange(blocks[k], "src", k)
        return total
    summed = lax.psum(blocks[0], "src")
    share = columns // split
    return lax.dynamic_slice_in_dim(summed, lax.axis_index("src") * share, share, 2)


def solution(mesh):
    return jax.shard_map(
        per_device,
        mesh=mesh,
        in_specs=(
            P("src", None, "space", None),
            P("src", None, "space", None),
            P(None, "space", "src"),
            P("src", None),
            P("src", None, None),
            P("src", None),
        ),
        out_specs=P(None, "space", "src"),
        check_vma=False,
    )
```

time: 98.6 us -> 68.5 us (0.69)
  Pallas kernels: 42.8 us -> 26.5 us
  waiting for transfers between devices: 16 us -> 11.4 us
  starting transfers between devices: 31.5 us -> 27 us
  other arithmetic: 3.31 us -> 0.66 us
  local copies, waits for them, and re-layouts: 4.33 us -> 2.46 us
    pallas_call x6 -> x9, Pallas kernels: 42.8 us -> 26.5 us  [the longest x1 9.73 us: finish_adjoint(): pl.pallas_call(functools.partial(adjoint_kernel, groups, parts), out_shap...]
    ppermute x3 -> x2, waiting for transfers between devices: 4.84 us -> 0.01 us  [shift_up(): return lax.ppermute(value, axis, [(i + 1, i) for i in range(count - 1)])]
    ppermute x3 -> x2, starting transfers between devices: 9.03 us -> 5 us  [shift_down(): return lax.ppermute(value, axis, [(i, i + 1) for i in range(count - 1)])]
    ppermute x3 -> x2, starting transfers between devices: 3.87 us -> 2.58 us  [shift_up(): return lax.ppermute(value, axis, [(i + 1, i) for i in range(count - 1)])]
    reshape x2 -> x0, local copies, waits for them, and re-layouts: 1.24 us -> none  [the longest x1 0.62 us: per_device(): jnp.broadcast_to(observed[:, None, :], (sources, 2, observed.shape[1]))]
    add x3 -> x2, other arithmetic: 1.21 us -> 0.01 us  [per_device(): readings = readings + other]
    unnamed x27 -> x12, local copies, waits for them, and re-layouts: 3.09 us -> 2.46 us
  transfers between devices with their start and end apart: 15 -> 13, of which waited for: 6 -> 7; matrix products, arithmetic and copies ran while one was open for 3% -> 0% of each run, Pallas kernels for 29% -> 15%
where the time goes in v2:
time: 68.5 us; the launch traced here: 68.2 us
  starting transfers between devices  27 us (39%)
  Pallas kernels  26.5 us (39%)
  waiting for transfers between devices  11.4 us (17%)
  local copies, waits for them, and re-layouts  2.46 us (4%)
    ppermute x9, starting transfers between devices, exchange(): return lax.ppermute(value, axis, [(i, i ^ mask) for i in range(count)])  19.4 us
    ppermute x9, waiting for transfers between devices, exchange(): return lax.ppermute(value, axis, [(i, i ^ mask) for i in range(count)])  11.4 us
    pallas_call x1, Pallas kernels, finish_adjoint(): pl.pallas_call(functools.partial(adjoint_kernel, groups, parts), out_shap...  9.73 us
    pallas_call x1, Pallas kernels, inner_solve(): pl.pallas_call(functools.partial(inner_kernel, groups), out_shape=(jax.Sh...  6.87 us
    pallas_call x1, Pallas kernels, outer_solve(): pl.pallas_call(functools.partial(outer_kernel, groups), out_shape=kept +...  6.45 us
    ppermute x2, starting transfers between devices, shift_down(): return lax.ppermute(value, axis, [(i, i + 1) for i in range(count - 1)])  5 us
    pallas_call x3, Pallas kernels, begin_adjoint(): pl.pallas_call(functools.partial(begin_kernel, groups, part[0], part[-1]...  2.87 us
    ppermute x2, starting transfers between devices, shift_up(): return lax.ppermute(value, axis, [(i + 1, i) for i in range(count - 1)])  2.58 us
  transfers between devices with their start and end apart: 13, of which 7 were waited for; matrix products, arithmetic and copies ran while one was open for 0% of the time, Pallas kernels for 15%

profile of v2, /device:TPU:0, one launch (start us, length us, event | category | flops | bytes accessed | tf_op | source)
XLA Modules:
  0.0 68.2 jit_solution(11969670707630790017)
XLA Ops:
  0.0 0.0 copy-start
  0.0 1.2 %copy-done = f32[4,4,16,1024]{3,2,1,0:T(8,128)S(1)} copy-done((f32[4,4,16,1024]{3,2,1,0:T(8,128)S(1)}, f32[4,4,16,1024]{3,2,1,0:T(8,128)}, u32[]{:S(2)}) %copy-start) | copy-done | bytes 1048600
  1.2 0.0 copy-start.1
  1.2 1.2 %copy-done.1 = f32[4,4,16,1024]{3,2,1,0:T(8,128)S(1)} copy-done((f32[4,4,16,1024]{3,2,1,0:T(8,128)S(1)}, f32[4,4,16,1024]{3,2,1,0:T(8,128)}, u32[]{:S(2)}) %copy-start.1) | copy-done | bytes 1048600
  2.5 0.0 copy-start.2
  2.5 0.0 copy-start.3
  2.5 0.0 copy-start.5
  2.5 0.0 copy-start.4
  2.5 0.4 spread.1
  2.9 2.4 %collective-permute-start.5 = (f32[2,4,4,40,128]{4,3,2,1,0:T(8,128)S(1)}, f32[2,4,4,40,128]{4,3,2,1,0:T(8,128)S(1)}, u32[]{:S(2)}, u32[]{:S(2)}) collective-permute-start(f32[2,4,4,40,128]{4,3,2,1,0:T(8,128)S(1)} %get-tuple-element.37), channel_id=1, source_target_pairs={{0,4},{4,8},{8,12},{12,16},{16,20},{20,24},{24,28},{1,5},{5,9},{9,... | collective-permute-start | bytes 1966088 | tf_op jit(solution)/shard_map/ppermute | solution.py:557
  5.3 1.3 %collective-permute-start.6 = (f32[2,4,4,40,128]{4,3,2,1,0:T(8,128)S(1)}, f32[2,4,4,40,128]{4,3,2,1,0:T(8,128)S(1)}, u32[]{:S(2)}, u32[]{:S(2)}) collective-permute-start(f32[2,4,4,40,128]{4,3,2,1,0:T(8,128)S(1)} %get-tuple-element.38), channel_id=1, source_target_pairs={{4,0},{8,4},{12,8},{16,12},{20,16},{24,20},{28,24},{5,1},{9,5},{13... | collective-permute-start | bytes 1966088 | tf_op jit(solution)/shard_map/ppermute | solution.py:562
  6.6 0.0 copy-done.2
  6.6 3.5 %collective-permute-start.1 = (f32[4,16,256]{2,1,0:T(8,128)S(1)}, f32[4,16,256]{2,1,0:T(8,128)S(1)}, u32[]{:S(2)}, u32[]{:S(2)}) collective-permute-start(f32[4,16,256]{2,1,0:T(8,128)S(1)} %copy-done.2), channel_id=1, source_target_pairs={{0,2},{1,3},{2,0},{3,1},{4,6},{5,7},{6,4},{7,5},{8,10},{9,11},{10,... | collective-permute-start | bytes 196616 | tf_op jit(solution)/shard_map/ppermute | solution.py:552
  10.1 1.6 %collective-permute-start = (f32[4,16,256]{2,1,0:T(8,128)S(1)}, f32[4,16,256]{2,1,0:T(8,128)S(1)}, u32[]{:S(2)}, u32[]{:S(2)}) collective-permute-start(f32[4,16,256]{2,1,0:T(8,128)S(1)} %copy-done.2), channel_id=1, source_target_pairs={{0,1},{1,0},{2,3},{3,2},{4,5},{5,4},{6,7},{7,6},{8,9},{9,8},{10,11... | collective-permute-start | bytes 196616 | tf_op jit(solution)/shard_map/ppermute | solution.py:552
  11.7 0.0 collective-permute-start.2
  11.7 0.7 collective-permute-done.1.refs_2_
  12.3 3.0 %collective-permute-done.refs_1_ = f32[4,16,256]{2,1,0:T(8,128)S(1)} collective-permute-done((f32[4,16,256]{2,1,0:T(8,128)S(1)}, f32[4,16,256]{2,1,0:T(8,128)S(1)}, u32[]{:S(2)}, u32[]{:S(2)}) %collective-permute-start) | collective-permute-done | bytes 65568 | tf_op jit(solution)/shard_map/ppermute | solution.py:552
  15.3 2.4 %collective-permute-done.2.refs_3_ = f32[4,16,256]{2,1,0:T(8,128)S(1)} collective-permute-done((f32[4,16,256]{2,1,0:T(8,128)S(1)}, f32[4,16,256]{2,1,0:T(8,128)S(1)}, u32[]{:S(2)}, u32[]{:S(2)}) %collective-permute-start.2) | collective-permute-done | bytes 65568 | tf_op jit(solution)/shard_map/ppermute | solution.py:552
  17.7 0.1 sigma.1
  17.8 2.6 %collective-permute-start.3 = (f32[4,40,128]{2,1,0:T(8,128)S(1)}, f32[4,40,128]{2,1,0:T(8,128)S(1)}, u32[]{:S(2)}, u32[]{:S(2)}) collective-permute-start(f32[4,40,128]{2,1,0:T(8,128)S(1)} %get-tuple-element.35), channel_id=1, source_target_pairs={{0,4},{4,8},{8,12},{12,16},{16,20},{20,24},{24,28},{1,5},{5,9},{9,... | collective-permute-start | bytes 245768 | tf_op jit(solution)/shard_map/ppermute | solution.py:557
  20.4 1.3 %collective-permute-start.4 = (f32[4,40,128]{2,1,0:T(8,128)S(1)}, f32[4,40,128]{2,1,0:T(8,128)S(1)}, u32[]{:S(2)}, u32[]{:S(2)}) collective-permute-start(f32[4,40,128]{2,1,0:T(8,128)S(1)} %get-tuple-element.36), channel_id=1, source_target_pairs={{4,0},{8,4},{12,8},{16,12},{20,16},{24,20},{28,24},{5,1},{9,5},{13... | collective-permute-start | bytes 245768 | tf_op jit(solution)/shard_map/ppermute | solution.py:562
  21.7 0.0 copy-done.3
  21.7 0.0 copy-done.5
  21.7 0.1 nodes.1
  21.8 0.0 copy-done.4
  21.8 6.9 %inner.1 = (f32[4,4,208,128]{3,2,1,0:T(8,128)S(1)}, f32[6,4,208,128]{3,2,1,0:T(8,128)S(1)}, f32[208,128]{1,0:T(8,128)S(1)}, f32[4,4,208,128]{3,2,1,0:T(8,128)S(1)}, f32[4,208,128]{2,1,0:T(8,128)S(1)}) custom-call(s32[2,4]{1,0:T(2,128)S(1)} %bitcast.3, f32[4,208,128]{2,1,0:T(8,128)S(1)} %get-tuple-element.39.sigma.refs_0_, ...), custom_call_target="tpu_custom_call", output_to_operand_aliasing={{0}: (2, {})} | custom-call | tf_op jit(solution)/shard_map/inner/pallas_call | solution.py:306
  28.7 0.0 collective-permute-done.3.sigma_top
  28.7 0.0 collective-permute-done.4.sigma_bottom
  28.7 0.0 collective-permute-done.5.top_ref
  28.7 0.0 collective-permute-done.6.bottom_ref
  28.7 6.4 %outer.1 = (f32[4,208,128]{2,1,0:T(8,128)S(1)}, f32[4,4,208,128]{3,2,1,0:T(8,128)S(1)}, f32[6,4,208,128]{3,2,1,0:T(8,128)S(1)}, f32[208,128]{1,0:T(8,128)S(1)}, ...) custom-call(s32[2,4]{1,0:T(2,128)S(1)} %bitcast.4, ...), custom_call_target="tpu_custom_call", output_to_operand_aliasing={{0}: (6, {}), {1}: (7, {}), {2}: (8, {}), {3}: (9, {}), {4}... | custom-call | tf_op jit(solution)/shard_map/outer/pallas_call | solution.py:368
  35.2 4.1 %collective-permute-start.7 = (f32[1,256]{1,0:T(1,128)S(1)}, f32[1,256]{1,0:T(1,128)S(1)}, u32[]{:S(2)}, u32[]{:S(2)}) collective-permute-start(f32[1,256]{1,0:T(1,128)S(1)} %get-tuple-element.49), channel_id=1, source_target_pairs={{0,4},{4,0},{8,12},{12,8},{16,20},{20,16},{24,28},{28,24},{1,5},{5... | collective-permute-start | bytes 3080 | tf_op jit(solution)/shard_map/ppermute | solution.py:552
  39.3 0.8 %collective-permute-done.7 = f32[1,256]{1,0:T(1,128)S(1)} collective-permute-done((f32[1,256]{1,0:T(1,128)S(1)}, f32[1,256]{1,0:T(1,128)S(1)}, u32[]{:S(2)}, u32[]{:S(2)}) %collective-permute-start.7) | collective-permute-done | bytes 1056 | tf_op jit(solution)/shard_map/ppermute | solution.py:552
  40.1 2.4 %collective-permute-start.8 = (f32[1,256]{1,0:T(1,128)S(1)}, f32[1,256]{1,0:T(1,128)S(1)}, u32[]{:S(2)}, u32[]{:S(2)}) collective-permute-start(f32[1,256]{1,0:T(1,128)S(1)} %add.15), channel_id=1, source_target_pairs={{0,8},{4,12},{8,0},{12,4},{16,24},{20,28},{24,16},{28,20},{1,9},{5... | collective-permute-start | bytes 3080 | tf_op jit(solution)/shard_map/ppermute | solution.py:552
  42.5 1.6 %collective-permute-done.8 = f32[1,256]{1,0:T(1,128)S(1)} collective-permute-done((f32[1,256]{1,0:T(1,128)S(1)}, f32[1,256]{1,0:T(1,128)S(1)}, u32[]{:S(2)}, u32[]{:S(2)}) %collective-permute-start.8) | collective-permute-done | bytes 1056 | tf_op jit(solution)/shard_map/ppermute | solution.py:552
  44.1 3.4 %collective-permute-start.9 = (f32[1,256]{1,0:T(1,128)S(1)}, f32[1,256]{1,0:T(1,128)S(1)}, u32[]{:S(2)}, u32[]{:S(2)}) collective-permute-start(f32[1,256]{1,0:T(1,128)S(1)} %add.16.refs_0_), channel_id=1, source_target_pairs={{0,16},{4,20},{8,24},{12,28},{16,0},{20,4},{24,8},{28,12},{1,17},{... | collective-permute-start | bytes 3080 | tf_op jit(solution)/shard_map/ppermute | solution.py:552
  47.5 1.0 %begin.3 = (f32[4,4,208,128]{3,2,1,0:T(8,128)S(1)}, f32[4,4,208,128]{3,2,1,0:T(8,128)S(1)}) custom-call(f32[2,4,4,40,128]{4,3,2,1,0:T(8,128)S(1)} %collective-permute-done.5.top_ref, f32[2,4,4,40,128]{4,3,2,1,0:T(8,128)S(1)} %collective-permute-done.6.bottom_ref, f32[6,4,208,128]{3,2,1,0:T(8,128)S(1)} %get-tuple-element.46.coef, ...), custom_call_target="tpu_custom_call", output_to_operand_aliasing={{0}: (3, {})} | custom-call | tf_op jit(solution)/shard_map/begin/pallas_call | solution.py:393
  48.5 1.0 %begin.4 = (f32[4,4,208,128]{3,2,1,0:T(8,128)S(1)}, f32[4,4,208,128]{3,2,1,0:T(8,128)S(1)}) custom-call(f32[2,4,4,40,128]{4,3,2,1,0:T(8,128)S(1)} %collective-permute-done.5.top_ref, f32[2,4,4,40,128]{4,3,2,1,0:T(8,128)S(1)} %collective-permute-done.6.bottom_ref, ...), custom_call_target="tpu_custom_call", output_to_operand_aliasing={{0}: (3, {}), {1}: (4, {})} | custom-call | tf_op jit(solution)/shard_map/begin/pallas_call | solution.py:393
  49.4 1.0 %begin.5 = (f32[4,4,208,128]{3,2,1,0:T(8,128)S(1)}, f32[4,4,208,128]{3,2,1,0:T(8,128)S(1)}) custom-call(f32[2,4,4,40,128]{4,3,2,1,0:T(8,128)S(1)} %collective-permute-done.5.top_ref, f32[2,4,4,40,128]{4,3,2,1,0:T(8,128)S(1)} %collective-permute-done.6.bottom_ref, ...), custom_call_target="tpu_custom_call", output_to_operand_aliasing={{0}: (3, {}), {1}: (4, {})} | custom-call | tf_op jit(solution)/shard_map/begin/pallas_call | solution.py:393
  50.4 0.0 collective-permute-done.9.refs_1_
  50.4 9.7 %adjoint.1 = (f32[4,4,208,128]{3,2,1,0:T(8,128)S(1)}, f32[4,4,208,128]{3,2,1,0:T(8,128)S(1)}, f32[4,16,256]{2,1,0:T(8,128)S(1)}, f32[4,16,256]{2,1,0:T(8,128)S(1...) custom-call(s32[1,256]{1,0:T(1,128)S(1)} %get-tuple-element.33.nodes_ref, ...), custom_call_target="tpu_custom_call", output_to_operand_aliasing={{0}: (7, {}), {1}: (8, {})} | custom-call | tf_op jit(solution)/shard_map/adjoint/pallas_call | solution.py:529
  60.1 0.9 %collective-permute-start.10 = (f32[4,16,256]{2,1,0:T(8,128)S(1)}, f32[4,16,256]{2,1,0:T(8,128)S(1)}, u32[]{:S(2)}, u32[]{:S(2)}) collective-permute-start(f32[4,16,256]{2,1,0:T(8,128)S(1)} %get-tuple-element.58), channel_id=1, source_target_pairs={{0,3},{1,2},{2,1},{3,0},{4,7},{5,6},{6,5},{7,4},{8,11},{9,10},{10,... | collective-permute-start | bytes 196616 | tf_op jit(solution)/shard_map/ppermute | solution.py:552
  61.0 0.0 collective-permute-start.11
  61.0 3.6 %collective-permute-start.12 = (f32[4,16,256]{2,1,0:T(8,128)S(1)}, f32[4,16,256]{2,1,0:T(8,128)S(1)}, u32[]{:S(2)}, u32[]{:S(2)}) collective-permute-start(f32[4,16,256]{2,1,0:T(8,128)S(1)} %get-tuple-element.60), channel_id=1, source_target_pairs={{0,1},{1,0},{2,3},{3,2},{4,5},{5,4},{6,7},{7,6},{8,9},{9,8},{10,11... | collective-permute-start | bytes 196616 | tf_op jit(solution)/shard_map/ppermute | solution.py:552
  64.6 1.8 %collective-permute-done.10 = f32[4,16,256]{2,1,0:T(8,128)S(1)} collective-permute-done((f32[4,16,256]{2,1,0:T(8,128)S(1)}, f32[4,16,256]{2,1,0:T(8,128)S(1)}, u32[]{:S(2)}, u32[]{:S(2)}) %collective-permute-start.10) | collective-permute-done | bytes 65568 | tf_op jit(solution)/shard_map/ppermute | solution.py:552
  66.4 1.2 %collective-permute-done.11 = f32[4,16,256]{2,1,0:T(8,128)S(1)} collective-permute-done((f32[4,16,256]{2,1,0:T(8,128)S(1)}, f32[4,16,256]{2,1,0:T(8,128)S(1)}, u32[]{:S(2)}, u32[]{:S(2)}) %collective-permute-start.11) | collective-permute-done | bytes 65568 | tf_op jit(solution)/shard_map/ppermute | solution.py:552
  67.6 0.0 collective-permute-done.12
  67.6 0.6 add_add_fusion
  (2 shorter events, 0.0 us)
Async XLA Ops:
  0.0 1.2 %copy-start = (f32[4,4,16,1024]{3,2,1,0:T(8,128)S(1)}, f32[4,4,16,1024]{3,2,1,0:T(8,128)}, u32[]{:S(2)}) copy-start(f32[4,4,16,1024]{3,2,1,0:T(8,128)} %x_ref.1) | copy-start | bytes 3145732
  1.2 1.2 %copy-start.1 = (f32[4,4,16,1024]{3,2,1,0:T(8,128)S(1)}, f32[4,4,16,1024]{3,2,1,0:T(8,128)}, u32[]{:S(2)}) copy-start(f32[4,4,16,1024]{3,2,1,0:T(8,128)} %a_ref.1) | copy-start | bytes 3145732
  2.5 4.2 %copy-start.2 = (f32[4,16,256]{2,1,0:T(8,128)S(1)}, f32[4,16,256]{2,1,0:T(8,128)}, u32[]{:S(2)}) copy-start(f32[4,16,256]{2,1,0:T(8,128)} %refs_0_.1) | copy-start | bytes 196612
  2.5 19.2 %copy-start.3 = (s32[4,32,2]{1,2,0:T(2,128)S(1)}, s32[4,32,2]{1,2,0:T(2,128)}, u32[]{:S(2)}) copy-start(s32[4,32,2]{1,2,0:T(2,128)} %param.10) | copy-start | bytes 3076
  2.5 19.3 %copy-start.5 = (f32[4,32]{1,0:T(4,128)S(1)}, f32[4,32]{1,0:T(4,128)}, u32[]{:S(2)}) copy-start(f32[4,32]{1,0:T(4,128)} %observed_ref.1) | copy-start | bytes 1540
  2.5 19.3 %copy-start.4 = (s32[4,2]{0,1:T(2,128)S(1)}, s32[4,2]{0,1:T(2,128)}, u32[]{:S(2)}) copy-start(s32[4,2]{0,1:T(2,128)} %param.9) | copy-start | bytes 100
  2.9 25.8 %collective-permute-start.5 = (f32[2,4,4,40,128]{4,3,2,1,0:T(8,128)S(1)}, f32[2,4,4,40,128]{4,3,2,1,0:T(8,128)S(1)}, u32[]{:S(2)}, u32[]{:S(2)}) collective-permute-start(f32[2,4,4,40,128]{4,3,2,1,0:T(8,128)S(1)} %get-tuple-element.37), channel_id=1, source_target_pairs={{0,4},{4,8},{8,12},{12,16},{16,20},{20,24},{24,28},{1,5},{5,9},{9,... | collective-permute-start | bytes 1966088 | tf_op jit(solution)/shard_map/ppermute | solution.py:557
  5.3 23.4 %collective-permute-start.6 = (f32[2,4,4,40,128]{4,3,2,1,0:T(8,128)S(1)}, f32[2,4,4,40,128]{4,3,2,1,0:T(8,128)S(1)}, u32[]{:S(2)}, u32[]{:S(2)}) collective-permute-start(f32[2,4,4,40,128]{4,3,2,1,0:T(8,128)S(1)} %get-tuple-element.38), channel_id=1, source_target_pairs={{4,0},{8,4},{12,8},{16,12},{20,16},{24,20},{28,24},{5,1},{9,5},{13... | collective-permute-start | bytes 1966088 | tf_op jit(solution)/shard_map/ppermute | solution.py:562
  6.6 5.7 %collective-permute-start.1 = (f32[4,16,256]{2,1,0:T(8,128)S(1)}, f32[4,16,256]{2,1,0:T(8,128)S(1)}, u32[]{:S(2)}, u32[]{:S(2)}) collective-permute-start(f32[4,16,256]{2,1,0:T(8,128)S(1)} %copy-done.2), channel_id=1, source_target_pairs={{0,2},{1,3},{2,0},{3,1},{4,6},{5,7},{6,4},{7,5},{8,10},{9,11},{10,... | collective-permute-start | bytes 196616 | tf_op jit(solution)/shard_map/ppermute | solution.py:552
  10.1 5.2 %collective-permute-start = (f32[4,16,256]{2,1,0:T(8,128)S(1)}, f32[4,16,256]{2,1,0:T(8,128)S(1)}, u32[]{:S(2)}, u32[]{:S(2)}) collective-permute-start(f32[4,16,256]{2,1,0:T(8,128)S(1)} %copy-done.2), channel_id=1, source_target_pairs={{0,1},{1,0},{2,3},{3,2},{4,5},{5,4},{6,7},{7,6},{8,9},{9,8},{10,11... | collective-permute-start | bytes 196616 | tf_op jit(solution)/shard_map/ppermute | solution.py:552
  11.7 6.1 %collective-permute-start.2 = (f32[4,16,256]{2,1,0:T(8,128)S(1)}, f32[4,16,256]{2,1,0:T(8,128)S(1)}, u32[]{:S(2)}, u32[]{:S(2)}) collective-permute-start(f32[4,16,256]{2,1,0:T(8,128)S(1)} %copy-done.2), channel_id=1, source_target_pairs={{0,3},{1,2},{2,1},{3,0},{4,7},{5,6},{6,5},{7,4},{8,11},{9,10},{10,... | collective-permute-start | bytes 196616 | tf_op jit(solution)/shard_map/ppermute | solution.py:552
  17.8 10.9 %collective-permute-start.3 = (f32[4,40,128]{2,1,0:T(8,128)S(1)}, f32[4,40,128]{2,1,0:T(8,128)S(1)}, u32[]{:S(2)}, u32[]{:S(2)}) collective-permute-start(f32[4,40,128]{2,1,0:T(8,128)S(1)} %get-tuple-element.35), channel_id=1, source_target_pairs={{0,4},{4,8},{8,12},{12,16},{16,20},{20,24},{24,28},{1,5},{5,9},{9,... | collective-permute-start | bytes 245768 | tf_op jit(solution)/shard_map/ppermute | solution.py:557
  20.4 8.3 %collective-permute-start.4 = (f32[4,40,128]{2,1,0:T(8,128)S(1)}, f32[4,40,128]{2,1,0:T(8,128)S(1)}, u32[]{:S(2)}, u32[]{:S(2)}) collective-permute-start(f32[4,40,128]{2,1,0:T(8,128)S(1)} %get-tuple-element.36), channel_id=1, source_target_pairs={{4,0},{8,4},{12,8},{16,12},{20,16},{24,20},{28,24},{5,1},{9,5},{13... | collective-permute-start | bytes 245768 | tf_op jit(solution)/shard_map/ppermute | solution.py:562
  35.2 5.0 %collective-permute-start.7 = (f32[1,256]{1,0:T(1,128)S(1)}, f32[1,256]{1,0:T(1,128)S(1)}, u32[]{:S(2)}, u32[]{:S(2)}) collective-permute-start(f32[1,256]{1,0:T(1,128)S(1)} %get-tuple-element.49), channel_id=1, source_target_pairs={{0,4},{4,0},{8,12},{12,8},{16,20},{20,16},{24,28},{28,24},{1,5},{5... | collective-permute-start | bytes 3080 | tf_op jit(solution)/shard_map/ppermute | solution.py:552
  40.1 3.9 %collective-permute-start.8 = (f32[1,256]{1,0:T(1,128)S(1)}, f32[1,256]{1,0:T(1,128)S(1)}, u32[]{:S(2)}, u32[]{:S(2)}) collective-permute-start(f32[1,256]{1,0:T(1,128)S(1)} %add.15), channel_id=1, source_target_pairs={{0,8},{4,12},{8,0},{12,4},{16,24},{20,28},{24,16},{28,20},{1,9},{5... | collective-permute-start | bytes 3080 | tf_op jit(solution)/shard_map/ppermute | solution.py:552
  44.1 6.3 %collective-permute-start.9 = (f32[1,256]{1,0:T(1,128)S(1)}, f32[1,256]{1,0:T(1,128)S(1)}, u32[]{:S(2)}, u32[]{:S(2)}) collective-permute-start(f32[1,256]{1,0:T(1,128)S(1)} %add.16.refs_0_), channel_id=1, source_target_pairs={{0,16},{4,20},{8,24},{12,28},{16,0},{20,4},{24,8},{28,12},{1,17},{... | collective-permute-start | bytes 3080 | tf_op jit(solution)/shard_map/ppermute | solution.py:552
  60.1 6.3 %collective-permute-start.10 = (f32[4,16,256]{2,1,0:T(8,128)S(1)}, f32[4,16,256]{2,1,0:T(8,128)S(1)}, u32[]{:S(2)}, u32[]{:S(2)}) collective-permute-start(f32[4,16,256]{2,1,0:T(8,128)S(1)} %get-tuple-element.58), channel_id=1, source_target_pairs={{0,3},{1,2},{2,1},{3,0},{4,7},{5,6},{6,5},{7,4},{8,11},{9,10},{10,... | collective-permute-start | bytes 196616 | tf_op jit(solution)/shard_map/ppermute | solution.py:552
  61.0 6.6 %collective-permute-start.11 = (f32[4,16,256]{2,1,0:T(8,128)S(1)}, f32[4,16,256]{2,1,0:T(8,128)S(1)}, u32[]{:S(2)}, u32[]{:S(2)}) collective-permute-start(f32[4,16,256]{2,1,0:T(8,128)S(1)} %get-tuple-element.59), channel_id=1, source_target_pairs={{0,2},{1,3},{2,0},{3,1},{4,6},{5,7},{6,4},{7,5},{8,10},{9,11},{10,... | collective-permute-start | bytes 196616 | tf_op jit(solution)/shard_map/ppermute | solution.py:552
  61.0 6.6 %collective-permute-start.12 = (f32[4,16,256]{2,1,0:T(8,128)S(1)}, f32[4,16,256]{2,1,0:T(8,128)S(1)}, u32[]{:S(2)}, u32[]{:S(2)}) collective-permute-start(f32[4,16,256]{2,1,0:T(8,128)S(1)} %get-tuple-element.60), channel_id=1, source_target_pairs={{0,1},{1,0},{2,3},{3,2},{4,5},{5,4},{6,7},{7,6},{8,9},{9,8},{10,11... | collective-permute-start | bytes 196616 | tf_op jit(solution)/shard_map/ppermute | solution.py:552

commit v3 on v2

--- a/solution.py
+++ b/solution.py
@@ -78,32 +78,41 @@
     return jnp.where(c == columns, 1.0, 0.0).astype(jnp.bfloat16)
 
 
-def spread_kernel(groups, x_ref, a_ref, x_wide, a_wide, first_ref, last_ref):
+def facing(axis, rows, groups, sent):
+    even = lax.rem(lax.axis_index(axis), 2) == 0
+    low, high = (HALO, rows) if sent else (0, HALO + rows)
+    return [
+        pl.ds(pl.multiple_of(jnp.where(condition, high, low) * groups, groups), HALO * groups)
+        for condition in (even, jnp.logical_not(even))
+    ]
+
+
+def spread_kernel(groups, x_ref, wide, inner_ref, outer_ref):
     sources, layers, rows, _ = x_ref.shape
-    for i, (field, wide) in enumerate(((x_ref, x_wide), (a_ref, a_wide))):
-        for s in range(sources):
-            for l in range(layers):
-                for j in range(groups):
-                    wide[s, l, pl.ds(HALO * groups + j, rows, stride=groups), :] = field[
-                        s, l, :, j * LANES : (j + 1) * LANES
-                    ]
-        first_ref[i] = wide[:, :, HALO * groups : 2 * HALO * groups, :]
-        last_ref[i] = wide[:, :, rows * groups : (HALO + rows) * groups, :]
-
-
-def spread_rows(x, a):
+    for s in range(sources):
+        for l in range(layers):
+            for j in range(groups):
+                wide[s, l, pl.ds(HALO * groups + j, rows, stride=groups), :] = x_ref[
+                    s, l, :, j * LANES : (j + 1) * LANES
+                ]
+    to_inner, to_outer = facing("space", rows, groups, True)
+    inner_ref[...] = wide[:, :, to_inner, :]
+    outer_ref[...] = wide[:, :, to_outer, :]
+
+
+def spread_rows(x):
     sources, layers, rows, columns = x.shape
     groups = columns // LANES
     wide = jax.ShapeDtypeStruct((sources, layers, (rows + 2 * HALO) * groups, LANES), jnp.float32)
-    halo = jax.ShapeDtypeStruct((2, sources, layers, HALO * groups, LANES), jnp.float32)
+    halo = jax.ShapeDtypeStruct((sources, layers, HALO * groups, LANES), jnp.float32)
     return pl.pallas_call(
         functools.partial(spread_kernel, groups),
-        out_shape=(wide, wide, halo, halo),
-        in_specs=[VMEM, VMEM],
-        out_specs=(VMEM,) * 4,
+        out_shape=(wide, halo, halo),
+        in_specs=[VMEM],
+        out_specs=(VMEM,) * 3,
         compiler_params=GRANT,
         name="spread",
-    )(x, a)
+    )(x)
 
 
 def nodes_kernel(receivers_ref, observed_ref, nodes_ref, measured_ref):
@@ -130,7 +139,7 @@
 
 
 def sigma_kernel(groups, *refs):
-    pieces, (wide_ref, first_ref, last_ref, stage) = refs[:-4], refs[-4:]
+    pieces, (wide_ref, inner_ref, outer_ref, stage) = refs[:-4], refs[-4:]
     count = len(pieces)
     layers, rows, share = pieces[0].shape
     me = lax.axis_index("src") if count > 1 else 0
@@ -143,8 +152,9 @@
                 wide_ref[l, pl.ds(HALO * groups + q * per + t, rows, stride=groups), :] = stage[
                     q, l, :, t * LANES : (t + 1) * LANES
                 ]
-    first_ref[...] = wide_ref[:, HALO * groups : 2 * HALO * groups, :]
-    last_ref[...] = wide_ref[:, rows * groups : (HALO + rows) * groups, :]
+    to_inner, to_outer = facing("space", rows, groups, True)
+    inner_ref[...] = wide_ref[:, to_inner, :]
+    outer_ref[...] = wide_ref[:, to_outer, :]
 
 
 def assemble_sigma(pieces, groups):
@@ -322,18 +332,18 @@
 
 
 def outer_kernel(
-    groups, electrodes_ref, sigma_top, sigma_bottom, top_ref, bottom_ref, nodes_ref, *refs
+    groups, electrodes_ref, sigma_inner, sigma_outer, inner_ref, outer_ref, nodes_ref, *refs
 ):
     sigma, wide, coef, surface, other, plane, readings_ref, shifted = refs[6:]
     sources, _, tall, _ = wide.shape
     columns = groups * LANES
     rows = tall // groups - 2 * HALO
     first_row = lax.axis_index("space") * rows
-    bottom = (HALO + rows) * groups
-    sigma[:, : HALO * groups, :] = sigma_top[...]
-    sigma[:, bottom:, :] = sigma_bottom[...]
-    wide[:, :, : HALO * groups, :] = top_ref[0]
-    wide[:, :, bottom:, :] = bottom_ref[0]
+    from_inner, from_outer = facing("space", rows, groups, False)
+    sigma[:, from_inner, :] = sigma_inner[...]
+    sigma[:, from_outer, :] = sigma_outer[...]
+    wide[:, :, from_inner, :] = inner_ref[...]
+    wide[:, :, from_outer, :] = outer_ref[...]
     segments = outer_rows(0, rows)
     coefficient_rows(sigma, coef, surface, groups, segments)
     add_electrodes(electrodes_ref, plane, surface, rows, groups, segments)
@@ -360,7 +370,7 @@
     readings_ref[...] = FINAL * jnp.sum(jnp.where(hit, picked, 0.0), axis=0, keepdims=True)
 
 
-def outer_solve(groups, electrodes, sigma_top, sigma_bottom, top, bottom, nodes, sigma, inner):
+def outer_solve(groups, electrodes, sigma_inner, sigma_outer, from_inner, from_outer, nodes, sigma, inner):
     carried = (sigma,) + tuple(inner)
     sources, layers = inner[0].shape[:2]
     f32 = jnp.float32
@@ -374,29 +384,32 @@
         input_output_aliases={6 + i: i for i in range(6)},
         compiler_params=GRANT,
         name="outer",
-    )(electrodes, sigma_top, sigma_bottom, top, bottom, nodes, *carried)
-
-
-def begin_kernel(groups, start, end, top_ref, bottom_ref, coef, *refs):
+    )(electrodes, sigma_inner, sigma_outer, from_inner, from_outer, nodes, *carried)
+
+
+def begin_kernel(groups, segments, coef, *refs):
     wide, new, shifted = refs[-3:]
-    if start == 1:
+    if segments[0][0] == 1:
         rows = wide.shape[2] // groups - 2 * HALO
-        wide[:, :, : HALO * groups, :] = top_ref[1]
-        wide[:, :, (HALO + rows) * groups :, :] = bottom_ref[1]
-    sweep(0, wide, new, coef, None, shifted, groups, [(start, end)])
-
-
-def begin_adjoint(groups, part, top, bottom, coef, wide, new):
+        from_inner, from_outer = facing("space", rows, groups, False)
+        wide[:, :, from_inner, :] = refs[0][...]
+        wide[:, :, from_outer, :] = refs[1][...]
+    sweep(0, wide, new, coef, None, shifted, groups, segments)
+
+
+def begin_adjoint(groups, segments, coef, halos, wide, new):
     f32 = jnp.float32
     shape = jax.ShapeDtypeStruct(wide.shape, f32)
-    arguments = (top, bottom, coef, wide) + (() if new is None else (new,))
+    halos = halos if segments[0][0] == 1 else ()
+    arguments = (coef,) + halos + (wide,) + (() if new is None else (new,))
+    at = 1 + len(halos)
     return pl.pallas_call(
-        functools.partial(begin_kernel, groups, part[0], part[-1] + 1),
+        functools.partial(begin_kernel, groups, segments),
         out_shape=(shape, shape),
         in_specs=[VMEM] * len(arguments),
         out_specs=(VMEM, VMEM),
         scratch_shapes=[pltpu.VMEM((2,) + wide.shape[:2] + (groups, LANES), f32)],
-        input_output_aliases={3: 0} if new is None else {3: 0, 4: 1},
+        input_output_aliases={at: 0} if new is None else {at: 0, at + 1: 1},
         compiler_params=GRANT,
         name="begin",
     )(*arguments)
@@ -552,19 +565,9 @@
     return lax.ppermute(value, axis, [(i, i ^ mask) for i in range(count)])
 
 
-def shift_down(value, axis):
-    count = lax.axis_size(axis)
-    return lax.ppermute(value, axis, [(i, i + 1) for i in range(count - 1)])
-
-
-def shift_up(value, axis):
-    count = lax.axis_size(axis)
-    return lax.ppermute(value, axis, [(i + 1, i) for i in range(count - 1)])
-
-
-def shares(first, last, parts):
-    cuts = [first + (last - first) * i // parts for i in range(parts + 1)]
-    return [range(a, b) for a, b in zip(cuts, cuts[1:])]
+def neighbour_pairs(value, axis, first):
+    lower = range(first, lax.axis_size(axis) - 1, 2)
+    return lax.ppermute(value, axis, [(i, i + 1) for i in lower] + [(i + 1, i) for i in lower])
 
 
 def per_device(potential_start, adjoint_start, conductivity, electrodes, receivers, observed):
@@ -579,35 +582,40 @@
             pieces[k] = exchange(conductivity, "src", k)
     else:
         pieces = [lax.all_gather(conductivity, "src", axis=2, tiled=True)]
-    x_wide, a_wide, first, last = spread_rows(potential_start, adjoint_start)
-    top = shift_down(last, "space")
-    bottom = shift_up(first, "space")
+    x_wide, to_inner, to_outer = spread_rows(potential_start)
+    from_inner = neighbour_pairs(to_inner, "space", 0)
+    from_outer = neighbour_pairs(to_outer, "space", 1)
+    a_wide, a_inner, a_outer = spread_rows(adjoint_start)
+    a_inner = neighbour_pairs(a_inner, "space", 0)
+    a_outer = neighbour_pairs(a_outer, "space", 1)
     nodes, measured = lay_out_nodes(receivers.transpose(0, 2, 1), observed)
-    sigma, sigma_first, sigma_last = assemble_sigma(pieces, groups)
-    sigma_top = shift_down(sigma_last, "space")
-    sigma_bottom = shift_up(sigma_first, "space")
+    sigma, sigma_inner, sigma_outer = assemble_sigma(pieces, groups)
+    sigma_outer = neighbour_pairs(sigma_outer, "space", 1)
+    sigma_inner = neighbour_pairs(sigma_inner, "space", 0)
     ends = electrodes.T
     inner = inner_solve(groups, ends, sigma, x_wide)
     _, forward, coef, surface, _, _, readings = outer_solve(
-        groups, ends, sigma_top, sigma_bottom, top, bottom, nodes, sigma, inner
+        groups, ends, sigma_inner, sigma_outer, from_inner, from_outer, nodes, sigma, inner
     )
 
-    begun = None
+    parts, begun = [inner_rows(0, rows), outer_rows(0, rows)], None
+
+    def begin(wide, new):
+        return begin_adjoint(groups, parts.pop(0), coef, (a_inner, a_outer), wide, new)
+
     if is_power_of_two(strips):
         rounds = strips.bit_length() - 1
-        parts = shares(1, rows + 2 * HALO - 1, max(rounds, 1))
         for i in range(rounds):
             other = exchange(readings, "space", 1 << i)
-            a_wide, begun = begin_adjoint(groups, parts[i], top, bottom, coef, a_wide, begun)
+            if i >= rounds - 2:
+                a_wide, begun = begin(a_wide, begun)
             if i + 1 < rounds:
                 readings = readings + other
         terms = [readings, other] if rounds else [readings]
-        parts = parts[rounds:]
     else:
         terms = [lax.psum(readings, "space")]
-        parts = shares(1, rows + 2 * HALO - 1, 1)
-    for part in parts:
-        a_wide, begun = begin_adjoint(groups, part, top, bottom, coef, a_wide, begun)
+    while parts:
+        a_wide, begun = begin(a_wide, begun)
     blocks = finish_adjoint(
         groups, nodes, terms, measured, a_wide, begun, coef, surface, forward, split if direct else 1
     )

time: 68.5 us -> 69.3 us (1.012)
  waiting for transfers between devices: 11.4 us -> 15.1 us
  starting transfers between devices: 27 us -> 25.6 us
  local copies, waits for them, and re-layouts: 2.46 us -> 1.33 us
    ppermute x9, waiting for transfers between devices: 11.4 us -> 14.1 us  [exchange(): return lax.ppermute(value, axis, [(i, i ^ mask) for i in range(count)])]
    ppermute x4 -> x6, starting transfers between devices: 7.58 us -> 5.63 us  [neighbour_pairs(): lax.ppermute(value, axis, [(i, i + 1) for i in lower] + [(i + 1, i) for i...]
    unnamed x12, local copies, waits for them, and re-layouts: 2.46 us -> 1.33 us
    ppermute x4 -> x6, waiting for transfers between devices: 0.01 us -> 0.94 us  [neighbour_pairs(): lax.ppermute(value, axis, [(i, i + 1) for i in lower] + [(i + 1, i) for i...]
    pallas_call x3 -> x2, Pallas kernels: 2.87 us -> 2.82 us  [begin_adjoint(): pl.pallas_call(functools.partial(begin_kernel, groups, segments), out_sha...]
  transfers between devices with their start and end apart: 13 -> 15, of which waited for: 7 -> 7; matrix products, arithmetic and copies ran while one was open for 0% -> 0% of each run, Pallas kernels for 15% -> 24%
where the time goes in v3:
time: 69.3 us; the launch traced here: 69.2 us
  Pallas kernels  26.3 us (38%)
  starting transfers between devices  25.6 us (37%)
  waiting for transfers between devices  15.1 us (22%)
  local copies, waits for them, and re-layouts  1.33 us (2%)
    ppermute x9, starting transfers between devices, exchange(): return lax.ppermute(value, axis, [(i, i ^ mask) for i in range(count)])  20 us
    ppermute x9, waiting for transfers between devices, exchange(): return lax.ppermute(value, axis, [(i, i ^ mask) for i in range(count)])  14.1 us
    pallas_call x1, Pallas kernels, finish_adjoint(): pl.pallas_call(functools.partial(adjoint_kernel, groups, parts), out_shap...  9.57 us
    pallas_call x1, Pallas kernels, inner_solve(): pl.pallas_call(functools.partial(inner_kernel, groups), out_shape=(jax.Sh...  6.87 us
    pallas_call x1, Pallas kernels, outer_solve(): pl.pallas_call(functools.partial(outer_kernel, groups), out_shape=kept +...  6.46 us
    ppermute x6, starting transfers between devices, neighbour_pairs(): lax.ppermute(value, axis, [(i, i + 1) for i in lower] + [(i + 1, i) for i...  5.63 us
    pallas_call x2, Pallas kernels, begin_adjoint(): pl.pallas_call(functools.partial(begin_kernel, groups, segments), out_sha...  2.82 us
  transfers between devices with their start and end apart: 15, of which 7 were waited for; matrix products, arithmetic and copies ran while one was open for 0% of the time, Pallas kernels for 24%

profile of v3, /device:TPU:0, one launch (start us, length us, event | category | flops | bytes accessed | tf_op | source)
XLA Modules:
  0.0 69.2 jit_solution(4487514282650882555)
XLA Ops:
  0.0 3.1 %collective-permute-start = (f32[4,16,256]{2,1,0:T(8,128)}, f32[4,16,256]{2,1,0:T(8,128)S(1)}, u32[]{:S(2)}, u32[]{:S(2)}) collective-permute-start(f32[4,16,256]{2,1,0:T(8,128)} %refs_0_.1), channel_id=1, source_target_pairs={{0,1},{1,0},{2,3},{3,2},{4,5},{5,4},{6,7},{7,6},{8,9},{9,8},{10,11... | collective-permute-start | bytes 196616 | tf_op jit(solution)/shard_map/ppermute | solution.py:565
  3.1 0.0 copy-start
  3.1 1.2 %copy-done = f32[4,4,16,1024]{3,2,1,0:T(8,128)S(1)} copy-done((f32[4,4,16,1024]{3,2,1,0:T(8,128)S(1)}, f32[4,4,16,1024]{3,2,1,0:T(8,128)}, u32[]{:S(2)}) %copy-start) | copy-done | bytes 1048600
  4.3 0.0 copy-start.3
  4.3 0.2 spread.2
  4.5 0.1 collective-permute-start.5
  4.6 0.8 %collective-permute-start.6 = (f32[4,4,40,128]{3,2,1,0:T(8,128)S(1)}, f32[4,4,40,128]{3,2,1,0:T(8,128)S(1)}, u32[]{:S(2)}, u32[]{:S(2)}) collective-permute-start(f32[4,4,40,128]{3,2,1,0:T(8,128)S(1)} %get-tuple-element.38), channel_id=1, source_target_pairs={{4,8},{12,16},{20,24},{8,4},{16,12},{24,20},{5,9},{13,17},{21,25},... | collective-permute-start | bytes 983048 | tf_op jit(solution)/shard_map/ppermute | solution.py:570
  5.4 0.1 copy-done.1
  5.5 0.2 spread.3
  5.7 2.8 %collective-permute-start.10 = (f32[4,4,40,128]{3,2,1,0:T(8,128)S(1)}, f32[4,4,40,128]{3,2,1,0:T(8,128)S(1)}, u32[]{:S(2)}, u32[]{:S(2)}) collective-permute-start(f32[4,4,40,128]{3,2,1,0:T(8,128)S(1)} %get-tuple-element.50), channel_id=1, source_target_pairs={{0,4},{8,12},{16,20},{24,28},{4,0},{12,8},{20,16},{28,24},{1,5},{9... | collective-permute-start | bytes 983048 | tf_op jit(solution)/shard_map/ppermute | solution.py:570
  8.5 0.7 collective-permute-start.11
  9.2 0.0 collective-permute-done.refs_1_
  9.2 0.0 copy-done.2
  9.2 2.7 %collective-permute-start.1 = (f32[4,16,256]{2,1,0:T(8,128)S(1)}, f32[4,16,256]{2,1,0:T(8,128)S(1)}, u32[]{:S(2)}, u32[]{:S(2)}) collective-permute-start(f32[4,16,256]{2,1,0:T(8,128)S(1)} %copy-done.2), channel_id=1, source_target_pairs={{0,2},{1,3},{2,0},{3,1},{4,6},{5,7},{6,4},{7,5},{8,10},{9,11},{10,... | collective-permute-start | bytes 196616 | tf_op jit(solution)/shard_map/ppermute | solution.py:565
  11.9 3.2 %collective-permute-done.1.refs_2_ = f32[4,16,256]{2,1,0:T(8,128)S(1)} collective-permute-done((f32[4,16,256]{2,1,0:T(8,128)S(1)}, f32[4,16,256]{2,1,0:T(8,128)S(1)}, u32[]{:S(2)}, u32[]{:S(2)}) %collective-permute-start.1) | collective-permute-done | bytes 65568 | tf_op jit(solution)/shard_map/ppermute | solution.py:565
  15.1 1.9 %collective-permute-start.2 = (f32[4,16,256]{2,1,0:T(8,128)S(1)}, f32[4,16,256]{2,1,0:T(8,128)S(1)}, u32[]{:S(2)}, u32[]{:S(2)}) collective-permute-start(f32[4,16,256]{2,1,0:T(8,128)S(1)} %copy-done.2), channel_id=1, source_target_pairs={{0,3},{1,2},{2,1},{3,0},{4,7},{5,6},{6,5},{7,4},{8,11},{9,10},{10,... | collective-permute-start | bytes 196616 | tf_op jit(solution)/shard_map/ppermute | solution.py:565
  16.9 4.2 %collective-permute-done.2.refs_3_ = f32[4,16,256]{2,1,0:T(8,128)S(1)} collective-permute-done((f32[4,16,256]{2,1,0:T(8,128)S(1)}, f32[4,16,256]{2,1,0:T(8,128)S(1)}, u32[]{:S(2)}, u32[]{:S(2)}) %collective-permute-start.2) | collective-permute-done | bytes 65568 | tf_op jit(solution)/shard_map/ppermute | solution.py:565
  21.1 0.1 sigma.1
  21.2 0.6 collective-permute-start.3
  21.8 0.9 %collective-permute-done.3.sigma_inner = f32[4,40,128]{2,1,0:T(8,128)S(1)} collective-permute-done((f32[4,40,128]{2,1,0:T(8,128)S(1)}, f32[4,40,128]{2,1,0:T(8,128)S(1)}, u32[]{:S(2)}, u32[]{:S(2)}) %collective-permute-start.3) | collective-permute-done | bytes 81952 | tf_op jit(solution)/shard_map/ppermute | solution.py:570
  22.7 0.7 collective-permute-start.4
  23.4 0.0 copy-done.4
  23.4 0.0 copy-done.5
  23.4 0.1 nodes.1
  23.5 0.0 copy-done.3
  23.5 6.9 %inner.1 = (f32[4,4,208,128]{3,2,1,0:T(8,128)S(1)}, f32[6,4,208,128]{3,2,1,0:T(8,128)S(1)}, f32[208,128]{1,0:T(8,128)S(1)}, f32[4,4,208,128]{3,2,1,0:T(8,128)S(1)}, f32[4,208,128]{2,1,0:T(8,128)S(1)}) custom-call(s32[2,4]{1,0:T(2,128)S(1)} %bitcast.2, f32[4,208,128]{2,1,0:T(8,128)S(1)} %get-tuple-element.39.sigma.refs_0_, ...), custom_call_target="tpu_custom_call", output_to_operand_aliasing={{0}: (2, {})} | custom-call | tf_op jit(solution)/shard_map/inner/pallas_call | solution.py:316
  30.4 0.0 collective-permute-done.4.sigma_outer
  30.4 0.0 collective-permute-done.5.inner_ref
  30.4 0.0 collective-permute-done.6.outer_ref
  30.4 6.5 %outer.1 = (f32[4,208,128]{2,1,0:T(8,128)S(1)}, f32[4,4,208,128]{3,2,1,0:T(8,128)S(1)}, f32[6,4,208,128]{3,2,1,0:T(8,128)S(1)}, f32[208,128]{1,0:T(8,128)S(1)}, ...) custom-call(s32[2,4]{1,0:T(2,128)S(1)} %bitcast.3, ...), custom_call_target="tpu_custom_call", output_to_operand_aliasing={{0}: (6, {}), {1}: (7, {}), {2}: (8, {}), {3}: (9, {}), {4}... | custom-call | tf_op jit(solution)/shard_map/outer/pallas_call | solution.py:378
  36.9 5.5 %collective-permute-start.7 = (f32[1,256]{1,0:T(1,128)S(1)}, f32[1,256]{1,0:T(1,128)S(1)}, u32[]{:S(2)}, u32[]{:S(2)}) collective-permute-start(f32[1,256]{1,0:T(1,128)S(1)} %get-tuple-element.49), channel_id=1, source_target_pairs={{0,4},{4,0},{8,12},{12,8},{16,20},{20,16},{24,28},{28,24},{1,5},{5... | collective-permute-start | bytes 3080 | tf_op jit(solution)/shard_map/ppermute | solution.py:565
  42.4 0.8 %collective-permute-done.7 = f32[1,256]{1,0:T(1,128)S(1)} collective-permute-done((f32[1,256]{1,0:T(1,128)S(1)}, f32[1,256]{1,0:T(1,128)S(1)}, u32[]{:S(2)}, u32[]{:S(2)}) %collective-permute-start.7) | collective-permute-done | bytes 1056 | tf_op jit(solution)/shard_map/ppermute | solution.py:565
  43.2 1.0 %collective-permute-start.8 = (f32[1,256]{1,0:T(1,128)S(1)}, f32[1,256]{1,0:T(1,128)S(1)}, u32[]{:S(2)}, u32[]{:S(2)}) collective-permute-start(f32[1,256]{1,0:T(1,128)S(1)} %add.15), channel_id=1, source_target_pairs={{0,8},{4,12},{8,0},{12,4},{16,24},{20,28},{24,16},{28,20},{1,9},{5... | collective-permute-start | bytes 3080 | tf_op jit(solution)/shard_map/ppermute | solution.py:565
  44.2 2.5 %collective-permute-done.8 = f32[1,256]{1,0:T(1,128)S(1)} collective-permute-done((f32[1,256]{1,0:T(1,128)S(1)}, f32[1,256]{1,0:T(1,128)S(1)}, u32[]{:S(2)}, u32[]{:S(2)}) %collective-permute-start.8) | collective-permute-done | bytes 1056 | tf_op jit(solution)/shard_map/ppermute | solution.py:565
  46.8 1.5 %collective-permute-start.9 = (f32[1,256]{1,0:T(1,128)S(1)}, f32[1,256]{1,0:T(1,128)S(1)}, u32[]{:S(2)}, u32[]{:S(2)}) collective-permute-start(f32[1,256]{1,0:T(1,128)S(1)} %add.16.refs_0_), channel_id=1, source_target_pairs={{0,16},{4,20},{8,24},{12,28},{16,0},{20,4},{24,8},{28,12},{1,17},{... | collective-permute-start | bytes 3080 | tf_op jit(solution)/shard_map/ppermute | solution.py:565
  48.2 1.6 %begin.2 = (f32[4,4,208,128]{3,2,1,0:T(8,128)S(1)}, f32[4,4,208,128]{3,2,1,0:T(8,128)S(1)}) custom-call(f32[6,4,208,128]{3,2,1,0:T(8,128)S(1)} %get-tuple-element.46.coef, f32[4,4,208,128]{3,2,1,0:T(8,128)S(1)} %get-tuple-element.52.refs_0_), custom_call_target="tpu_custom_call", output_to_operand_aliasing={{0}: (1, {})} | custom-call | tf_op jit(solution)/shard_map/begin/pallas_call | solution.py:406
  49.8 0.0 collective-permute-done.10.refs_0_
  49.8 0.0 collective-permute-done.11.refs_1_
  49.8 1.2 %begin.3 = (f32[4,4,208,128]{3,2,1,0:T(8,128)S(1)}, f32[4,4,208,128]{3,2,1,0:T(8,128)S(1)}) custom-call(f32[6,4,208,128]{3,2,1,0:T(8,128)S(1)} %get-tuple-element.46.coef, f32[4,4,40,128]{3,2,1,0:T(8,128)S(1)} %collective-permute-done.10.refs_0_, ...), custom_call_target="tpu_custom_call", output_to_operand_aliasing={{0}: (3, {}), {1}: (4, {})} | custom-call | tf_op jit(solution)/shard_map/begin/pallas_call | solution.py:406
  51.1 0.0 collective-permute-done.9.refs_1_
  51.1 9.6 %adjoint.1 = (f32[4,4,208,128]{3,2,1,0:T(8,128)S(1)}, f32[4,4,208,128]{3,2,1,0:T(8,128)S(1)}, f32[4,16,256]{2,1,0:T(8,128)S(1)}, f32[4,16,256]{2,1,0:T(8,128)S(1...) custom-call(s32[1,256]{1,0:T(1,128)S(1)} %get-tuple-element.33.nodes_ref, ...), custom_call_target="tpu_custom_call", output_to_operand_aliasing={{0}: (7, {}), {1}: (8, {})} | custom-call | tf_op jit(solution)/shard_map/adjoint/pallas_call | solution.py:542
  60.6 0.1 collective-permute-start.14
  60.7 1.7 %collective-permute-start.13 = (f32[4,16,256]{2,1,0:T(8,128)S(1)}, f32[4,16,256]{2,1,0:T(8,128)S(1)}, u32[]{:S(2)}, u32[]{:S(2)}) collective-permute-start(f32[4,16,256]{2,1,0:T(8,128)S(1)} %get-tuple-element.59), channel_id=1, source_target_pairs={{0,2},{1,3},{2,0},{3,1},{4,6},{5,7},{6,4},{7,5},{8,10},{9,11},{10,... | collective-permute-start | bytes 196616 | tf_op jit(solution)/shard_map/ppermute | solution.py:565
  62.4 2.7 %collective-permute-start.12 = (f32[4,16,256]{2,1,0:T(8,128)S(1)}, f32[4,16,256]{2,1,0:T(8,128)S(1)}, u32[]{:S(2)}, u32[]{:S(2)}) collective-permute-start(f32[4,16,256]{2,1,0:T(8,128)S(1)} %get-tuple-element.58), channel_id=1, source_target_pairs={{0,3},{1,2},{2,1},{3,0},{4,7},{5,6},{6,5},{7,4},{8,11},{9,10},{10,... | collective-permute-start | bytes 196616 | tf_op jit(solution)/shard_map/ppermute | solution.py:565
  65.1 0.0 collective-permute-done.14
  65.1 1.4 %collective-permute-done.13 = f32[4,16,256]{2,1,0:T(8,128)S(1)} collective-permute-done((f32[4,16,256]{2,1,0:T(8,128)S(1)}, f32[4,16,256]{2,1,0:T(8,128)S(1)}, u32[]{:S(2)}, u32[]{:S(2)}) %collective-permute-start.13) | collective-permute-done | bytes 65568 | tf_op jit(solution)/shard_map/ppermute | solution.py:565
  66.5 2.0 %collective-permute-done.12 = f32[4,16,256]{2,1,0:T(8,128)S(1)} collective-permute-done((f32[4,16,256]{2,1,0:T(8,128)S(1)}, f32[4,16,256]{2,1,0:T(8,128)S(1)}, u32[]{:S(2)}, u32[]{:S(2)}) %collective-permute-start.12) | collective-permute-done | bytes 65568 | tf_op jit(solution)/shard_map/ppermute | solution.py:565
  68.5 0.6 add_add_fusion
  (6 shorter events, 0.0 us)
Async XLA Ops:
  0.0 9.2 %collective-permute-start = (f32[4,16,256]{2,1,0:T(8,128)}, f32[4,16,256]{2,1,0:T(8,128)S(1)}, u32[]{:S(2)}, u32[]{:S(2)}) collective-permute-start(f32[4,16,256]{2,1,0:T(8,128)} %refs_0_.1), channel_id=1, source_target_pairs={{0,1},{1,0},{2,3},{3,2},{4,5},{5,4},{6,7},{7,6},{8,9},{9,8},{10,11... | collective-permute-start | bytes 196616 | tf_op jit(solution)/shard_map/ppermute | solution.py:565
  3.1 1.2 %copy-start = (f32[4,4,16,1024]{3,2,1,0:T(8,128)S(1)}, f32[4,4,16,1024]{3,2,1,0:T(8,128)}, u32[]{:S(2)}) copy-start(f32[4,4,16,1024]{3,2,1,0:T(8,128)} %x_ref.2) | copy-start | bytes 3145732
  4.3 1.2 %copy-start.1 = (f32[4,4,16,1024]{3,2,1,0:T(8,128)S(1)}, f32[4,4,16,1024]{3,2,1,0:T(8,128)}, u32[]{:S(2)}) copy-start(f32[4,4,16,1024]{3,2,1,0:T(8,128)} %x_ref.3) | copy-start | bytes 3145732
  4.3 4.9 %copy-start.2 = (f32[4,16,256]{2,1,0:T(8,128)S(1)}, f32[4,16,256]{2,1,0:T(8,128)}, u32[]{:S(2)}) copy-start(f32[4,16,256]{2,1,0:T(8,128)} %refs_0_.1) | copy-start | bytes 196612
  4.3 19.1 %copy-start.4 = (s32[4,32,2]{1,2,0:T(2,128)S(1)}, s32[4,32,2]{1,2,0:T(2,128)}, u32[]{:S(2)}) copy-start(s32[4,32,2]{1,2,0:T(2,128)} %param.10) | copy-start | bytes 3076
  4.3 19.1 %copy-start.5 = (f32[4,32]{1,0:T(4,128)S(1)}, f32[4,32]{1,0:T(4,128)}, u32[]{:S(2)}) copy-start(f32[4,32]{1,0:T(4,128)} %observed_ref.1) | copy-start | bytes 1540
  4.3 19.2 %copy-start.3 = (s32[4,2]{0,1:T(2,128)S(1)}, s32[4,2]{0,1:T(2,128)}, u32[]{:S(2)}) copy-start(s32[4,2]{0,1:T(2,128)} %param.9) | copy-start | bytes 100
  4.5 25.9 %collective-permute-start.5 = (f32[4,4,40,128]{3,2,1,0:T(8,128)S(1)}, f32[4,4,40,128]{3,2,1,0:T(8,128)S(1)}, u32[]{:S(2)}, u32[]{:S(2)}) collective-permute-start(f32[4,4,40,128]{3,2,1,0:T(8,128)S(1)} %get-tuple-element.37), channel_id=1, source_target_pairs={{0,4},{8,12},{16,20},{24,28},{4,0},{12,8},{20,16},{28,24},{1,5},{9... | collective-permute-start | bytes 983048 | tf_op jit(solution)/shard_map/ppermute | solution.py:570
  4.6 25.8 %collective-permute-start.6 = (f32[4,4,40,128]{3,2,1,0:T(8,128)S(1)}, f32[4,4,40,128]{3,2,1,0:T(8,128)S(1)}, u32[]{:S(2)}, u32[]{:S(2)}) collective-permute-start(f32[4,4,40,128]{3,2,1,0:T(8,128)S(1)} %get-tuple-element.38), channel_id=1, source_target_pairs={{4,8},{12,16},{20,24},{8,4},{16,12},{24,20},{5,9},{13,17},{21,25},... | collective-permute-start | bytes 983048 | tf_op jit(solution)/shard_map/ppermute | solution.py:570
  5.7 44.1 %collective-permute-start.10 = (f32[4,4,40,128]{3,2,1,0:T(8,128)S(1)}, f32[4,4,40,128]{3,2,1,0:T(8,128)S(1)}, u32[]{:S(2)}, u32[]{:S(2)}) collective-permute-start(f32[4,4,40,128]{3,2,1,0:T(8,128)S(1)} %get-tuple-element.50), channel_id=1, source_target_pairs={{0,4},{8,12},{16,20},{24,28},{4,0},{12,8},{20,16},{28,24},{1,5},{9... | collective-permute-start | bytes 983048 | tf_op jit(solution)/shard_map/ppermute | solution.py:570
  8.5 41.3 %collective-permute-start.11 = (f32[4,4,40,128]{3,2,1,0:T(8,128)S(1)}, f32[4,4,40,128]{3,2,1,0:T(8,128)S(1)}, u32[]{:S(2)}, u32[]{:S(2)}) collective-permute-start(f32[4,4,40,128]{3,2,1,0:T(8,128)S(1)} %get-tuple-element.51), channel_id=1, source_target_pairs={{4,8},{12,16},{20,24},{8,4},{16,12},{24,20},{5,9},{13,17},{21,25},... | collective-permute-start | bytes 983048 | tf_op jit(solution)/shard_map/ppermute | solution.py:570
  9.2 5.8 %collective-permute-start.1 = (f32[4,16,256]{2,1,0:T(8,128)S(1)}, f32[4,16,256]{2,1,0:T(8,128)S(1)}, u32[]{:S(2)}, u32[]{:S(2)}) collective-permute-start(f32[4,16,256]{2,1,0:T(8,128)S(1)} %copy-done.2), channel_id=1, source_target_pairs={{0,2},{1,3},{2,0},{3,1},{4,6},{5,7},{6,4},{7,5},{8,10},{9,11},{10,... | collective-permute-start | bytes 196616 | tf_op jit(solution)/shard_map/ppermute | solution.py:565
  15.1 6.1 %collective-permute-start.2 = (f32[4,16,256]{2,1,0:T(8,128)S(1)}, f32[4,16,256]{2,1,0:T(8,128)S(1)}, u32[]{:S(2)}, u32[]{:S(2)}) collective-permute-start(f32[4,16,256]{2,1,0:T(8,128)S(1)} %copy-done.2), channel_id=1, source_target_pairs={{0,3},{1,2},{2,1},{3,0},{4,7},{5,6},{6,5},{7,4},{8,11},{9,10},{10,... | collective-permute-start | bytes 196616 | tf_op jit(solution)/shard_map/ppermute | solution.py:565
  21.2 1.5 %collective-permute-start.3 = (f32[4,40,128]{2,1,0:T(8,128)S(1)}, f32[4,40,128]{2,1,0:T(8,128)S(1)}, u32[]{:S(2)}, u32[]{:S(2)}) collective-permute-start(f32[4,40,128]{2,1,0:T(8,128)S(1)} %get-tuple-element.35), channel_id=1, source_target_pairs={{0,4},{8,12},{16,20},{24,28},{4,0},{12,8},{20,16},{28,24},{1,5},{9... | collective-permute-start | bytes 245768 | tf_op jit(solution)/shard_map/ppermute | solution.py:570
  22.7 7.6 %collective-permute-start.4 = (f32[4,40,128]{2,1,0:T(8,128)S(1)}, f32[4,40,128]{2,1,0:T(8,128)S(1)}, u32[]{:S(2)}, u32[]{:S(2)}) collective-permute-start(f32[4,40,128]{2,1,0:T(8,128)S(1)} %get-tuple-element.36), channel_id=1, source_target_pairs={{4,8},{12,16},{20,24},{8,4},{16,12},{24,20},{5,9},{13,17},{21,25},... | collective-permute-start | bytes 245768 | tf_op jit(solution)/shard_map/ppermute | solution.py:570
  36.9 6.3 %collective-permute-start.7 = (f32[1,256]{1,0:T(1,128)S(1)}, f32[1,256]{1,0:T(1,128)S(1)}, u32[]{:S(2)}, u32[]{:S(2)}) collective-permute-start(f32[1,256]{1,0:T(1,128)S(1)} %get-tuple-element.49), channel_id=1, source_target_pairs={{0,4},{4,0},{8,12},{12,8},{16,20},{20,16},{24,28},{28,24},{1,5},{5... | collective-permute-start | bytes 3080 | tf_op jit(solution)/shard_map/ppermute | solution.py:565
  43.2 3.6 %collective-permute-start.8 = (f32[1,256]{1,0:T(1,128)S(1)}, f32[1,256]{1,0:T(1,128)S(1)}, u32[]{:S(2)}, u32[]{:S(2)}) collective-permute-start(f32[1,256]{1,0:T(1,128)S(1)} %add.15), channel_id=1, source_target_pairs={{0,8},{4,12},{8,0},{12,4},{16,24},{20,28},{24,16},{28,20},{1,9},{5... | collective-permute-start | bytes 3080 | tf_op jit(solution)/shard_map/ppermute | solution.py:565
  46.8 4.3 %collective-permute-start.9 = (f32[1,256]{1,0:T(1,128)S(1)}, f32[1,256]{1,0:T(1,128)S(1)}, u32[]{:S(2)}, u32[]{:S(2)}) collective-permute-start(f32[1,256]{1,0:T(1,128)S(1)} %add.16.refs_0_), channel_id=1, source_target_pairs={{0,16},{4,20},{8,24},{12,28},{16,0},{20,4},{24,8},{28,12},{1,17},{... | collective-permute-start | bytes 3080 | tf_op jit(solution)/shard_map/ppermute | solution.py:565
  60.6 4.5 %collective-permute-start.14 = (f32[4,16,256]{2,1,0:T(8,128)S(1)}, f32[4,16,256]{2,1,0:T(8,128)S(1)}, u32[]{:S(2)}, u32[]{:S(2)}) collective-permute-start(f32[4,16,256]{2,1,0:T(8,128)S(1)} %get-tuple-element.60), channel_id=1, source_target_pairs={{0,1},{1,0},{2,3},{3,2},{4,5},{5,4},{6,7},{7,6},{8,9},{9,8},{10,11... | collective-permute-start | bytes 196616 | tf_op jit(solution)/shard_map/ppermute | solution.py:565
  60.7 5.8 %collective-permute-start.13 = (f32[4,16,256]{2,1,0:T(8,128)S(1)}, f32[4,16,256]{2,1,0:T(8,128)S(1)}, u32[]{:S(2)}, u32[]{:S(2)}) collective-permute-start(f32[4,16,256]{2,1,0:T(8,128)S(1)} %get-tuple-element.59), channel_id=1, source_target_pairs={{0,2},{1,3},{2,0},{3,1},{4,6},{5,7},{6,4},{7,5},{8,10},{9,11},{10,... | collective-permute-start | bytes 196616 | tf_op jit(solution)/shard_map/ppermute | solution.py:565
  62.4 6.1 %collective-permute-start.12 = (f32[4,16,256]{2,1,0:T(8,128)S(1)}, f32[4,16,256]{2,1,0:T(8,128)S(1)}, u32[]{:S(2)}, u32[]{:S(2)}) collective-permute-start(f32[4,16,256]{2,1,0:T(8,128)S(1)} %get-tuple-element.58), channel_id=1, source_target_pairs={{0,3},{1,2},{2,1},{3,0},{4,7},{5,6},{6,5},{7,4},{8,11},{9,10},{10,... | collective-permute-start | bytes 196616 | tf_op jit(solution)/shard_map/ppermute | solution.py:565

commit v4 on v3

--- a/solution.py
+++ b/solution.py
@@ -16,6 +16,7 @@
 DELTA = 0.975
 LANES = 128
 HALO = SWEEPS + 1
+BATCH = 8
 
 VMEM = pl.BlockSpec(memory_space=pltpu.VMEM)
 SMEM = pl.BlockSpec(memory_space=pltpu.SMEM)
@@ -36,32 +37,79 @@
 STEPS, FINAL = product_form()
 
 
-def rows_of(start, count, groups):
-    begin = start * groups
-    if not isinstance(begin, int):
-        begin = pl.multiple_of(begin, groups)
-    return pl.ds(begin, count * groups)
-
-
-def from_right(v, last_lane):
-    groups = v.shape[0]
-    turned = pltpu.roll(v, LANES - 1, 1)
-    return jnp.where(last_lane, pltpu.roll(turned, groups - 1, 0), turned)
-
-
-def from_left(v, first_lane):
-    turned = pltpu.roll(v, 1, 1)
-    return jnp.where(first_lane, pltpu.roll(turned, 1, 0), turned)
-
-
-def lane_masks(groups):
+def dense(e, groups):
+    begin = e * groups
+    return pl.ds(begin if isinstance(begin, int) else pl.multiple_of(begin, groups), groups)
+
+
+def tile(e, groups):
+    begin = (2 * e + 1) * groups
+    return pl.ds(begin if isinstance(begin, int) else pl.multiple_of(begin, groups), groups)
+
+
+def left_of(e, groups):
+    return pl.ds((2 * e + 1) * groups - 1, groups)
+
+
+def right_of(e, groups):
+    return pl.ds((2 * e + 1) * groups + 1, groups)
+
+
+def sublane(first, j, count, groups):
+    return pl.ds((2 * first + 1) * groups + j, count, stride=2 * groups)
+
+
+def extent_of(wide, groups):
+    return wide.shape[-2] // (2 * groups) - 1
+
+
+def wide_length(rows, columns):
+    return (rows + 2 * HALO + 1) * 2 * (columns // LANES)
+
+
+def refill(planes, groups, first, last):
+    extent = extent_of(planes[0], groups)
+    for start in range(first, last, BATCH):
+        start = min(start, extent - BATCH)
+        for plane in planes:
+            plane[sublane(start, -1, BATCH, groups), :] = pltpu.roll(
+                plane[sublane(start, groups - 1, BATCH, groups), :], 1, 1
+            )
+            plane[sublane(start, groups, BATCH, groups), :] = pltpu.roll(
+                plane[sublane(start, 0, BATCH, groups), :], LANES - 1, 1
+            )
+
+
+def planes_of(field, layers=None):
+    layers = range(field.shape[1]) if layers is None else layers
+    return [field.at[s, l] for s in range(field.shape[0]) for l in layers]
+
+
+def doubled(rows):
+    count = rows.shape[0]
+    if count == LANES:
+        return rows
+    return jnp.concatenate([rows] * (LANES // count) + ([rows[: LANES % count]] if LANES % count else []), axis=0)
+
+
+def columns_to_sublanes(read, write, work, groups):
+    for j in range(groups):
+        work[j * LANES : (j + 1) * LANES, :] = doubled(read(j)).T
+    for s in range(groups):
+        write(s, work[pl.ds(s, LANES, stride=groups), :].T)
+
+
+def columns_to_lanes(read, write, work, groups):
+    for s in range(groups):
+        work[pl.ds(s, LANES, stride=groups), :] = doubled(read(s)).T
+    for j in range(groups):
+        write(j, work[j * LANES : (j + 1) * LANES, :].T)
+
+
+def end_masks(groups):
     lane = lax.broadcasted_iota(jnp.int32, (groups, LANES), 1)
     group = lax.broadcasted_iota(jnp.int32, (groups, LANES), 0)
-    first_lane = lane == 0
-    last_lane = lane == LANES - 1
-    first_column = first_lane & (group == 0)
-    last_column = last_lane & (group == groups - 1)
-    return first_lane, last_lane, first_column, last_column
+    return (lane == 0) & (group == 0), (lane == LANES - 1) & (group == groups - 1)
 
 
 def three_parts(x):
@@ -72,44 +120,60 @@
     return jnp.concatenate([high, middle, low], axis=0)
 
 
-def column_hits(columns, j):
+def column_hits(columns, j, groups):
     nodes = columns.shape[1]
-    c = lax.broadcasted_iota(jnp.int32, (LANES, nodes), 0) + j * LANES
+    c = lax.broadcasted_iota(jnp.int32, (LANES, nodes), 0) * groups + j
     return jnp.where(c == columns, 1.0, 0.0).astype(jnp.bfloat16)
 
 
-def facing(axis, rows, groups, sent):
+def facing(axis, rows, sent):
     even = lax.rem(lax.axis_index(axis), 2) == 0
     low, high = (HALO, rows) if sent else (0, HALO + rows)
-    return [
-        pl.ds(pl.multiple_of(jnp.where(condition, high, low) * groups, groups), HALO * groups)
-        for condition in (even, jnp.logical_not(even))
-    ]
-
-
-def spread_kernel(groups, x_ref, wide, inner_ref, outer_ref):
+    return jnp.where(even, high, low), jnp.where(even, low, high)
+
+
+def take_rows(wide, first, out, groups):
+    for h in range(HALO):
+        out[..., h * groups : (h + 1) * groups, :] = wide[..., tile(first + h, groups), :]
+
+
+def put_rows(wide, first, received, groups):
+    for h in range(HALO):
+        wide[..., tile(first + h, groups), :] = received[..., h * groups : (h + 1) * groups, :]
+
+
+def spread_kernel(groups, x_ref, wide, inner_ref, outer_ref, work):
     sources, layers, rows, _ = x_ref.shape
-    for s in range(sources):
-        for l in range(layers):
-            for j in range(groups):
-                wide[s, l, pl.ds(HALO * groups + j, rows, stride=groups), :] = x_ref[
-                    s, l, :, j * LANES : (j + 1) * LANES
-                ]
-    to_inner, to_outer = facing("space", rows, groups, True)
-    inner_ref[...] = wide[:, :, to_inner, :]
-    outer_ref[...] = wide[:, :, to_outer, :]
+    fields = [(s, l) for s in range(sources) for l in range(layers)]
+    per = LANES // rows
+    for at in range(0, len(fields), per):
+        block = fields[at : at + per]
+
+        def read(j):
+            return jnp.concatenate([x_ref[s, l, :, j * LANES : (j + 1) * LANES] for s, l in block], axis=0)
+
+        def write(j, turned):
+            for i, (s, l) in enumerate(block):
+                wide[s, l, sublane(HALO, j, rows, groups), :] = turned[i * rows : (i + 1) * rows]
+
+        columns_to_sublanes(read, write, work, groups)
+    refill(planes_of(wide), groups, HALO, HALO + rows)
+    to_inner, to_outer = facing("space", rows, True)
+    take_rows(wide, to_inner, inner_ref, groups)
+    take_rows(wide, to_outer, outer_ref, groups)
 
 
 def spread_rows(x):
     sources, layers, rows, columns = x.shape
     groups = columns // LANES
-    wide = jax.ShapeDtypeStruct((sources, layers, (rows + 2 * HALO) * groups, LANES), jnp.float32)
+    wide = jax.ShapeDtypeStruct((sources, layers, wide_length(rows, columns), LANES), jnp.float32)
     halo = jax.ShapeDtypeStruct((sources, layers, HALO * groups, LANES), jnp.float32)
     return pl.pallas_call(
         functools.partial(spread_kernel, groups),
         out_shape=(wide, halo, halo),
         in_specs=[VMEM],
         out_specs=(VMEM,) * 3,
+        scratch_shapes=[pltpu.VMEM((columns, LANES), jnp.float32)],
         compiler_params=GRANT,
         name="spread",
     )(x)
@@ -139,34 +203,42 @@
 
 
 def sigma_kernel(groups, *refs):
-    pieces, (wide_ref, inner_ref, outer_ref, stage) = refs[:-4], refs[-4:]
+    pieces, (wide_ref, inner_ref, outer_ref, stage, work) = refs[:-5], refs[-5:]
     count = len(pieces)
     layers, rows, share = pieces[0].shape
     me = lax.axis_index("src") if count > 1 else 0
     for k, piece in enumerate(pieces):
         stage[me ^ k] = piece[...]
     per = share // LANES
-    for q in range(count):
+
+    def read(j):
+        return stage[j // per, :, :, (j % per) * LANES : (j % per + 1) * LANES].reshape(layers * rows, LANES)
+
+    def write(j, turned):
         for l in range(layers):
-            for t in range(per):
-                wide_ref[l, pl.ds(HALO * groups + q * per + t, rows, stride=groups), :] = stage[
-                    q, l, :, t * LANES : (t + 1) * LANES
-                ]
-    to_inner, to_outer = facing("space", rows, groups, True)
-    inner_ref[...] = wide_ref[:, to_inner, :]
-    outer_ref[...] = wide_ref[:, to_outer, :]
+            wide_ref[l, sublane(HALO, j, rows, groups), :] = turned[l * rows : (l + 1) * rows]
+
+    columns_to_sublanes(read, write, work, groups)
+    refill([wide_ref.at[l] for l in range(layers)], groups, HALO, HALO + rows)
+    to_inner, to_outer = facing("space", rows, True)
+    take_rows(wide_ref, to_inner, inner_ref, groups)
+    take_rows(wide_ref, to_outer, outer_ref, groups)
 
 
 def assemble_sigma(pieces, groups):
     layers, rows, share = pieces[0].shape
-    wide = jax.ShapeDtypeStruct((layers, (rows + 2 * HALO) * groups, LANES), jnp.float32)
+    columns = groups * LANES
+    wide = jax.ShapeDtypeStruct((layers, wide_length(rows, columns), LANES), jnp.float32)
     halo = jax.ShapeDtypeStruct((layers, HALO * groups, LANES), jnp.float32)
     return pl.pallas_call(
         functools.partial(sigma_kernel, groups),
         out_shape=(wide, halo, halo),
         in_specs=[VMEM] * len(pieces),
         out_specs=(VMEM, VMEM, VMEM),
-        scratch_shapes=[pltpu.VMEM((len(pieces), layers, rows, share), jnp.float32)],
+        scratch_shapes=[
+            pltpu.VMEM((len(pieces), layers, rows, share), jnp.float32),
+            pltpu.VMEM((columns, LANES), jnp.float32),
+        ],
         compiler_params=GRANT,
         name="sigma",
     )(*pieces)
@@ -188,21 +260,19 @@
 
 def coefficient_rows(sigma, coef, surface, groups, segments):
     layers = sigma.shape[0]
-    first_lane, last_lane, first_column, last_column = lane_masks(groups)
+    first_column, last_column = end_masks(groups)
     count, number = row_numbers(segments)
 
     def body(i, carry):
         e = number(i)
-        here = rows_of(e, 1, groups)
-        above = rows_of(e - 1, 1, groups)
-        below = rows_of(e + 1, 1, groups)
-        centre = [sigma[l, here, :] for l in range(layers)]
+        here = dense(e, groups)
+        centre = [sigma[l, tile(e, groups), :] for l in range(layers)]
         for l in range(layers):
             c = centre[l]
-            up = 0.5 * (c + sigma[l, above, :])
-            down = 0.5 * (c + sigma[l, below, :])
-            left = 0.5 * (c + jnp.where(first_column, 0.0, from_left(c, first_lane)))
-            right = 0.5 * (c + jnp.where(last_column, 0.0, from_right(c, last_lane)))
+            up = 0.5 * (c + sigma[l, tile(e - 1, groups), :])
+            down = 0.5 * (c + sigma[l, tile(e + 1, groups), :])
+            left = 0.5 * (c + jnp.where(first_column, 0.0, sigma[l, left_of(e, groups), :]))
+            right = 0.5 * (c + jnp.where(last_column, 0.0, sigma[l, right_of(e, groups), :]))
             lower = 0.5 * (c + centre[l - 1]) if l > 0 else 0.5 * c
             upper = 0.5 * (c + centre[l + 1]) if l + 1 < layers else 0.5 * c
             diagonal = up + down + left + right + lower + upper + GAMMA * c
@@ -223,53 +293,40 @@
     lax.fori_loop(0, count, body, 0)
 
 
-def sweep(step, old, new, coef, plane, shifted, groups, segments):
+def sweep(step, old, new, coef, plane, groups, segments):
     p, g = STEPS[step]
     sources, layers = old.shape[:2]
-    first_lane, last_lane, _, _ = lane_masks(groups)
     count, number = row_numbers(segments)
 
-    def turn(e):
-        here = rows_of(e, 1, groups)
-        before = pl.ds(e * groups - 1, groups)
-        after = pl.ds(e * groups + 1, groups)
-        for l in range(layers):
-            for s in range(sources):
-                v = old[s, l, here, :]
-                shifted[0, s, l] = pltpu.roll(jnp.where(last_lane, old[s, l, before, :], v), 1, 1)
-                shifted[1, s, l] = pltpu.roll(jnp.where(first_lane, old[s, l, after, :], v), LANES - 1, 1)
-
     def row(e):
-        here = rows_of(e, 1, groups)
-        above = rows_of(e - 1, 1, groups)
-        below = rows_of(e + 1, 1, groups)
+        here = dense(e, groups)
         for l in range(layers):
             weight = [coef[i, l, here, :] for i in range(4)]
             lower = coef[4, l, here, :] if l > 0 else None
             upper = coef[5, l, here, :] if l + 1 < layers else None
             for s in range(sources):
-                total = p * old[s, l, here, :]
-                total += weight[0] * old[s, l, above, :]
-                total += weight[1] * old[s, l, below, :]
-                total += weight[2] * shifted[0, s, l]
-                total += weight[3] * shifted[1, s, l]
+                total = p * old[s, l, tile(e, groups), :]
+                total += weight[0] * old[s, l, tile(e - 1, groups), :]
+                total += weight[1] * old[s, l, tile(e + 1, groups), :]
+                total += weight[2] * old[s, l, left_of(e, groups), :]
+                total += weight[3] * old[s, l, right_of(e, groups), :]
                 if lower is not None:
-                    total += lower * old[s, l - 1, here, :]
+                    total += lower * old[s, l - 1, tile(e, groups), :]
                 if upper is not None:
-                    total += upper * old[s, l + 1, here, :]
+                    total += upper * old[s, l + 1, tile(e, groups), :]
                 if l == 0 and plane is not None:
                     amount = plane[s, here, :]
                     total += amount if g == 1.0 else g * amount
-                new[s, l, here, :] = total
+                new[s, l, tile(e, groups), :] = total
 
     def body(i, carry):
-        row(number(i))
-        turn(number(i + 1))
+        row(number(2 * i))
+        row(number(2 * i + 1))
         return carry
 
-    turn(number(0))
-    lax.fori_loop(0, count - 1, body, 0)
-    row(number(count - 1))
+    lax.fori_loop(0, count // 2, body, 0)
+    if count % 2:
+        row(number(count - 1))
 
 
 def inner_rows(step, rows):
@@ -284,8 +341,8 @@
     columns = groups * LANES
     first_row = lax.axis_index("space") * rows
     lowest, highest = segments[0][0], segments[-1][1] - 1
-    column = lax.broadcasted_iota(jnp.int32, (groups, LANES), 0) * LANES + lax.broadcasted_iota(
-        jnp.int32, (groups, LANES), 1
+    column = lax.broadcasted_iota(jnp.int32, (groups, LANES), 1) * groups + lax.broadcasted_iota(
+        jnp.int32, (groups, LANES), 0
     )
     for s in range(plane.shape[0]):
         for k, current in enumerate((CURRENT, -CURRENT)):
@@ -293,25 +350,27 @@
             row = node // columns
             e = row - first_row + HALO
             inside = functools.reduce(jnp.logical_or, [(e >= a) & (e < b) for a, b in segments])
-            here = rows_of(jnp.clip(e, lowest, highest), 1, groups)
+            here = dense(jnp.clip(e, lowest, highest), groups)
             hit = (column == node - row * columns) & inside
             plane[s, here, :] += jnp.where(hit, current * surface[here, :], 0.0)
 
 
-def inner_kernel(groups, electrodes_ref, sigma, _, wide, coef, surface, other, plane, shifted):
-    rows = wide.shape[2] // groups - 2 * HALO
+def inner_kernel(groups, electrodes_ref, sigma, _, wide, coef, surface, other, plane):
+    rows = extent_of(wide, groups) - 2 * HALO
     segments = inner_rows(0, rows)
     coefficient_rows(sigma, coef, surface, groups, segments)
     plane[...] = jnp.zeros(plane.shape, jnp.float32)
     add_electrodes(electrodes_ref, plane, surface, rows, groups, segments)
     old, new = wide, other
     for step in range(SWEEPS):
-        sweep(step, old, new, coef, plane, shifted, groups, inner_rows(step, rows))
+        sweep(step, old, new, coef, plane, groups, inner_rows(step, rows))
+        refill(planes_of(new), groups, *inner_rows(step, rows)[0])
         old, new = new, old
 
 
 def inner_solve(groups, electrodes, sigma, wide):
-    sources, layers, tall, _ = wide.shape
+    sources, layers = wide.shape[:2]
+    tall = extent_of(wide, groups) * groups
     f32 = jnp.float32
     return pl.pallas_call(
         functools.partial(inner_kernel, groups),
@@ -324,7 +383,6 @@
         ),
         in_specs=[SMEM, VMEM, VMEM],
         out_specs=(VMEM,) * 5,
-        scratch_shapes=[pltpu.VMEM((2, sources, layers, groups, LANES), f32)],
         input_output_aliases={2: 0},
         compiler_params=GRANT,
         name="inner",
@@ -334,22 +392,29 @@
 def outer_kernel(
     groups, electrodes_ref, sigma_inner, sigma_outer, inner_ref, outer_ref, nodes_ref, *refs
 ):
-    sigma, wide, coef, surface, other, plane, readings_ref, shifted = refs[6:]
-    sources, _, tall, _ = wide.shape
+    sigma, wide, coef, surface, other, plane, readings_ref = refs[6:]
+    sources, layers = wide.shape[:2]
     columns = groups * LANES
-    rows = tall // groups - 2 * HALO
+    extent = extent_of(wide, groups)
+    rows = extent - 2 * HALO
     first_row = lax.axis_index("space") * rows
-    from_inner, from_outer = facing("space", rows, groups, False)
-    sigma[:, from_inner, :] = sigma_inner[...]
-    sigma[:, from_outer, :] = sigma_outer[...]
-    wide[:, :, from_inner, :] = inner_ref[...]
-    wide[:, :, from_outer, :] = outer_ref[...]
+    from_inner, from_outer = facing("space", rows, False)
+    put_rows(sigma, from_inner, sigma_inner, groups)
+    put_rows(sigma, from_outer, sigma_outer, groups)
+    put_rows(wide, from_inner, inner_ref, groups)
+    put_rows(wide, from_outer, outer_ref, groups)
+    conductivity = [sigma.at[l] for l in range(layers)]
+    for first, last in ((0, HALO), (HALO + rows, extent)):
+        refill(conductivity, groups, first, last)
+        refill(planes_of(wide), groups, first, last)
     segments = outer_rows(0, rows)
     coefficient_rows(sigma, coef, surface, groups, segments)
     add_electrodes(electrodes_ref, plane, surface, rows, groups, segments)
     old, new = wide, other
     for step in range(SWEEPS):
-        sweep(step, old, new, coef, plane, shifted, groups, outer_rows(step, rows))
+        sweep(step, old, new, coef, plane, groups, outer_rows(step, rows))
+        for first, last in outer_rows(step, rows):
+            refill(planes_of(new), groups, first, last)
         old, new = new, old
 
     node = nodes_ref[...]
@@ -358,10 +423,8 @@
     count = node.shape[1]
     picked = jnp.zeros((3 * sources * rows, count), jnp.float32)
     for j in range(groups):
-        tile = jnp.concatenate(
-            [old[s, 0, pl.ds(HALO * groups + j, rows, stride=groups), :] for s in range(sources)], axis=0
-        )
-        picked += jnp.dot(three_parts(tile), column_hits(node_column, j), preferred_element_type=jnp.float32)
+        values = jnp.concatenate([old[s, 0, sublane(HALO, j, rows, groups), :] for s in range(sources)], axis=0)
+        picked += jnp.dot(three_parts(values), column_hits(node_column, j, groups), preferred_element_type=jnp.float32)
     size = sources * rows
     picked = picked[:size] + picked[size : 2 * size] + picked[2 * size :]
     r = lax.broadcasted_iota(jnp.int32, (size, count), 0)
@@ -372,7 +435,6 @@
 
 def outer_solve(groups, electrodes, sigma_inner, sigma_outer, from_inner, from_outer, nodes, sigma, inner):
     carried = (sigma,) + tuple(inner)
-    sources, layers = inner[0].shape[:2]
     f32 = jnp.float32
     kept = tuple(jax.ShapeDtypeStruct(x.shape, f32) for x in carried)
     return pl.pallas_call(
@@ -380,7 +442,6 @@
         out_shape=kept + (jax.ShapeDtypeStruct((1, nodes.shape[1]), f32),),
         in_specs=[SMEM] + [VMEM] * 11,
         out_specs=(VMEM,) * 7,
-        scratch_shapes=[pltpu.VMEM((2, sources, layers, groups, LANES), f32)],
         input_output_aliases={6 + i: i for i in range(6)},
         compiler_params=GRANT,
         name="outer",
@@ -388,13 +449,18 @@
 
 
 def begin_kernel(groups, segments, coef, *refs):
-    wide, new, shifted = refs[-3:]
+    wide, new = refs[-2:]
+    extent = extent_of(wide, groups)
+    rows = extent - 2 * HALO
     if segments[0][0] == 1:
-        rows = wide.shape[2] // groups - 2 * HALO
-        from_inner, from_outer = facing("space", rows, groups, False)
-        wide[:, :, from_inner, :] = refs[0][...]
-        wide[:, :, from_outer, :] = refs[1][...]
-    sweep(0, wide, new, coef, None, shifted, groups, segments)
+        from_inner, from_outer = facing("space", rows, False)
+        put_rows(wide, from_inner, refs[0], groups)
+        put_rows(wide, from_outer, refs[1], groups)
+        for first, last in ((0, HALO), (HALO + rows, extent)):
+            refill(planes_of(wide), groups, first, last)
+    sweep(0, wide, new, coef, None, groups, segments)
+    for first, last in segments:
+        refill(planes_of(new, range(1, wide.shape[1])), groups, first, last)
 
 
 def begin_adjoint(groups, segments, coef, halos, wide, new):
@@ -408,7 +474,6 @@
         out_shape=(shape, shape),
         in_specs=[VMEM] * len(arguments),
         out_specs=(VMEM, VMEM),
-        scratch_shapes=[pltpu.VMEM((2,) + wide.shape[:2] + (groups, LANES), f32)],
         input_output_aliases={at: 0} if new is None else {at: 0, at + 1: 1},
         compiler_params=GRANT,
         name="begin",
@@ -417,10 +482,10 @@
 
 def adjoint_kernel(groups, parts, nodes_ref, observed_ref, coef, surface, forward, *refs):
     readings_refs, refs = refs[:parts], refs[parts + 2 :]
-    (wide, new), blocks, (plane, gradient, staged, shifted) = refs[:2], refs[2:-4], refs[-4:]
-    sources, layers, tall, _ = wide.shape
+    (wide, new), blocks, (plane, gradient, staged, work) = refs[:2], refs[2:-4], refs[-4:]
+    sources, layers = wide.shape[:2]
     columns = groups * LANES
-    extent = tall // groups
+    extent = extent_of(wide, groups)
     rows = extent - 2 * HALO
     count = nodes_ref.shape[1]
     per_source = count // sources
@@ -445,7 +510,7 @@
     spread = three_parts(jnp.where(hit, amounts, 0.0))
     for j in range(groups):
         part = lax.dot_general(
-            spread, column_hits(node_column, j), (((1,), (1,)), ((), ())), preferred_element_type=jnp.float32
+            spread, column_hits(node_column, j, groups), (((1,), (1,)), ((), ())), preferred_element_type=jnp.float32
         )
         part = part[:size] + part[size : 2 * size] + part[2 * size :]
         where = pl.ds(groups + j, span, stride=groups)
@@ -453,29 +518,22 @@
         for s in range(sources):
             amount = part[s * span : (s + 1) * span] * weight
             plane[s, where, :] = amount
-            new[s, 0, where, :] += amount
+            new[s, 0, sublane(1, j, span, groups), :] += amount
+    refill(planes_of(new, range(1)), groups, 1, extent - 1)
 
     old, newer = new, wide
     for step in range(1, SWEEPS):
-        sweep(step, old, newer, coef, plane, shifted, groups, [(1 + step, extent - 1 - step)])
+        segment = (1 + step, extent - 1 - step)
+        sweep(step, old, newer, coef, plane, groups, [segment])
+        refill(planes_of(newer), groups, *segment)
         old, newer = newer, old
     adjoint = old
 
-    first_lane, _, first_column, last_column = lane_masks(groups)
-    both = (forward, adjoint)
-
-    def turn(e):
-        here = rows_of(e, 1, groups)
-        after = pl.ds(e * groups + 1, groups)
-        for i, field in enumerate(both):
-            for l in range(layers):
-                for s in range(sources):
-                    v = jnp.where(first_lane, field[s, l, after, :], field[s, l, here, :])
-                    shifted[i, s, l] = pltpu.roll(v, LANES - 1, 1)
+    first_column, last_column = end_masks(groups)
+    first_sublane = lax.broadcasted_iota(jnp.int32, (groups, LANES), 0) == 0
 
     def row(e, above_faces):
-        here = rows_of(e, 1, groups)
-        below = rows_of(e + 1, 1, groups)
+        here, below, right_here = tile(e, groups), tile(e + 1, groups), right_of(e, groups)
         sums = []
         for l in range(layers):
             for s in range(sources):
@@ -483,7 +541,7 @@
                 terms = [
                     u * a,
                     (u - forward[s, l, below, :]) * (a - adjoint[s, l, below, :]),
-                    (u - shifted[0, s, l]) * (a - shifted[1, s, l]),
+                    (u - forward[s, l, right_here, :]) * (a - adjoint[s, l, right_here, :]),
                 ]
                 if l + 1 < layers:
                     terms.append((u - forward[s, l + 1, here, :]) * (a - adjoint[s, l + 1, here, :]))
@@ -492,48 +550,48 @@
         for l in range(layers):
             product, down, right = sums[l][:3]
             right = jnp.where(last_column, product, right)
-            left = jnp.where(first_column, product, from_left(right, first_lane))
+            turned = pltpu.roll(right, 1, 0)
+            left = jnp.where(first_sublane, pltpu.roll(turned, 1, 1), turned)
+            left = jnp.where(first_column, product, left)
             upper = sums[l][3] if l + 1 < layers else product
             lower = sums[l - 1][3] if l > 0 else product
             total = product + above_faces[l] + down + right + left + lower + upper
-            gradient[l, rows_of(e - HALO, 1, groups), :] = (-0.5 * FINAL * FINAL) * total
+            gradient[l, dense(e - HALO, groups), :] = (-0.5 * FINAL * FINAL) * total
         return tuple(sums[l][1] for l in range(layers))
 
     above_faces = []
     for l in range(layers):
         for s in range(sources):
-            above, here = rows_of(HALO - 1, 1, groups), rows_of(HALO, 1, groups)
+            above, here = tile(HALO - 1, groups), tile(HALO, groups)
             term = (forward[s, l, above, :] - forward[s, l, here, :]) * (
                 adjoint[s, l, above, :] - adjoint[s, l, here, :]
             )
             total = term if s == 0 else total + term
         above_faces.append(total)
 
-    def body(e, above_faces):
-        above_faces = row(e, above_faces)
-        turn(e + 1)
-        return above_faces
-
-    turn(HALO)
-    above_faces = lax.fori_loop(HALO, HALO + rows - 1, body, tuple(above_faces))
-    row(HALO + rows - 1, above_faces)
+    lax.fori_loop(HALO, HALO + rows, row, tuple(above_faces))
 
     count_blocks = len(blocks)
     me = lax.axis_index("src") if count_blocks > 1 else 0
     per = groups // count_blocks
-    for q in range(count_blocks):
+
+    def read(j):
+        return jnp.concatenate([gradient[l, pl.ds(j, rows, stride=groups), :] for l in range(layers)], axis=0)
+
+    def write(j, turned):
         for l in range(layers):
-            for t in range(per):
-                staged[q, l, :, t * LANES : (t + 1) * LANES] = gradient[
-                    l, pl.ds(q * per + t, rows, stride=groups), :
-                ]
+            staged[j // per, l, :, (j % per) * LANES : (j % per + 1) * LANES] = turned[l * rows : (l + 1) * rows]
+
+    columns_to_lanes(read, write, work, groups)
     for i, block in enumerate(blocks):
         block[...] = staged[me ^ i]
 
 
 def finish_adjoint(groups, nodes, readings, observed, wide, new, coef, surface, forward, blocks):
-    sources, layers, tall, _ = wide.shape
-    rows = tall // groups - 2 * HALO
+    sources, layers = wide.shape[:2]
+    extent = extent_of(wide, groups)
+    tall = extent * groups
+    rows = extent - 2 * HALO
     columns = groups * LANES
     f32 = jnp.float32
     block = jax.ShapeDtypeStruct((layers, rows, columns // blocks), f32)
@@ -548,7 +606,7 @@
             pltpu.VMEM((sources, tall, LANES), f32),
             pltpu.VMEM((layers, rows * groups, LANES), f32),
             pltpu.VMEM((blocks, layers, rows, columns // blocks), f32),
-            pltpu.VMEM((2, sources, layers, groups, LANES), f32),
+            pltpu.VMEM((columns, LANES), f32),
         ],
         input_output_aliases={5 + parts: 0, 6 + parts: 1},
         compiler_params=GRANT,

time: 69.3 us -> 65 us (0.938)
  Pallas kernels: 26.3 us -> 16.7 us
  local copies, waits for them, and re-layouts: 1.33 us -> 5.34 us
  waiting for transfers between devices: 15.1 us -> 16.2 us
    unnamed x12 -> x14, local copies, waits for them, and re-layouts: 1.33 us -> 5.34 us
    pallas_call x1, Pallas kernels: 9.57 us -> 5.61 us  [finish_adjoint(): pl.pallas_call(functools.partial(adjoint_kernel, groups, parts), out_shap...]
    pallas_call x1, Pallas kernels: 6.87 us -> 3.18 us  [inner_solve(): pl.pallas_call(functools.partial(inner_kernel, groups), out_shape=(jax.Sh...]
    pallas_call x1, Pallas kernels: 6.46 us -> 3.78 us  [outer_solve(): pl.pallas_call(functools.partial(outer_kernel, groups), out_shape=kept +...]
    pallas_call x2, Pallas kernels: 0.41 us -> 2.1 us  [spread_rows(): pl.pallas_call(functools.partial(spread_kernel, groups), out_shape=(wide,...]
    pallas_call x2, Pallas kernels: 2.82 us -> 1.41 us  [begin_adjoint(): pl.pallas_call(functools.partial(begin_kernel, groups, segments), out_sha...]
    ppermute x9, waiting for transfers between devices: 14.1 us -> 15.3 us  [exchange(): return lax.ppermute(value, axis, [(i, i ^ mask) for i in range(count)])]
  transfers between devices with their start and end apart: 15 -> 15, of which waited for: 7 -> 8; matrix products, arithmetic and copies ran while one was open for 0% -> 0% of each run, Pallas kernels for 24% -> 17%
where the time goes in v4:
time: 65 us; the launch traced here: 64.7 us
  starting transfers between devices  25.6 us (39%)
  Pallas kernels  16.7 us (26%)
  waiting for transfers between devices  16.2 us (25%)
  local copies, waits for them, and re-layouts  5.34 us (8%)
  other arithmetic  0.65 us (1%)
    ppermute x9, starting transfers between devices, exchange(): return lax.ppermute(value, axis, [(i, i ^ mask) for i in range(count)])  20 us
    ppermute x9, waiting for transfers between devices, exchange(): return lax.ppermute(value, axis, [(i, i ^ mask) for i in range(count)])  15.3 us
    pallas_call x1, Pallas kernels, finish_adjoint(): pl.pallas_call(functools.partial(adjoint_kernel, groups, parts), out_shap...  5.61 us
    ppermute x6, starting transfers between devices, neighbour_pairs(): lax.ppermute(value, axis, [(i, i + 1) for i in lower] + [(i + 1, i) for i...  5.56 us
    unnamed x14, local copies, waits for them, and re-layouts  5.34 us
    pallas_call x1, Pallas kernels, outer_solve(): pl.pallas_call(functools.partial(outer_kernel, groups), out_shape=kept +...  3.78 us
    pallas_call x1, Pallas kernels, inner_solve(): pl.pallas_call(functools.partial(inner_kernel, groups), out_shape=(jax.Sh...  3.18 us
    pallas_call x2, Pallas kernels, spread_rows(): pl.pallas_call(functools.partial(spread_kernel, groups), out_shape=(wide,...  2.1 us
  transfers between devices with their start and end apart: 15, of which 8 were waited for; matrix products, arithmetic and copies ran while one was open for 0% of the time, Pallas kernels for 17%

profile of v4, /device:TPU:0, one launch (start us, length us, event | category | flops | bytes accessed | tf_op | source)
XLA Modules:
  0.0 64.7 jit_solution(13625393485876030510)
XLA Ops:
  0.0 3.1 %collective-permute-start = (f32[4,16,256]{2,1,0:T(8,128)}, f32[4,16,256]{2,1,0:T(8,128)S(1)}, u32[]{:S(2)}, u32[]{:S(2)}) collective-permute-start(f32[4,16,256]{2,1,0:T(8,128)} %refs_0_.1), channel_id=1, source_target_pairs={{0,1},{1,0},{2,3},{3,2},{4,5},{5,4},{6,7},{7,6},{8,9},{9,8},{10,11... | collective-permute-start | bytes 196616 | tf_op jit(solution)/shard_map/ppermute | solution.py:623
  3.1 1.2 %copy-done = f32[4,4,16,1024]{3,2,1,0:T(8,128)S(1)} copy-done((f32[4,4,16,1024]{3,2,1,0:T(8,128)S(1)}, f32[4,4,16,1024]{3,2,1,0:T(8,128)}, u32[]{:S(2)}) %copy-start) | copy-done | bytes 1048600
  4.3 1.1 %spread.2 = (f32[4,4,432,128]{3,2,1,0:T(8,128)S(1)}, f32[4,4,40,128]{3,2,1,0:T(8,128)S(1)}, f32[4,4,40,128]{3,2,1,0:T(8,128)S(1)}) custom-call(f32[4,4,16,1024]{3,2,1,0:T(8,128)S(1)} %copy-done), custom_call_target="tpu_custom_call" | custom-call | tf_op jit(solution)/shard_map/spread/pallas_call | solution.py:171
  5.3 0.1 collective-permute-start.5
  5.4 0.7 %collective-permute-start.6 = (f32[4,4,40,128]{3,2,1,0:T(8,128)S(1)}, f32[4,4,40,128]{3,2,1,0:T(8,128)S(1)}, u32[]{:S(2)}, u32[]{:S(2)}) collective-permute-start(f32[4,4,40,128]{3,2,1,0:T(8,128)S(1)} %get-tuple-element.38), channel_id=1, source_target_pairs={{4,8},{12,16},{20,24},{8,4},{16,12},{24,20},{5,9},{13,17},{21,25},... | collective-permute-start | bytes 983048 | tf_op jit(solution)/shard_map/ppermute | solution.py:628
  6.1 0.0 copy-start.1
  6.1 1.2 %copy-done.1 = f32[4,4,16,1024]{3,2,1,0:T(8,128)S(1)} copy-done((f32[4,4,16,1024]{3,2,1,0:T(8,128)S(1)}, f32[4,4,16,1024]{3,2,1,0:T(8,128)}, u32[]{:S(2)}) %copy-start.1) | copy-done | bytes 1048600
  7.3 1.1 %spread.3 = (f32[4,4,432,128]{3,2,1,0:T(8,128)S(1)}, f32[4,4,40,128]{3,2,1,0:T(8,128)S(1)}, f32[4,4,40,128]{3,2,1,0:T(8,128)S(1)}) custom-call(f32[4,4,16,1024]{3,2,1,0:T(8,128)S(1)} %copy-done.1), custom_call_target="tpu_custom_call" | custom-call | tf_op jit(solution)/shard_map/spread/pallas_call | solution.py:171
  8.4 2.9 %collective-permute-start.10 = (f32[4,4,40,128]{3,2,1,0:T(8,128)S(1)}, f32[4,4,40,128]{3,2,1,0:T(8,128)S(1)}, u32[]{:S(2)}, u32[]{:S(2)}) collective-permute-start(f32[4,4,40,128]{3,2,1,0:T(8,128)S(1)} %get-tuple-element.50), channel_id=1, source_target_pairs={{0,4},{8,12},{16,20},{24,28},{4,0},{12,8},{20,16},{28,24},{1,5},{9... | collective-permute-start | bytes 983048 | tf_op jit(solution)/shard_map/ppermute | solution.py:628
  11.3 0.7 %collective-permute-start.11 = (f32[4,4,40,128]{3,2,1,0:T(8,128)S(1)}, f32[4,4,40,128]{3,2,1,0:T(8,128)S(1)}, u32[]{:S(2)}, u32[]{:S(2)}) collective-permute-start(f32[4,4,40,128]{3,2,1,0:T(8,128)S(1)} %get-tuple-element.51), channel_id=1, source_target_pairs={{4,8},{12,16},{20,24},{8,4},{16,12},{24,20},{5,9},{13,17},{21,25},... | collective-permute-start | bytes 983048 | tf_op jit(solution)/shard_map/ppermute | solution.py:628
  12.0 0.0 collective-permute-done.refs_1_
  12.0 2.7 %collective-permute-start.1 = (f32[4,16,256]{2,1,0:T(8,128)}, f32[4,16,256]{2,1,0:T(8,128)S(1)}, u32[]{:S(2)}, u32[]{:S(2)}) collective-permute-start(f32[4,16,256]{2,1,0:T(8,128)} %refs_0_.1), channel_id=1, source_target_pairs={{0,2},{1,3},{2,0},{3,1},{4,6},{5,7},{6,4},{7,5},{8,10},{9,11},{10,... | collective-permute-start | bytes 196616 | tf_op jit(solution)/shard_map/ppermute | solution.py:623
  14.6 3.4 %collective-permute-done.1.refs_2_ = f32[4,16,256]{2,1,0:T(8,128)S(1)} collective-permute-done((f32[4,16,256]{2,1,0:T(8,128)}, f32[4,16,256]{2,1,0:T(8,128)S(1)}, u32[]{:S(2)}, u32[]{:S(2)}) %collective-permute-start.1) | collective-permute-done | bytes 65568 | tf_op jit(solution)/shard_map/ppermute | solution.py:623
  18.0 1.9 %collective-permute-start.2 = (f32[4,16,256]{2,1,0:T(8,128)}, f32[4,16,256]{2,1,0:T(8,128)S(1)}, u32[]{:S(2)}, u32[]{:S(2)}) collective-permute-start(f32[4,16,256]{2,1,0:T(8,128)} %refs_0_.1), channel_id=1, source_target_pairs={{0,3},{1,2},{2,1},{3,0},{4,7},{5,6},{6,5},{7,4},{8,11},{9,10},{10,... | collective-permute-start | bytes 196616 | tf_op jit(solution)/shard_map/ppermute | solution.py:623
  19.9 4.4 %collective-permute-done.2.refs_3_ = f32[4,16,256]{2,1,0:T(8,128)S(1)} collective-permute-done((f32[4,16,256]{2,1,0:T(8,128)}, f32[4,16,256]{2,1,0:T(8,128)S(1)}, u32[]{:S(2)}, u32[]{:S(2)}) %collective-permute-start.2) | collective-permute-done | bytes 65568 | tf_op jit(solution)/shard_map/ppermute | solution.py:623
  24.3 0.8 %copy-done.2 = f32[4,16,256]{2,1,0:T(8,128)S(1)} copy-done((f32[4,16,256]{2,1,0:T(8,128)S(1)}, f32[4,16,256]{2,1,0:T(8,128)}, u32[]{:S(2)}) %copy-start.2) | copy-done | bytes 65560
  25.1 0.5 sigma.1
  25.7 0.6 collective-permute-start.3
  26.3 0.9 %collective-permute-done.3.sigma_inner = f32[4,40,128]{2,1,0:T(8,128)S(1)} collective-permute-done((f32[4,40,128]{2,1,0:T(8,128)S(1)}, f32[4,40,128]{2,1,0:T(8,128)S(1)}, u32[]{:S(2)}, u32[]{:S(2)}) %collective-permute-start.3) | collective-permute-done | bytes 81952 | tf_op jit(solution)/shard_map/ppermute | solution.py:628
  27.2 0.7 %collective-permute-start.4 = (f32[4,40,128]{2,1,0:T(8,128)S(1)}, f32[4,40,128]{2,1,0:T(8,128)S(1)}, u32[]{:S(2)}, u32[]{:S(2)}) collective-permute-start(f32[4,40,128]{2,1,0:T(8,128)S(1)} %get-tuple-element.36), channel_id=1, source_target_pairs={{4,8},{12,16},{20,24},{8,4},{16,12},{24,20},{5,9},{13,17},{21,25},... | collective-permute-start | bytes 245768 | tf_op jit(solution)/shard_map/ppermute | solution.py:628
  27.8 0.0 copy-start.5
  27.9 0.7 %copy-done.5 = s32[4,32,2]{1,2,0:T(2,128)S(1)} copy-done((s32[4,32,2]{1,2,0:T(2,128)S(1)}, s32[4,32,2]{1,2,0:T(2,128)}, u32[]{:S(2)}) %copy-start.5) | copy-done | bytes 1048
  28.5 0.7 %copy-done.6 = f32[4,32]{1,0:T(4,128)S(1)} copy-done((f32[4,32]{1,0:T(4,128)S(1)}, f32[4,32]{1,0:T(4,128)}, u32[]{:S(2)}) %copy-start.6) | copy-done | bytes 536
  29.2 0.1 nodes.1
  29.3 0.7 %copy-done.3 = s32[4,2]{0,1:T(2,128)S(1)} copy-done((s32[4,2]{0,1:T(2,128)S(1)}, s32[4,2]{0,1:T(2,128)}, u32[]{:S(2)}) %copy-start.3) | copy-done | bytes 56
  30.0 3.2 %inner.1 = (f32[4,4,432,128]{3,2,1,0:T(8,128)S(1)}, f32[6,4,208,128]{3,2,1,0:T(8,128)S(1)}, f32[208,128]{1,0:T(8,128)S(1)}, f32[4,4,432,128]{3,2,1,0:T(8,128)S(1)}, f32[4,208,128]{2,1,0:T(8,128)S(1)}) custom-call(s32[2,4]{1,0:T(2,128)S(1)} %bitcast.2, f32[4,432,128]{2,1,0:T(8,128)S(1)} %get-tuple-element.39.sigma.refs_0_, ...), custom_call_target="tpu_custom_call", output_to_operand_aliasing={{0}: (2, {})} | custom-call | tf_op jit(solution)/shard_map/inner/pallas_call | solution.py:375
  33.2 0.0 collective-permute-done.4.sigma_outer
  33.2 0.0 collective-permute-done.5.inner_ref
  33.2 0.0 collective-permute-done.6.outer_ref
  33.2 3.8 %outer.1 = (f32[4,432,128]{2,1,0:T(8,128)S(1)}, f32[4,4,432,128]{3,2,1,0:T(8,128)S(1)}, f32[6,4,208,128]{3,2,1,0:T(8,128)S(1)}, f32[208,128]{1,0:T(8,128)S(1)}, ...) custom-call(s32[2,4]{1,0:T(2,128)S(1)} %bitcast.3, ...), custom_call_target="tpu_custom_call", output_to_operand_aliasing={{0}: (6, {}), {1}: (7, {}), {2}: (8, {}), {3}: (9, {}), {4}... | custom-call | tf_op jit(solution)/shard_map/outer/pallas_call | solution.py:440
  37.0 5.5 %collective-permute-start.7 = (f32[1,256]{1,0:T(1,128)S(1)}, f32[1,256]{1,0:T(1,128)S(1)}, u32[]{:S(2)}, u32[]{:S(2)}) collective-permute-start(f32[1,256]{1,0:T(1,128)S(1)} %get-tuple-element.49), channel_id=1, source_target_pairs={{0,4},{4,0},{8,12},{12,8},{16,20},{20,16},{24,28},{28,24},{1,5},{5... | collective-permute-start | bytes 3080 | tf_op jit(solution)/shard_map/ppermute | solution.py:623
  42.5 0.8 %collective-permute-done.7 = f32[1,256]{1,0:T(1,128)S(1)} collective-permute-done((f32[1,256]{1,0:T(1,128)S(1)}, f32[1,256]{1,0:T(1,128)S(1)}, u32[]{:S(2)}, u32[]{:S(2)}) %collective-permute-start.7) | collective-permute-done | bytes 1056 | tf_op jit(solution)/shard_map/ppermute | solution.py:623
  43.3 1.0 %collective-permute-start.8 = (f32[1,256]{1,0:T(1,128)S(1)}, f32[1,256]{1,0:T(1,128)S(1)}, u32[]{:S(2)}, u32[]{:S(2)}) collective-permute-start(f32[1,256]{1,0:T(1,128)S(1)} %add.15), channel_id=1, source_target_pairs={{0,8},{4,12},{8,0},{12,4},{16,24},{20,28},{24,16},{28,20},{1,9},{5... | collective-permute-start | bytes 3080 | tf_op jit(solution)/shard_map/ppermute | solution.py:623
  44.3 2.5 %collective-permute-done.8 = f32[1,256]{1,0:T(1,128)S(1)} collective-permute-done((f32[1,256]{1,0:T(1,128)S(1)}, f32[1,256]{1,0:T(1,128)S(1)}, u32[]{:S(2)}, u32[]{:S(2)}) %collective-permute-start.8) | collective-permute-done | bytes 1056 | tf_op jit(solution)/shard_map/ppermute | solution.py:623
  46.9 1.5 %collective-permute-start.9 = (f32[1,256]{1,0:T(1,128)S(1)}, f32[1,256]{1,0:T(1,128)S(1)}, u32[]{:S(2)}, u32[]{:S(2)}) collective-permute-start(f32[1,256]{1,0:T(1,128)S(1)} %add.16.refs_0_), channel_id=1, source_target_pairs={{0,16},{4,20},{8,24},{12,28},{16,0},{20,4},{24,8},{28,12},{1,17},{... | collective-permute-start | bytes 3080 | tf_op jit(solution)/shard_map/ppermute | solution.py:623
  48.3 0.6 begin.2
  48.9 0.0 collective-permute-done.10.refs_0_
  49.0 0.0 collective-permute-done.11.refs_1_
  49.0 0.8 %begin.3 = (f32[4,4,432,128]{3,2,1,0:T(8,128)S(1)}, f32[4,4,432,128]{3,2,1,0:T(8,128)S(1)}) custom-call(f32[6,4,208,128]{3,2,1,0:T(8,128)S(1)} %get-tuple-element.46.coef, f32[4,4,40,128]{3,2,1,0:T(8,128)S(1)} %collective-permute-done.10.refs_0_, ...), custom_call_target="tpu_custom_call", output_to_operand_aliasing={{0}: (3, {}), {1}: (4, {})} | custom-call | tf_op jit(solution)/shard_map/begin/pallas_call | solution.py:472
  49.8 0.7 %collective-permute-done.9.refs_1_ = f32[1,256]{1,0:T(1,128)S(1)} collective-permute-done((f32[1,256]{1,0:T(1,128)S(1)}, f32[1,256]{1,0:T(1,128)S(1)}, u32[]{:S(2)}, u32[]{:S(2)}) %collective-permute-start.9) | collective-permute-done | bytes 1056 | tf_op jit(solution)/shard_map/ppermute | solution.py:623
  50.5 5.6 %adjoint.1 = (f32[4,4,432,128]{3,2,1,0:T(8,128)S(1)}, f32[4,4,432,128]{3,2,1,0:T(8,128)S(1)}, f32[4,16,256]{2,1,0:T(8,128)S(1)}, f32[4,16,256]{2,1,0:T(8,128)S(1...) custom-call(s32[1,256]{1,0:T(1,128)S(1)} %get-tuple-element.33.nodes_ref, ...), custom_call_target="tpu_custom_call", output_to_operand_aliasing={{0}: (7, {}), {1}: (8, {})} | custom-call | tf_op jit(solution)/shard_map/adjoint/pallas_call | solution.py:600
  56.1 0.1 collective-permute-start.14
  56.2 1.8 %collective-permute-start.13 = (f32[4,16,256]{2,1,0:T(8,128)S(1)}, f32[4,16,256]{2,1,0:T(8,128)S(1)}, u32[]{:S(2)}, u32[]{:S(2)}) collective-permute-start(f32[4,16,256]{2,1,0:T(8,128)S(1)} %get-tuple-element.59), channel_id=1, source_target_pairs={{0,2},{1,3},{2,0},{3,1},{4,6},{5,7},{6,4},{7,5},{8,10},{9,11},{10,... | collective-permute-start | bytes 196616 | tf_op jit(solution)/shard_map/ppermute | solution.py:623
  58.0 2.6 %collective-permute-start.12 = (f32[4,16,256]{2,1,0:T(8,128)S(1)}, f32[4,16,256]{2,1,0:T(8,128)S(1)}, u32[]{:S(2)}, u32[]{:S(2)}) collective-permute-start(f32[4,16,256]{2,1,0:T(8,128)S(1)} %get-tuple-element.58), channel_id=1, source_target_pairs={{0,3},{1,2},{2,1},{3,0},{4,7},{5,6},{6,5},{7,4},{8,11},{9,10},{10,... | collective-permute-start | bytes 196616 | tf_op jit(solution)/shard_map/ppermute | solution.py:623
  60.5 1.3 %collective-permute-done.14 = f32[4,16,256]{2,1,0:T(8,128)S(1)} collective-permute-done((f32[4,16,256]{2,1,0:T(8,128)S(1)}, f32[4,16,256]{2,1,0:T(8,128)S(1)}, u32[]{:S(2)}, u32[]{:S(2)}) %collective-permute-start.14) | collective-permute-done | bytes 65568 | tf_op jit(solution)/shard_map/ppermute | solution.py:623
  61.8 0.0 collective-permute-done.13
  61.8 2.2 %collective-permute-done.12 = f32[4,16,256]{2,1,0:T(8,128)S(1)} collective-permute-done((f32[4,16,256]{2,1,0:T(8,128)S(1)}, f32[4,16,256]{2,1,0:T(8,128)S(1)}, u32[]{:S(2)}, u32[]{:S(2)}) %collective-permute-start.12) | collective-permute-done | bytes 65568 | tf_op jit(solution)/shard_map/ppermute | solution.py:623
  64.0 0.6 %add_add_fusion = f32[4,16,256]{2,1,0:T(8,128)} fusion(f32[4,16,256]{2,1,0:T(8,128)S(1)} %collective-permute-done.14, f32[4,16,256]{2,1,0:T(8,128)S(1)} %collective-permute-done.13, f32[4,16,256]{2,1,0:T(8,128)S(1)} %get-tuple-element.57, f32[4,16,256]{2,1,0:T(8,128)S(1)} %collective-permute-done.12), kind=kLoop, calls=%fused_computation | loop fusion | flops 49152 | bytes 327680 | tf_op jit(solution)/shard_map/add | solution.py:683
  (8 shorter events, 0.0 us)
Async XLA Ops:
  0.0 12.0 %collective-permute-start = (f32[4,16,256]{2,1,0:T(8,128)}, f32[4,16,256]{2,1,0:T(8,128)S(1)}, u32[]{:S(2)}, u32[]{:S(2)}) collective-permute-start(f32[4,16,256]{2,1,0:T(8,128)} %refs_0_.1), channel_id=1, source_target_pairs={{0,1},{1,0},{2,3},{3,2},{4,5},{5,4},{6,7},{7,6},{8,9},{9,8},{10,11... | collective-permute-start | bytes 196616 | tf_op jit(solution)/shard_map/ppermute | solution.py:623
  3.1 1.2 %copy-start = (f32[4,4,16,1024]{3,2,1,0:T(8,128)S(1)}, f32[4,4,16,1024]{3,2,1,0:T(8,128)}, u32[]{:S(2)}) copy-start(f32[4,4,16,1024]{3,2,1,0:T(8,128)} %x_ref.2) | copy-start | bytes 3145732
  4.3 28.9 %copy-start.4 = (s32[4,2]{0,1:T(2,128)S(1)}, s32[4,2]{0,1:T(2,128)}, u32[]{:S(2)}) copy-start(s32[4,2]{0,1:T(2,128)} %param.9) | copy-start | bytes 100
  5.3 27.8 %collective-permute-start.5 = (f32[4,4,40,128]{3,2,1,0:T(8,128)S(1)}, f32[4,4,40,128]{3,2,1,0:T(8,128)S(1)}, u32[]{:S(2)}, u32[]{:S(2)}) collective-permute-start(f32[4,4,40,128]{3,2,1,0:T(8,128)S(1)} %get-tuple-element.37), channel_id=1, source_target_pairs={{0,4},{8,12},{16,20},{24,28},{4,0},{12,8},{20,16},{28,24},{1,5},{9... | collective-permute-start | bytes 983048 | tf_op jit(solution)/shard_map/ppermute | solution.py:628
  5.4 27.8 %collective-permute-start.6 = (f32[4,4,40,128]{3,2,1,0:T(8,128)S(1)}, f32[4,4,40,128]{3,2,1,0:T(8,128)S(1)}, u32[]{:S(2)}, u32[]{:S(2)}) collective-permute-start(f32[4,4,40,128]{3,2,1,0:T(8,128)S(1)} %get-tuple-element.38), channel_id=1, source_target_pairs={{4,8},{12,16},{20,24},{8,4},{16,12},{24,20},{5,9},{13,17},{21,25},... | collective-permute-start | bytes 983048 | tf_op jit(solution)/shard_map/ppermute | solution.py:628
  6.1 1.2 %copy-start.1 = (f32[4,4,16,1024]{3,2,1,0:T(8,128)S(1)}, f32[4,4,16,1024]{3,2,1,0:T(8,128)}, u32[]{:S(2)}) copy-start(f32[4,4,16,1024]{3,2,1,0:T(8,128)} %x_ref.3) | copy-start | bytes 3145732
  8.4 40.6 %collective-permute-start.10 = (f32[4,4,40,128]{3,2,1,0:T(8,128)S(1)}, f32[4,4,40,128]{3,2,1,0:T(8,128)S(1)}, u32[]{:S(2)}, u32[]{:S(2)}) collective-permute-start(f32[4,4,40,128]{3,2,1,0:T(8,128)S(1)} %get-tuple-element.50), channel_id=1, source_target_pairs={{0,4},{8,12},{16,20},{24,28},{4,0},{12,8},{20,16},{28,24},{1,5},{9... | collective-permute-start | bytes 983048 | tf_op jit(solution)/shard_map/ppermute | solution.py:628
  11.3 37.7 %collective-permute-start.11 = (f32[4,4,40,128]{3,2,1,0:T(8,128)S(1)}, f32[4,4,40,128]{3,2,1,0:T(8,128)S(1)}, u32[]{:S(2)}, u32[]{:S(2)}) collective-permute-start(f32[4,4,40,128]{3,2,1,0:T(8,128)S(1)} %get-tuple-element.51), channel_id=1, source_target_pairs={{4,8},{12,16},{20,24},{8,4},{16,12},{24,20},{5,9},{13,17},{21,25},... | collective-permute-start | bytes 983048 | tf_op jit(solution)/shard_map/ppermute | solution.py:628
  12.0 6.0 %collective-permute-start.1 = (f32[4,16,256]{2,1,0:T(8,128)}, f32[4,16,256]{2,1,0:T(8,128)S(1)}, u32[]{:S(2)}, u32[]{:S(2)}) collective-permute-start(f32[4,16,256]{2,1,0:T(8,128)} %refs_0_.1), channel_id=1, source_target_pairs={{0,2},{1,3},{2,0},{3,1},{4,6},{5,7},{6,4},{7,5},{8,10},{9,11},{10,... | collective-permute-start | bytes 196616 | tf_op jit(solution)/shard_map/ppermute | solution.py:623
  18.0 6.3 %collective-permute-start.2 = (f32[4,16,256]{2,1,0:T(8,128)}, f32[4,16,256]{2,1,0:T(8,128)S(1)}, u32[]{:S(2)}, u32[]{:S(2)}) collective-permute-start(f32[4,16,256]{2,1,0:T(8,128)} %refs_0_.1), channel_id=1, source_target_pairs={{0,3},{1,2},{2,1},{3,0},{4,7},{5,6},{6,5},{7,4},{8,11},{9,10},{10,... | collective-permute-start | bytes 196616 | tf_op jit(solution)/shard_map/ppermute | solution.py:623
  24.3 0.8 %copy-start.2 = (f32[4,16,256]{2,1,0:T(8,128)S(1)}, f32[4,16,256]{2,1,0:T(8,128)}, u32[]{:S(2)}) copy-start(f32[4,16,256]{2,1,0:T(8,128)} %refs_0_.1) | copy-start | bytes 196612
  25.7 1.5 %collective-permute-start.3 = (f32[4,40,128]{2,1,0:T(8,128)S(1)}, f32[4,40,128]{2,1,0:T(8,128)S(1)}, u32[]{:S(2)}, u32[]{:S(2)}) collective-permute-start(f32[4,40,128]{2,1,0:T(8,128)S(1)} %get-tuple-element.35), channel_id=1, source_target_pairs={{0,4},{8,12},{16,20},{24,28},{4,0},{12,8},{20,16},{28,24},{1,5},{9... | collective-permute-start | bytes 245768 | tf_op jit(solution)/shard_map/ppermute | solution.py:628
  27.2 6.0 %collective-permute-start.4 = (f32[4,40,128]{2,1,0:T(8,128)S(1)}, f32[4,40,128]{2,1,0:T(8,128)S(1)}, u32[]{:S(2)}, u32[]{:S(2)}) collective-permute-start(f32[4,40,128]{2,1,0:T(8,128)S(1)} %get-tuple-element.36), channel_id=1, source_target_pairs={{4,8},{12,16},{20,24},{8,4},{16,12},{24,20},{5,9},{13,17},{21,25},... | collective-permute-start | bytes 245768 | tf_op jit(solution)/shard_map/ppermute | solution.py:628
  27.8 0.7 %copy-start.5 = (s32[4,32,2]{1,2,0:T(2,128)S(1)}, s32[4,32,2]{1,2,0:T(2,128)}, u32[]{:S(2)}) copy-start(s32[4,32,2]{1,2,0:T(2,128)} %param.10) | copy-start | bytes 3076
  28.5 0.7 %copy-start.6 = (f32[4,32]{1,0:T(4,128)S(1)}, f32[4,32]{1,0:T(4,128)}, u32[]{:S(2)}) copy-start(f32[4,32]{1,0:T(4,128)} %observed_ref.1) | copy-start | bytes 1540
  29.3 0.7 %copy-start.3 = (s32[4,2]{0,1:T(2,128)S(1)}, s32[4,2]{0,1:T(2,128)}, u32[]{:S(2)}) copy-start(s32[4,2]{0,1:T(2,128)} %param.9) | copy-start | bytes 100
  37.0 6.3 %collective-permute-start.7 = (f32[1,256]{1,0:T(1,128)S(1)}, f32[1,256]{1,0:T(1,128)S(1)}, u32[]{:S(2)}, u32[]{:S(2)}) collective-permute-start(f32[1,256]{1,0:T(1,128)S(1)} %get-tuple-element.49), channel_id=1, source_target_pairs={{0,4},{4,0},{8,12},{12,8},{16,20},{20,16},{24,28},{28,24},{1,5},{5... | collective-permute-start | bytes 3080 | tf_op jit(solution)/shard_map/ppermute | solution.py:623
  43.3 3.6 %collective-permute-start.8 = (f32[1,256]{1,0:T(1,128)S(1)}, f32[1,256]{1,0:T(1,128)S(1)}, u32[]{:S(2)}, u32[]{:S(2)}) collective-permute-start(f32[1,256]{1,0:T(1,128)S(1)} %add.15), channel_id=1, source_target_pairs={{0,8},{4,12},{8,0},{12,4},{16,24},{20,28},{24,16},{28,20},{1,9},{5... | collective-permute-start | bytes 3080 | tf_op jit(solution)/shard_map/ppermute | solution.py:623
  46.9 3.6 %collective-permute-start.9 = (f32[1,256]{1,0:T(1,128)S(1)}, f32[1,256]{1,0:T(1,128)S(1)}, u32[]{:S(2)}, u32[]{:S(2)}) collective-permute-start(f32[1,256]{1,0:T(1,128)S(1)} %add.16.refs_0_), channel_id=1, source_target_pairs={{0,16},{4,20},{8,24},{12,28},{16,0},{20,4},{24,8},{28,12},{1,17},{... | collective-permute-start | bytes 3080 | tf_op jit(solution)/shard_map/ppermute | solution.py:623
  56.1 5.7 %collective-permute-start.14 = (f32[4,16,256]{2,1,0:T(8,128)S(1)}, f32[4,16,256]{2,1,0:T(8,128)S(1)}, u32[]{:S(2)}, u32[]{:S(2)}) collective-permute-start(f32[4,16,256]{2,1,0:T(8,128)S(1)} %get-tuple-element.60), channel_id=1, source_target_pairs={{0,1},{1,0},{2,3},{3,2},{4,5},{5,4},{6,7},{7,6},{8,9},{9,8},{10,11... | collective-permute-start | bytes 196616 | tf_op jit(solution)/shard_map/ppermute | solution.py:623
  56.2 5.7 %collective-permute-start.13 = (f32[4,16,256]{2,1,0:T(8,128)S(1)}, f32[4,16,256]{2,1,0:T(8,128)S(1)}, u32[]{:S(2)}, u32[]{:S(2)}) collective-permute-start(f32[4,16,256]{2,1,0:T(8,128)S(1)} %get-tuple-element.59), channel_id=1, source_target_pairs={{0,2},{1,3},{2,0},{3,1},{4,6},{5,7},{6,4},{7,5},{8,10},{9,11},{10,... | collective-permute-start | bytes 196616 | tf_op jit(solution)/shard_map/ppermute | solution.py:623
  58.0 6.1 %collective-permute-start.12 = (f32[4,16,256]{2,1,0:T(8,128)S(1)}, f32[4,16,256]{2,1,0:T(8,128)S(1)}, u32[]{:S(2)}, u32[]{:S(2)}) collective-permute-start(f32[4,16,256]{2,1,0:T(8,128)S(1)} %get-tuple-element.58), channel_id=1, source_target_pairs={{0,3},{1,2},{2,1},{3,0},{4,7},{5,6},{6,5},{7,4},{8,11},{9,10},{10,... | collective-permute-start | bytes 196616 | tf_op jit(solution)/shard_map/ppermute | solution.py:623

commit v5 on v4

--- a/solution.py
+++ b/solution.py
@@ -67,17 +67,29 @@
     return (rows + 2 * HALO + 1) * 2 * (columns // LANES)
 
 
-def refill(planes, groups, first, last):
-    extent = extent_of(planes[0], groups)
+def refill(planes, groups, start):
+    for plane in planes:
+        plane[sublane(start, -1, BATCH, groups), :] = pltpu.roll(plane[sublane(start, groups - 1, BATCH, groups), :], 1, 1)
+        plane[sublane(start, groups, BATCH, groups), :] = pltpu.roll(
+            plane[sublane(start, 0, BATCH, groups), :], LANES - 1, 1
+        )
+
+
+def refill_rows(planes, groups, first, last):
     for start in range(first, last, BATCH):
-        start = min(start, extent - BATCH)
-        for plane in planes:
-            plane[sublane(start, -1, BATCH, groups), :] = pltpu.roll(
-                plane[sublane(start, groups - 1, BATCH, groups), :], 1, 1
-            )
-            plane[sublane(start, groups, BATCH, groups), :] = pltpu.roll(
-                plane[sublane(start, 0, BATCH, groups), :], LANES - 1, 1
-            )
+        refill(planes, groups, min(start, extent_of(planes[0], groups) - BATCH))
+
+
+def refill_two(planes, groups, low, high):
+    def both(plane, j):
+        return jnp.concatenate([plane[sublane(at, j, SWEEPS, groups), :] for at in (low, high)], axis=0)
+
+    for plane in planes:
+        left = pltpu.roll(both(plane, groups - 1), 1, 1)
+        right = pltpu.roll(both(plane, 0), LANES - 1, 1)
+        for i, at in enumerate((low, high)):
+            plane[sublane(at, -1, SWEEPS, groups), :] = left[i * SWEEPS : (i + 1) * SWEEPS]
+            plane[sublane(at, groups, SWEEPS, groups), :] = right[i * SWEEPS : (i + 1) * SWEEPS]
 
 
 def planes_of(field, layers=None):
@@ -142,7 +154,7 @@
         wide[..., tile(first + h, groups), :] = received[..., h * groups : (h + 1) * groups, :]
 
 
-def spread_kernel(groups, x_ref, wide, inner_ref, outer_ref, work):
+def spread_kernel(groups, complete, x_ref, wide, inner_ref, outer_ref, work):
     sources, layers, rows, _ = x_ref.shape
     fields = [(s, l) for s in range(sources) for l in range(layers)]
     per = LANES // rows
@@ -157,19 +169,20 @@
                 wide[s, l, sublane(HALO, j, rows, groups), :] = turned[i * rows : (i + 1) * rows]
 
         columns_to_sublanes(read, write, work, groups)
-    refill(planes_of(wide), groups, HALO, HALO + rows)
+    if complete:
+        refill_rows(planes_of(wide), groups, HALO, HALO + rows)
     to_inner, to_outer = facing("space", rows, True)
     take_rows(wide, to_inner, inner_ref, groups)
     take_rows(wide, to_outer, outer_ref, groups)
 
 
-def spread_rows(x):
+def spread_rows(x, complete):
     sources, layers, rows, columns = x.shape
     groups = columns // LANES
     wide = jax.ShapeDtypeStruct((sources, layers, wide_length(rows, columns), LANES), jnp.float32)
     halo = jax.ShapeDtypeStruct((sources, layers, HALO * groups, LANES), jnp.float32)
     return pl.pallas_call(
-        functools.partial(spread_kernel, groups),
+        functools.partial(spread_kernel, groups, complete),
         out_shape=(wide, halo, halo),
         in_specs=[VMEM],
         out_specs=(VMEM,) * 3,
@@ -194,9 +207,12 @@
     total = sources * ends * count
     return pl.pallas_call(
         nodes_kernel,
-        out_shape=(jax.ShapeDtypeStruct((1, total), jnp.int32), jax.ShapeDtypeStruct((1, total), jnp.float32)),
-        in_specs=[VMEM, VMEM],
-        out_specs=(VMEM, VMEM),
+        out_shape=(
+            jax.ShapeDtypeStruct((1, total), jnp.int32),
+            jax.ShapeDtypeStruct((1, total), jnp.float32),
+        ),
+        in_specs=[VMEM] * 2,
+        out_specs=(VMEM,) * 2,
         compiler_params=GRANT,
         name="nodes",
     )(receivers, observed)
@@ -219,7 +235,7 @@
             wide_ref[l, sublane(HALO, j, rows, groups), :] = turned[l * rows : (l + 1) * rows]
 
     columns_to_sublanes(read, write, work, groups)
-    refill([wide_ref.at[l] for l in range(layers)], groups, HALO, HALO + rows)
+    refill_rows([wide_ref.at[l] for l in range(layers)], groups, HALO, HALO + rows)
     to_inner, to_outer = facing("space", rows, True)
     take_rows(wide_ref, to_inner, inner_ref, groups)
     take_rows(wide_ref, to_outer, outer_ref, groups)
@@ -293,7 +309,7 @@
     lax.fori_loop(0, count, body, 0)
 
 
-def sweep(step, old, new, coef, plane, groups, segments):
+def sweep(step, old, new, coef, plane, groups, segments, layers_refilled=None):
     p, g = STEPS[step]
     sources, layers = old.shape[:2]
     count, number = row_numbers(segments)
@@ -319,14 +335,26 @@
                     total += amount if g == 1.0 else g * amount
                 new[s, l, tile(e, groups), :] = total
 
-    def body(i, carry):
-        row(number(2 * i))
-        row(number(2 * i + 1))
-        return carry
-
-    lax.fori_loop(0, count // 2, body, 0)
-    if count % 2:
-        row(number(count - 1))
+    if len(segments) > 1:
+
+        def body(i, carry):
+            row(number(2 * i))
+            row(number(2 * i + 1))
+            return carry
+
+        lax.fori_loop(0, count // 2, body, 0)
+        if count % 2:
+            row(number(count - 1))
+        return
+
+    first, last = segments[0]
+    planes = planes_of(new, layers_refilled)
+
+    edge = extent_of(new, groups) - BATCH
+    for start in range(first, last, BATCH):
+        for e in range(start, min(start + BATCH, last)):
+            row(e)
+        refill(planes, groups, min(start, edge))
 
 
 def inner_rows(step, rows):
@@ -364,7 +392,6 @@
     old, new = wide, other
     for step in range(SWEEPS):
         sweep(step, old, new, coef, plane, groups, inner_rows(step, rows))
-        refill(planes_of(new), groups, *inner_rows(step, rows)[0])
         old, new = new, old
 
 
@@ -403,18 +430,16 @@
     put_rows(sigma, from_outer, sigma_outer, groups)
     put_rows(wide, from_inner, inner_ref, groups)
     put_rows(wide, from_outer, outer_ref, groups)
-    conductivity = [sigma.at[l] for l in range(layers)]
-    for first, last in ((0, HALO), (HALO + rows, extent)):
-        refill(conductivity, groups, first, last)
-        refill(planes_of(wide), groups, first, last)
+    refill_two([sigma.at[l] for l in range(layers)], groups, 1, extent - 1 - SWEEPS)
+    refill_two(planes_of(wide), groups, 1, extent - 1 - SWEEPS)
     segments = outer_rows(0, rows)
     coefficient_rows(sigma, coef, surface, groups, segments)
     add_electrodes(electrodes_ref, plane, surface, rows, groups, segments)
     old, new = wide, other
     for step in range(SWEEPS):
         sweep(step, old, new, coef, plane, groups, outer_rows(step, rows))
-        for first, last in outer_rows(step, rows):
-            refill(planes_of(new), groups, first, last)
+        (first, _), (_, last) = outer_rows(step, rows)
+        refill_two(planes_of(new), groups, first + 1, last - 1 - SWEEPS)
         old, new = new, old
 
     node = nodes_ref[...]
@@ -456,11 +481,13 @@
         from_inner, from_outer = facing("space", rows, False)
         put_rows(wide, from_inner, refs[0], groups)
         put_rows(wide, from_outer, refs[1], groups)
-        for first, last in ((0, HALO), (HALO + rows, extent)):
-            refill(planes_of(wide), groups, first, last)
-    sweep(0, wide, new, coef, None, groups, segments)
-    for first, last in segments:
-        refill(planes_of(new, range(1, wide.shape[1])), groups, first, last)
+        refill_two(planes_of(wide), groups, 1, extent - 1 - SWEEPS)
+    else:
+        refill_rows(planes_of(wide), groups, HALO, HALO + rows)
+    above_surface = range(1, wide.shape[1])
+    sweep(0, wide, new, coef, None, groups, segments, above_surface)
+    if len(segments) > 1:
+        refill_two(planes_of(new, above_surface), groups, segments[0][0] + 1, segments[1][1] - 1 - SWEEPS)
 
 
 def begin_adjoint(groups, segments, coef, halos, wide, new):
@@ -519,13 +546,12 @@
             amount = part[s * span : (s + 1) * span] * weight
             plane[s, where, :] = amount
             new[s, 0, sublane(1, j, span, groups), :] += amount
-    refill(planes_of(new, range(1)), groups, 1, extent - 1)
+    refill_rows(planes_of(new, range(1)), groups, 1, extent - 1)
 
     old, newer = new, wide
     for step in range(1, SWEEPS):
         segment = (1 + step, extent - 1 - step)
         sweep(step, old, newer, coef, plane, groups, [segment])
-        refill(planes_of(newer), groups, *segment)
         old, newer = newer, old
     adjoint = old
 
@@ -569,7 +595,12 @@
             total = term if s == 0 else total + term
         above_faces.append(total)
 
-    lax.fori_loop(HALO, HALO + rows, row, tuple(above_faces))
+    def two_rows(i, above_faces):
+        return row(HALO + 2 * i + 1, row(HALO + 2 * i, above_faces))
+
+    above_faces = lax.fori_loop(0, rows // 2, two_rows, tuple(above_faces))
+    if rows % 2:
+        row(HALO + rows - 1, above_faces)
 
     count_blocks = len(blocks)
     me = lax.axis_index("src") if count_blocks > 1 else 0
@@ -640,17 +671,17 @@
             pieces[k] = exchange(conductivity, "src", k)
     else:
         pieces = [lax.all_gather(conductivity, "src", axis=2, tiled=True)]
-    x_wide, to_inner, to_outer = spread_rows(potential_start)
+    x_wide, to_inner, to_outer = spread_rows(potential_start, True)
     from_inner = neighbour_pairs(to_inner, "space", 0)
     from_outer = neighbour_pairs(to_outer, "space", 1)
-    a_wide, a_inner, a_outer = spread_rows(adjoint_start)
+    a_wide, a_inner, a_outer = spread_rows(adjoint_start, False)
     a_inner = neighbour_pairs(a_inner, "space", 0)
     a_outer = neighbour_pairs(a_outer, "space", 1)
     nodes, measured = lay_out_nodes(receivers.transpose(0, 2, 1), observed)
+    ends = electrodes.T
     sigma, sigma_inner, sigma_outer = assemble_sigma(pieces, groups)
     sigma_outer = neighbour_pairs(sigma_outer, "space", 1)
     sigma_inner = neighbour_pairs(sigma_inner, "space", 0)
-    ends = electrodes.T
     inner = inner_solve(groups, ends, sigma, x_wide)
     _, forward, coef, surface, _, _, readings = outer_solve(
         groups, ends, sigma_inner, sigma_outer, from_inner, from_outer, nodes, sigma, inner

time: 65 us -> 64.1 us (0.986)
  Pallas kernels: 16.7 us -> 15.9 us
    pallas_call x1, Pallas kernels: 5.61 us -> 4.95 us  [finish_adjoint(): pl.pallas_call(functools.partial(adjoint_kernel, groups, parts), out_shap...]
where the time goes in v5:
time: 64.1 us; the launch traced here: 63.8 us
  starting transfers between devices  25.6 us (40%)
  waiting for transfers between devices  16.1 us (25%)
  Pallas kernels  15.9 us (25%)
  local copies, waits for them, and re-layouts  5.34 us (8%)
  other arithmetic  0.65 us (1%)
    ppermute x9, starting transfers between devices, exchange(): return lax.ppermute(value, axis, [(i, i ^ mask) for i in range(count)])  20 us
    ppermute x9, waiting for transfers between devices, exchange(): return lax.ppermute(value, axis, [(i, i ^ mask) for i in range(count)])  15.2 us
    ppermute x6, starting transfers between devices, neighbour_pairs(): lax.ppermute(value, axis, [(i, i + 1) for i in lower] + [(i + 1, i) for i...  5.56 us
    unnamed x14, local copies, waits for them, and re-layouts  5.34 us
    pallas_call x1, Pallas kernels, finish_adjoint(): pl.pallas_call(functools.partial(adjoint_kernel, groups, parts), out_shap...  4.95 us
    pallas_call x1, Pallas kernels, outer_solve(): pl.pallas_call(functools.partial(outer_kernel, groups), out_shape=kept +...  3.64 us
    pallas_call x1, Pallas kernels, inner_solve(): pl.pallas_call(functools.partial(inner_kernel, groups), out_shape=(jax.Sh...  3.24 us
    pallas_call x2, Pallas kernels, spread_rows(): pl.pallas_call(functools.partial(spread_kernel, groups, complete), out_sh...  1.94 us
  transfers between devices with their start and end apart: 15, of which 8 were waited for; matrix products, arithmetic and copies ran while one was open for 0% of the time, Pallas kernels for 17%

profile of v5, /device:TPU:0, one launch (start us, length us, event | category | flops | bytes accessed | tf_op | source)
XLA Modules:
  0.0 63.8 jit_solution(14893530182697968824)
XLA Ops:
  0.0 3.1 %collective-permute-start = (f32[4,16,256]{2,1,0:T(8,128)}, f32[4,16,256]{2,1,0:T(8,128)S(1)}, u32[]{:S(2)}, u32[]{:S(2)}) collective-permute-start(f32[4,16,256]{2,1,0:T(8,128)} %refs_0_.1), channel_id=1, source_target_pairs={{0,1},{1,0},{2,3},{3,2},{4,5},{5,4},{6,7},{7,6},{8,9},{9,8},{10,11... | collective-permute-start | bytes 196616 | tf_op jit(solution)/shard_map/ppermute | solution.py:654
  3.1 1.2 %copy-done = f32[4,4,16,1024]{3,2,1,0:T(8,128)S(1)} copy-done((f32[4,4,16,1024]{3,2,1,0:T(8,128)S(1)}, f32[4,4,16,1024]{3,2,1,0:T(8,128)}, u32[]{:S(2)}) %copy-start) | copy-done | bytes 1048600
  4.3 1.1 %spread.2 = (f32[4,4,432,128]{3,2,1,0:T(8,128)S(1)}, f32[4,4,40,128]{3,2,1,0:T(8,128)S(1)}, f32[4,4,40,128]{3,2,1,0:T(8,128)S(1)}) custom-call(f32[4,4,16,1024]{3,2,1,0:T(8,128)S(1)} %copy-done), custom_call_target="tpu_custom_call" | custom-call | tf_op jit(solution)/shard_map/spread/pallas_call | solution.py:184
  5.3 0.1 collective-permute-start.5
  5.4 0.7 %collective-permute-start.6 = (f32[4,4,40,128]{3,2,1,0:T(8,128)S(1)}, f32[4,4,40,128]{3,2,1,0:T(8,128)S(1)}, u32[]{:S(2)}, u32[]{:S(2)}) collective-permute-start(f32[4,4,40,128]{3,2,1,0:T(8,128)S(1)} %get-tuple-element.38), channel_id=1, source_target_pairs={{4,8},{12,16},{20,24},{8,4},{16,12},{24,20},{5,9},{13,17},{21,25},... | collective-permute-start | bytes 983048 | tf_op jit(solution)/shard_map/ppermute | solution.py:659
  6.1 0.0 copy-start.1
  6.1 1.2 %copy-done.1 = f32[4,4,16,1024]{3,2,1,0:T(8,128)S(1)} copy-done((f32[4,4,16,1024]{3,2,1,0:T(8,128)S(1)}, f32[4,4,16,1024]{3,2,1,0:T(8,128)}, u32[]{:S(2)}) %copy-start.1) | copy-done | bytes 1048600
  7.3 0.9 %spread.3 = (f32[4,4,432,128]{3,2,1,0:T(8,128)S(1)}, f32[4,4,40,128]{3,2,1,0:T(8,128)S(1)}, f32[4,4,40,128]{3,2,1,0:T(8,128)S(1)}) custom-call(f32[4,4,16,1024]{3,2,1,0:T(8,128)S(1)} %copy-done.1), custom_call_target="tpu_custom_call" | custom-call | tf_op jit(solution)/shard_map/spread/pallas_call | solution.py:184
  8.2 2.9 %collective-permute-start.10 = (f32[4,4,40,128]{3,2,1,0:T(8,128)S(1)}, f32[4,4,40,128]{3,2,1,0:T(8,128)S(1)}, u32[]{:S(2)}, u32[]{:S(2)}) collective-permute-start(f32[4,4,40,128]{3,2,1,0:T(8,128)S(1)} %get-tuple-element.50), channel_id=1, source_target_pairs={{0,4},{8,12},{16,20},{24,28},{4,0},{12,8},{20,16},{28,24},{1,5},{9... | collective-permute-start | bytes 983048 | tf_op jit(solution)/shard_map/ppermute | solution.py:659
  11.1 0.7 %collective-permute-start.11 = (f32[4,4,40,128]{3,2,1,0:T(8,128)S(1)}, f32[4,4,40,128]{3,2,1,0:T(8,128)S(1)}, u32[]{:S(2)}, u32[]{:S(2)}) collective-permute-start(f32[4,4,40,128]{3,2,1,0:T(8,128)S(1)} %get-tuple-element.51), channel_id=1, source_target_pairs={{4,8},{12,16},{20,24},{8,4},{16,12},{24,20},{5,9},{13,17},{21,25},... | collective-permute-start | bytes 983048 | tf_op jit(solution)/shard_map/ppermute | solution.py:659
  11.8 0.0 collective-permute-done.refs_1_
  11.8 2.7 %collective-permute-start.1 = (f32[4,16,256]{2,1,0:T(8,128)}, f32[4,16,256]{2,1,0:T(8,128)S(1)}, u32[]{:S(2)}, u32[]{:S(2)}) collective-permute-start(f32[4,16,256]{2,1,0:T(8,128)} %refs_0_.1), channel_id=1, source_target_pairs={{0,2},{1,3},{2,0},{3,1},{4,6},{5,7},{6,4},{7,5},{8,10},{9,11},{10,... | collective-permute-start | bytes 196616 | tf_op jit(solution)/shard_map/ppermute | solution.py:654
  14.5 3.4 %collective-permute-done.1.refs_2_ = f32[4,16,256]{2,1,0:T(8,128)S(1)} collective-permute-done((f32[4,16,256]{2,1,0:T(8,128)}, f32[4,16,256]{2,1,0:T(8,128)S(1)}, u32[]{:S(2)}, u32[]{:S(2)}) %collective-permute-start.1) | collective-permute-done | bytes 65568 | tf_op jit(solution)/shard_map/ppermute | solution.py:654
  17.8 1.9 %collective-permute-start.2 = (f32[4,16,256]{2,1,0:T(8,128)}, f32[4,16,256]{2,1,0:T(8,128)S(1)}, u32[]{:S(2)}, u32[]{:S(2)}) collective-permute-start(f32[4,16,256]{2,1,0:T(8,128)} %refs_0_.1), channel_id=1, source_target_pairs={{0,3},{1,2},{2,1},{3,0},{4,7},{5,6},{6,5},{7,4},{8,11},{9,10},{10,... | collective-permute-start | bytes 196616 | tf_op jit(solution)/shard_map/ppermute | solution.py:654
  19.7 4.4 %collective-permute-done.2.refs_3_ = f32[4,16,256]{2,1,0:T(8,128)S(1)} collective-permute-done((f32[4,16,256]{2,1,0:T(8,128)}, f32[4,16,256]{2,1,0:T(8,128)S(1)}, u32[]{:S(2)}, u32[]{:S(2)}) %collective-permute-start.2) | collective-permute-done | bytes 65568 | tf_op jit(solution)/shard_map/ppermute | solution.py:654
  24.1 0.8 %copy-done.2 = f32[4,16,256]{2,1,0:T(8,128)S(1)} copy-done((f32[4,16,256]{2,1,0:T(8,128)S(1)}, f32[4,16,256]{2,1,0:T(8,128)}, u32[]{:S(2)}) %copy-start.2) | copy-done | bytes 65560
  25.0 0.5 sigma.1
  25.5 0.6 collective-permute-start.3
  26.1 0.9 %collective-permute-done.3.sigma_inner = f32[4,40,128]{2,1,0:T(8,128)S(1)} collective-permute-done((f32[4,40,128]{2,1,0:T(8,128)S(1)}, f32[4,40,128]{2,1,0:T(8,128)S(1)}, u32[]{:S(2)}, u32[]{:S(2)}) %collective-permute-start.3) | collective-permute-done | bytes 81952 | tf_op jit(solution)/shard_map/ppermute | solution.py:659
  27.0 0.7 %collective-permute-start.4 = (f32[4,40,128]{2,1,0:T(8,128)S(1)}, f32[4,40,128]{2,1,0:T(8,128)S(1)}, u32[]{:S(2)}, u32[]{:S(2)}) collective-permute-start(f32[4,40,128]{2,1,0:T(8,128)S(1)} %get-tuple-element.36), channel_id=1, source_target_pairs={{4,8},{12,16},{20,24},{8,4},{16,12},{24,20},{5,9},{13,17},{21,25},... | collective-permute-start | bytes 245768 | tf_op jit(solution)/shard_map/ppermute | solution.py:659
  27.7 0.0 copy-start.5
  27.7 0.7 %copy-done.5 = s32[4,32,2]{1,2,0:T(2,128)S(1)} copy-done((s32[4,32,2]{1,2,0:T(2,128)S(1)}, s32[4,32,2]{1,2,0:T(2,128)}, u32[]{:S(2)}) %copy-start.5) | copy-done | bytes 1048
  28.4 0.7 %copy-done.6 = f32[4,32]{1,0:T(4,128)S(1)} copy-done((f32[4,32]{1,0:T(4,128)S(1)}, f32[4,32]{1,0:T(4,128)}, u32[]{:S(2)}) %copy-start.6) | copy-done | bytes 536
  29.0 0.1 nodes.1
  29.1 0.7 %copy-done.3 = s32[4,2]{0,1:T(2,128)S(1)} copy-done((s32[4,2]{0,1:T(2,128)S(1)}, s32[4,2]{0,1:T(2,128)}, u32[]{:S(2)}) %copy-start.3) | copy-done | bytes 56
  29.8 3.2 %inner.1 = (f32[4,4,432,128]{3,2,1,0:T(8,128)S(1)}, f32[6,4,208,128]{3,2,1,0:T(8,128)S(1)}, f32[208,128]{1,0:T(8,128)S(1)}, f32[4,4,432,128]{3,2,1,0:T(8,128)S(1)}, f32[4,208,128]{2,1,0:T(8,128)S(1)}) custom-call(s32[2,4]{1,0:T(2,128)S(1)} %bitcast.2, f32[4,432,128]{2,1,0:T(8,128)S(1)} %get-tuple-element.39.sigma.refs_0_, ...), custom_call_target="tpu_custom_call", output_to_operand_aliasing={{0}: (2, {})} | custom-call | tf_op jit(solution)/shard_map/inner/pallas_call | solution.py:402
  33.1 0.0 collective-permute-done.4.sigma_outer
  33.1 0.0 collective-permute-done.5.inner_ref
  33.1 0.0 collective-permute-done.6.outer_ref
  33.1 3.6 %outer.1 = (f32[4,432,128]{2,1,0:T(8,128)S(1)}, f32[4,4,432,128]{3,2,1,0:T(8,128)S(1)}, f32[6,4,208,128]{3,2,1,0:T(8,128)S(1)}, f32[208,128]{1,0:T(8,128)S(1)}, ...) custom-call(s32[2,4]{1,0:T(2,128)S(1)} %bitcast.3, ...), custom_call_target="tpu_custom_call", output_to_operand_aliasing={{0}: (6, {}), {1}: (7, {}), {2}: (8, {}), {3}: (9, {}), {4}... | custom-call | tf_op jit(solution)/shard_map/outer/pallas_call | solution.py:465
  36.7 5.5 %collective-permute-start.7 = (f32[1,256]{1,0:T(1,128)S(1)}, f32[1,256]{1,0:T(1,128)S(1)}, u32[]{:S(2)}, u32[]{:S(2)}) collective-permute-start(f32[1,256]{1,0:T(1,128)S(1)} %get-tuple-element.49), channel_id=1, source_target_pairs={{0,4},{4,0},{8,12},{12,8},{16,20},{20,16},{24,28},{28,24},{1,5},{5... | collective-permute-start | bytes 3080 | tf_op jit(solution)/shard_map/ppermute | solution.py:654
  42.2 0.8 %collective-permute-done.7 = f32[1,256]{1,0:T(1,128)S(1)} collective-permute-done((f32[1,256]{1,0:T(1,128)S(1)}, f32[1,256]{1,0:T(1,128)S(1)}, u32[]{:S(2)}, u32[]{:S(2)}) %collective-permute-start.7) | collective-permute-done | bytes 1056 | tf_op jit(solution)/shard_map/ppermute | solution.py:654
  43.1 1.1 %collective-permute-start.8 = (f32[1,256]{1,0:T(1,128)S(1)}, f32[1,256]{1,0:T(1,128)S(1)}, u32[]{:S(2)}, u32[]{:S(2)}) collective-permute-start(f32[1,256]{1,0:T(1,128)S(1)} %add.15), channel_id=1, source_target_pairs={{0,8},{4,12},{8,0},{12,4},{16,24},{20,28},{24,16},{28,20},{1,9},{5... | collective-permute-start | bytes 3080 | tf_op jit(solution)/shard_map/ppermute | solution.py:654
  44.1 2.5 %collective-permute-done.8 = f32[1,256]{1,0:T(1,128)S(1)} collective-permute-done((f32[1,256]{1,0:T(1,128)S(1)}, f32[1,256]{1,0:T(1,128)S(1)}, u32[]{:S(2)}, u32[]{:S(2)}) %collective-permute-start.8) | collective-permute-done | bytes 1056 | tf_op jit(solution)/shard_map/ppermute | solution.py:654
  46.6 1.4 %collective-permute-start.9 = (f32[1,256]{1,0:T(1,128)S(1)}, f32[1,256]{1,0:T(1,128)S(1)}, u32[]{:S(2)}, u32[]{:S(2)}) collective-permute-start(f32[1,256]{1,0:T(1,128)S(1)} %add.16.refs_0_), channel_id=1, source_target_pairs={{0,16},{4,20},{8,24},{12,28},{16,0},{20,4},{24,8},{28,12},{1,17},{... | collective-permute-start | bytes 3080 | tf_op jit(solution)/shard_map/ppermute | solution.py:654
  48.1 0.7 %begin.2 = (f32[4,4,432,128]{3,2,1,0:T(8,128)S(1)}, f32[4,4,432,128]{3,2,1,0:T(8,128)S(1)}) custom-call(f32[6,4,208,128]{3,2,1,0:T(8,128)S(1)} %get-tuple-element.46.coef, f32[4,4,432,128]{3,2,1,0:T(8,128)S(1)} %get-tuple-element.52.refs_0_), custom_call_target="tpu_custom_call", output_to_operand_aliasing={{0}: (1, {})} | custom-call | tf_op jit(solution)/shard_map/begin/pallas_call | solution.py:499
  48.8 0.0 collective-permute-done.10.refs_0_
  48.8 0.0 collective-permute-done.11.refs_1_
  48.8 0.8 %begin.3 = (f32[4,4,432,128]{3,2,1,0:T(8,128)S(1)}, f32[4,4,432,128]{3,2,1,0:T(8,128)S(1)}) custom-call(f32[6,4,208,128]{3,2,1,0:T(8,128)S(1)} %get-tuple-element.46.coef, f32[4,4,40,128]{3,2,1,0:T(8,128)S(1)} %collective-permute-done.10.refs_0_, ...), custom_call_target="tpu_custom_call", output_to_operand_aliasing={{0}: (3, {}), {1}: (4, {})} | custom-call | tf_op jit(solution)/shard_map/begin/pallas_call | solution.py:499
  49.6 0.6 collective-permute-done.9.refs_1_
  50.2 4.9 %adjoint.1 = (f32[4,4,432,128]{3,2,1,0:T(8,128)S(1)}, f32[4,4,432,128]{3,2,1,0:T(8,128)S(1)}, f32[4,16,256]{2,1,0:T(8,128)S(1)}, f32[4,16,256]{2,1,0:T(8,128)S(1...) custom-call(s32[1,256]{1,0:T(1,128)S(1)} %get-tuple-element.33.nodes_ref, ...), custom_call_target="tpu_custom_call", output_to_operand_aliasing={{0}: (7, {}), {1}: (8, {})} | custom-call | tf_op jit(solution)/shard_map/adjoint/pallas_call | solution.py:631
  55.2 0.1 collective-permute-start.14
  55.2 1.8 %collective-permute-start.13 = (f32[4,16,256]{2,1,0:T(8,128)S(1)}, f32[4,16,256]{2,1,0:T(8,128)S(1)}, u32[]{:S(2)}, u32[]{:S(2)}) collective-permute-start(f32[4,16,256]{2,1,0:T(8,128)S(1)} %get-tuple-element.59), channel_id=1, source_target_pairs={{0,2},{1,3},{2,0},{3,1},{4,6},{5,7},{6,4},{7,5},{8,10},{9,11},{10,... | collective-permute-start | bytes 196616 | tf_op jit(solution)/shard_map/ppermute | solution.py:654
  57.1 2.6 %collective-permute-start.12 = (f32[4,16,256]{2,1,0:T(8,128)S(1)}, f32[4,16,256]{2,1,0:T(8,128)S(1)}, u32[]{:S(2)}, u32[]{:S(2)}) collective-permute-start(f32[4,16,256]{2,1,0:T(8,128)S(1)} %get-tuple-element.58), channel_id=1, source_target_pairs={{0,3},{1,2},{2,1},{3,0},{4,7},{5,6},{6,5},{7,4},{8,11},{9,10},{10,... | collective-permute-start | bytes 196616 | tf_op jit(solution)/shard_map/ppermute | solution.py:654
  59.6 0.0 collective-permute-done.14
  59.6 1.3 %collective-permute-done.13 = f32[4,16,256]{2,1,0:T(8,128)S(1)} collective-permute-done((f32[4,16,256]{2,1,0:T(8,128)S(1)}, f32[4,16,256]{2,1,0:T(8,128)S(1)}, u32[]{:S(2)}, u32[]{:S(2)}) %collective-permute-start.13) | collective-permute-done | bytes 65568 | tf_op jit(solution)/shard_map/ppermute | solution.py:654
  60.9 2.2 %collective-permute-done.12 = f32[4,16,256]{2,1,0:T(8,128)S(1)} collective-permute-done((f32[4,16,256]{2,1,0:T(8,128)S(1)}, f32[4,16,256]{2,1,0:T(8,128)S(1)}, u32[]{:S(2)}, u32[]{:S(2)}) %collective-permute-start.12) | collective-permute-done | bytes 65568 | tf_op jit(solution)/shard_map/ppermute | solution.py:654
  63.1 0.6 %add_add_fusion = f32[4,16,256]{2,1,0:T(8,128)} fusion(f32[4,16,256]{2,1,0:T(8,128)S(1)} %collective-permute-done.14, f32[4,16,256]{2,1,0:T(8,128)S(1)} %collective-permute-done.13, f32[4,16,256]{2,1,0:T(8,128)S(1)} %get-tuple-element.57, f32[4,16,256]{2,1,0:T(8,128)S(1)} %collective-permute-done.12), kind=kLoop, calls=%fused_computation | loop fusion | flops 49152 | bytes 327680 | tf_op jit(solution)/shard_map/add | solution.py:714
  (8 shorter events, 0.0 us)
Async XLA Ops:
  0.0 11.8 %collective-permute-start = (f32[4,16,256]{2,1,0:T(8,128)}, f32[4,16,256]{2,1,0:T(8,128)S(1)}, u32[]{:S(2)}, u32[]{:S(2)}) collective-permute-start(f32[4,16,256]{2,1,0:T(8,128)} %refs_0_.1), channel_id=1, source_target_pairs={{0,1},{1,0},{2,3},{3,2},{4,5},{5,4},{6,7},{7,6},{8,9},{9,8},{10,11... | collective-permute-start | bytes 196616 | tf_op jit(solution)/shard_map/ppermute | solution.py:654
  3.1 1.2 %copy-start = (f32[4,4,16,1024]{3,2,1,0:T(8,128)S(1)}, f32[4,4,16,1024]{3,2,1,0:T(8,128)}, u32[]{:S(2)}) copy-start(f32[4,4,16,1024]{3,2,1,0:T(8,128)} %x_ref.2) | copy-start | bytes 3145732
  4.3 28.8 %copy-start.4 = (s32[4,2]{0,1:T(2,128)S(1)}, s32[4,2]{0,1:T(2,128)}, u32[]{:S(2)}) copy-start(s32[4,2]{0,1:T(2,128)} %param.9) | copy-start | bytes 100
  5.3 27.7 %collective-permute-start.5 = (f32[4,4,40,128]{3,2,1,0:T(8,128)S(1)}, f32[4,4,40,128]{3,2,1,0:T(8,128)S(1)}, u32[]{:S(2)}, u32[]{:S(2)}) collective-permute-start(f32[4,4,40,128]{3,2,1,0:T(8,128)S(1)} %get-tuple-element.37), channel_id=1, source_target_pairs={{0,4},{8,12},{16,20},{24,28},{4,0},{12,8},{20,16},{28,24},{1,5},{9... | collective-permute-start | bytes 983048 | tf_op jit(solution)/shard_map/ppermute | solution.py:659
  5.4 27.7 %collective-permute-start.6 = (f32[4,4,40,128]{3,2,1,0:T(8,128)S(1)}, f32[4,4,40,128]{3,2,1,0:T(8,128)S(1)}, u32[]{:S(2)}, u32[]{:S(2)}) collective-permute-start(f32[4,4,40,128]{3,2,1,0:T(8,128)S(1)} %get-tuple-element.38), channel_id=1, source_target_pairs={{4,8},{12,16},{20,24},{8,4},{16,12},{24,20},{5,9},{13,17},{21,25},... | collective-permute-start | bytes 983048 | tf_op jit(solution)/shard_map/ppermute | solution.py:659
  6.1 1.2 %copy-start.1 = (f32[4,4,16,1024]{3,2,1,0:T(8,128)S(1)}, f32[4,4,16,1024]{3,2,1,0:T(8,128)}, u32[]{:S(2)}) copy-start(f32[4,4,16,1024]{3,2,1,0:T(8,128)} %x_ref.3) | copy-start | bytes 3145732
  8.2 40.6 %collective-permute-start.10 = (f32[4,4,40,128]{3,2,1,0:T(8,128)S(1)}, f32[4,4,40,128]{3,2,1,0:T(8,128)S(1)}, u32[]{:S(2)}, u32[]{:S(2)}) collective-permute-start(f32[4,4,40,128]{3,2,1,0:T(8,128)S(1)} %get-tuple-element.50), channel_id=1, source_target_pairs={{0,4},{8,12},{16,20},{24,28},{4,0},{12,8},{20,16},{28,24},{1,5},{9... | collective-permute-start | bytes 983048 | tf_op jit(solution)/shard_map/ppermute | solution.py:659
  11.1 37.7 %collective-permute-start.11 = (f32[4,4,40,128]{3,2,1,0:T(8,128)S(1)}, f32[4,4,40,128]{3,2,1,0:T(8,128)S(1)}, u32[]{:S(2)}, u32[]{:S(2)}) collective-permute-start(f32[4,4,40,128]{3,2,1,0:T(8,128)S(1)} %get-tuple-element.51), channel_id=1, source_target_pairs={{4,8},{12,16},{20,24},{8,4},{16,12},{24,20},{5,9},{13,17},{21,25},... | collective-permute-start | bytes 983048 | tf_op jit(solution)/shard_map/ppermute | solution.py:659
  11.8 6.0 %collective-permute-start.1 = (f32[4,16,256]{2,1,0:T(8,128)}, f32[4,16,256]{2,1,0:T(8,128)S(1)}, u32[]{:S(2)}, u32[]{:S(2)}) collective-permute-start(f32[4,16,256]{2,1,0:T(8,128)} %refs_0_.1), channel_id=1, source_target_pairs={{0,2},{1,3},{2,0},{3,1},{4,6},{5,7},{6,4},{7,5},{8,10},{9,11},{10,... | collective-permute-start | bytes 196616 | tf_op jit(solution)/shard_map/ppermute | solution.py:654
  17.8 6.3 %collective-permute-start.2 = (f32[4,16,256]{2,1,0:T(8,128)}, f32[4,16,256]{2,1,0:T(8,128)S(1)}, u32[]{:S(2)}, u32[]{:S(2)}) collective-permute-start(f32[4,16,256]{2,1,0:T(8,128)} %refs_0_.1), channel_id=1, source_target_pairs={{0,3},{1,2},{2,1},{3,0},{4,7},{5,6},{6,5},{7,4},{8,11},{9,10},{10,... | collective-permute-start | bytes 196616 | tf_op jit(solution)/shard_map/ppermute | solution.py:654
  24.1 0.8 %copy-start.2 = (f32[4,16,256]{2,1,0:T(8,128)S(1)}, f32[4,16,256]{2,1,0:T(8,128)}, u32[]{:S(2)}) copy-start(f32[4,16,256]{2,1,0:T(8,128)} %refs_0_.1) | copy-start | bytes 196612
  25.5 1.5 %collective-permute-start.3 = (f32[4,40,128]{2,1,0:T(8,128)S(1)}, f32[4,40,128]{2,1,0:T(8,128)S(1)}, u32[]{:S(2)}, u32[]{:S(2)}) collective-permute-start(f32[4,40,128]{2,1,0:T(8,128)S(1)} %get-tuple-element.35), channel_id=1, source_target_pairs={{0,4},{8,12},{16,20},{24,28},{4,0},{12,8},{20,16},{28,24},{1,5},{9... | collective-permute-start | bytes 245768 | tf_op jit(solution)/shard_map/ppermute | solution.py:659
  27.0 6.0 %collective-permute-start.4 = (f32[4,40,128]{2,1,0:T(8,128)S(1)}, f32[4,40,128]{2,1,0:T(8,128)S(1)}, u32[]{:S(2)}, u32[]{:S(2)}) collective-permute-start(f32[4,40,128]{2,1,0:T(8,128)S(1)} %get-tuple-element.36), channel_id=1, source_target_pairs={{4,8},{12,16},{20,24},{8,4},{16,12},{24,20},{5,9},{13,17},{21,25},... | collective-permute-start | bytes 245768 | tf_op jit(solution)/shard_map/ppermute | solution.py:659
  27.7 0.7 %copy-start.5 = (s32[4,32,2]{1,2,0:T(2,128)S(1)}, s32[4,32,2]{1,2,0:T(2,128)}, u32[]{:S(2)}) copy-start(s32[4,32,2]{1,2,0:T(2,128)} %param.10) | copy-start | bytes 3076
  28.4 0.7 %copy-start.6 = (f32[4,32]{1,0:T(4,128)S(1)}, f32[4,32]{1,0:T(4,128)}, u32[]{:S(2)}) copy-start(f32[4,32]{1,0:T(4,128)} %observed_ref.1) | copy-start | bytes 1540
  29.1 0.7 %copy-start.3 = (s32[4,2]{0,1:T(2,128)S(1)}, s32[4,2]{0,1:T(2,128)}, u32[]{:S(2)}) copy-start(s32[4,2]{0,1:T(2,128)} %param.9) | copy-start | bytes 100
  36.7 6.3 %collective-permute-start.7 = (f32[1,256]{1,0:T(1,128)S(1)}, f32[1,256]{1,0:T(1,128)S(1)}, u32[]{:S(2)}, u32[]{:S(2)}) collective-permute-start(f32[1,256]{1,0:T(1,128)S(1)} %get-tuple-element.49), channel_id=1, source_target_pairs={{0,4},{4,0},{8,12},{12,8},{16,20},{20,16},{24,28},{28,24},{1,5},{5... | collective-permute-start | bytes 3080 | tf_op jit(solution)/shard_map/ppermute | solution.py:654
  43.1 3.6 %collective-permute-start.8 = (f32[1,256]{1,0:T(1,128)S(1)}, f32[1,256]{1,0:T(1,128)S(1)}, u32[]{:S(2)}, u32[]{:S(2)}) collective-permute-start(f32[1,256]{1,0:T(1,128)S(1)} %add.15), channel_id=1, source_target_pairs={{0,8},{4,12},{8,0},{12,4},{16,24},{20,28},{24,16},{28,20},{1,9},{5... | collective-permute-start | bytes 3080 | tf_op jit(solution)/shard_map/ppermute | solution.py:654
  46.6 3.6 %collective-permute-start.9 = (f32[1,256]{1,0:T(1,128)S(1)}, f32[1,256]{1,0:T(1,128)S(1)}, u32[]{:S(2)}, u32[]{:S(2)}) collective-permute-start(f32[1,256]{1,0:T(1,128)S(1)} %add.16.refs_0_), channel_id=1, source_target_pairs={{0,16},{4,20},{8,24},{12,28},{16,0},{20,4},{24,8},{28,12},{1,17},{... | collective-permute-start | bytes 3080 | tf_op jit(solution)/shard_map/ppermute | solution.py:654
  55.2 4.5 %collective-permute-start.14 = (f32[4,16,256]{2,1,0:T(8,128)S(1)}, f32[4,16,256]{2,1,0:T(8,128)S(1)}, u32[]{:S(2)}, u32[]{:S(2)}) collective-permute-start(f32[4,16,256]{2,1,0:T(8,128)S(1)} %get-tuple-element.60), channel_id=1, source_target_pairs={{0,1},{1,0},{2,3},{3,2},{4,5},{5,4},{6,7},{7,6},{8,9},{9,8},{10,11... | collective-permute-start | bytes 196616 | tf_op jit(solution)/shard_map/ppermute | solution.py:654
  55.2 5.7 %collective-permute-start.13 = (f32[4,16,256]{2,1,0:T(8,128)S(1)}, f32[4,16,256]{2,1,0:T(8,128)S(1)}, u32[]{:S(2)}, u32[]{:S(2)}) collective-permute-start(f32[4,16,256]{2,1,0:T(8,128)S(1)} %get-tuple-element.59), channel_id=1, source_target_pairs={{0,2},{1,3},{2,0},{3,1},{4,6},{5,7},{6,4},{7,5},{8,10},{9,11},{10,... | collective-permute-start | bytes 196616 | tf_op jit(solution)/shard_map/ppermute | solution.py:654
  57.1 6.1 %collective-permute-start.12 = (f32[4,16,256]{2,1,0:T(8,128)S(1)}, f32[4,16,256]{2,1,0:T(8,128)S(1)}, u32[]{:S(2)}, u32[]{:S(2)}) collective-permute-start(f32[4,16,256]{2,1,0:T(8,128)S(1)} %get-tuple-element.58), channel_id=1, source_target_pairs={{0,3},{1,2},{2,1},{3,0},{4,7},{5,6},{6,5},{7,4},{8,11},{9,10},{10,... | collective-permute-start | bytes 196616 | tf_op jit(solution)/shard_map/ppermute | solution.py:654
